TPU v7x, 32 devices: a whole 2x2x4 slice. The times are simulated.
32 devices in a mesh: grp: 2 (over y), req: 4 (over z), kvh: 4 (over x, core).
Axes of the slice: x: 2, y: 2, z: 4, core: 2. Of those that a mesh axis runs over, the one named last changes fastest.
Arguments:
- store_kv: bfloat16 [32, 128, 8, 256], P(('grp', 'req'), None, 'kvh'), parts along dimension 0, may hold values from -7.25 to 7.25
- block_owner: int32 [8, 24, 1], P(('grp', 'req')), parts along dimension 0, may hold values from 0 to 3; in each aligned block of 24 rows (0 to 23, 24 to 47, ..., all dimensions but the last counted through in order) at most 6 rows name the same one
- block_slot: int32 [8, 24], P(('grp', 'req')), parts along dimension 0, may hold values from 0 to 3
- span_len: int32 [8, 4], P(('grp', 'req')), parts along dimension 0, may hold values from 1 to 12, 24 in all within a row
- row_index: int32 [8, 384], P(('grp', 'req')), parts along dimension 0, may hold values from 0 to 3071, as said below
- fresh_q: bfloat16 [8, 384, 8192], P(('grp', 'req'), None, 'kvh'), parts along dimension 0, may hold values from -12 to 12
- fresh_kv: bfloat16 [8, 384, 8, 256], P(('grp', 'req'), None, 'kvh'), parts along dimension 0, may hold values from -6 to 6
Outputs:
- attended: bfloat16 [8, 384, 8192], P(('grp', 'req'), None, 'kvh'), parts along dimension 0
There are 2 independent parts, one for each index of `grp`. A program takes and returns all parts, laid end to end along the dimension named above; each array names one. Nothing has to cross between parts.
Inputs may be any that keep to these rules, and one draw needn't show every extreme that they name: `block_owner`: among the 24 blocks of one request no store shard appears more than 6 times; in every draw some shard appears exactly 6 times for some request. `span_len`: each row sums to 24; its largest entry is 12. `row_index`: each row is ascending without repeats, starts with 0 and ends with 3071.
All inputs are finite; a program needn't handle non-finite values.
Results may differ from a plain program's by a relative error of at most 0.0095.
Values may be sent and summed in bfloat16 or wider, within the bound.
No kernel may reach another device: no remote copies, remote signals or barrier semaphores. Data moves between devices by JAX's collectives and lax.ppermute only.
A program may use at most 64 MiB of HBM per device.

v0:
```python
import jax
import jax.numpy as jnp
from jax import lax
from jax.sharding import PartitionSpec as P

rope_base = 500000.0


def rotate(field, position):
    half_dim = field.shape[-1] // 2
    pair_index = jnp.arange(half_dim, dtype=jnp.float32)
    inv_freq = jnp.exp(pair_index * (-2.0 / field.shape[-1]) * jnp.log(jnp.float32(rope_base)))
    angles = position[..., None] * inv_freq
    cosine = jnp.cos(angles)
    sine_part = jnp.sin(angles)
    first_half = field[..., :half_dim]
    second = field[..., half_dim:]
    return jnp.concatenate(
        [first_half * cosine - second * sine_part, second * cosine + first_half * sine_part],
        axis=-1,
    )


def span_offsets(lengths, block_count, block_len):
    starts = jnp.cumsum(lengths) - lengths
    block_ids = jnp.arange(block_count, dtype=jnp.int32)
    began = jnp.where(starts[None, :] <= block_ids[:, None], starts[None, :], 0)
    return jnp.max(began, axis=1) * block_len


def attend_head(query_rows, key_rows, value_rows, query_pos):
    key_pos = jnp.arange(key_rows.shape[0], dtype=jnp.int32)
    scores = lax.dot_general(
        query_rows, key_rows, (((1,), (1,)), ((), ())), preferred_element_type=jnp.float32
    )
    scores = scores * key_rows.shape[1] ** (-0.5)
    scores = jnp.where(key_pos[None, :] <= query_pos[:, None], scores, -jnp.inf)
    largest = jnp.max(scores, axis=1, keepdims=True)
    weights = jnp.exp(scores - largest)
    probs = (weights / jnp.sum(weights, axis=1, keepdims=True)).astype(jnp.bfloat16)
    return jnp.dot(probs, value_rows, preferred_element_type=jnp.float32).astype(jnp.bfloat16)


def on_device(store_kv, block_owner, block_slot, span_len, row_index, fresh_q, fresh_kv):
    stored, block_len, kv_heads, pair_width = store_kv.shape
    head_dim = pair_width // 2
    block_count = block_slot.shape[1]
    row_count = row_index.shape[1]
    context = block_count * block_len
    query_group = fresh_q.shape[2] // (kv_heads * head_dim)
    owners = block_owner[0, :, 0]
    slot_ids = block_slot[0]
    store_flat = store_kv.reshape(stored, block_len * kv_heads * pair_width)
    everything = lax.all_gather(store_flat, "req", axis=0, tiled=True)
    wanted = owners * stored + slot_ids
    cached = jnp.take(everything, wanted, axis=0)
    cached = cached.reshape(block_count, block_len, kv_heads, pair_width)
    offset = span_offsets(span_len[0], block_count, block_len)
    key_rows = rotate(
        cached[..., :head_dim].astype(jnp.float32), offset[:, None, None].astype(jnp.float32)
    )
    key_rows = key_rows.astype(jnp.bfloat16).reshape(context, kv_heads, head_dim)
    value_rows = cached[..., head_dim:].reshape(context, kv_heads, head_dim)
    row_pos = row_index[0]
    position = row_pos.astype(jnp.float32)
    fresh = fresh_kv[0]
    fresh_keys = rotate(fresh[..., :head_dim].astype(jnp.float32), position[:, None]).astype(
        jnp.bfloat16
    )
    key_rows = key_rows.at[row_pos].set(fresh_keys)
    value_rows = value_rows.at[row_pos].set(fresh[..., head_dim:])
    queries = rotate(
        fresh_q[0].reshape(row_count, kv_heads, query_group, head_dim).astype(jnp.float32),
        position[:, None, None],
    )
    queries = queries.astype(jnp.bfloat16)
    step_rows = 64
    block_total = row_count // step_rows
    query_pos = jnp.repeat(row_pos, query_group).reshape(block_total, step_rows * query_group)
    outputs = []
    for kv_index in range(kv_heads):
        key_head = key_rows[:, kv_index]
        value_head = value_rows[:, kv_index]
        query_blocks = queries[:, kv_index].reshape(block_total, step_rows * query_group, head_dim)

        def attend_block(block_pair, key_head=key_head, value_head=value_head):
            return attend_head(block_pair[0], key_head, value_head, block_pair[1])

        result = lax.map(attend_block, (query_blocks, query_pos))
        outputs.append(result.reshape(row_count, query_group, head_dim))
    return jnp.stack(outputs, axis=1).reshape(1, row_count, kv_heads * query_group * head_dim)


def solution(mesh):
    placed = (
        P(("grp", "req"), None, "kvh", None),
        P(("grp", "req"), None, None),
        P(("grp", "req"), None),
        P(("grp", "req"), None),
        P(("grp", "req"), None),
        P(("grp", "req"), None, "kvh"),
        P(("grp", "req"), None, "kvh", None),
    )
    return jax.shard_map(
        on_device,
        mesh=mesh,
        in_specs=placed,
        out_specs=P(("grp", "req"), None, "kvh"),
        check_vma=False,
    )
```

profile of v0, /device:TPU:0, one launch (start us, length us, event | category | flops | bytes accessed | tf_op | source)
XLA Modules:
  0.0 178.7 jit_solution(17499813460900487766)
XLA Ops:
  22.9 34.6 %all-gather.3.cloned.1.call-done = bf16[4,4,65536]{2,1,0:T(4,128)(2,1)} async-done(((bf16[1,4,65536]{2,1,0:T(4,128)(2,1)}), bf16[4,4,65536]{2,1,0:T(4,128)(2,1)}) %all-gather.3.cloned.1.call-update) | async-done | bytes 2097168 | tf_op jit(solution)/shard_map/all_gather | solution.py:54
  59.4 4.4 %gather_fusion = bf16[24,65536]{1,0:T(8,128)(2,1)} fusion(bf16[16,65536]{1,0:T(8,128)(2,1)S(1)} %reshape.338, s32[1024]{0:T(1024)} %pad_clamp_fusion), kind=kCustom, calls=%fused_computation | custom fusion | bytes 6291552 | tf_op jit(solution)/shard_map/jit(_take)/gather | solution.py:56
  63.8 4.2 %gather.7 = bf16[24,128,2,256]{3,2,1,0:T(2,128)(2,1)S(1)} reshape(bf16[24,65536]{1,0:T(8,128)(2,1)} %gather_fusion) | data formatting | bytes 6291456 | tf_op jit(solution)/shard_map/jit(_take)/gather | solution.py:56
  68.0 3.5 %broadcast_select_fusion = bf16[24,128,2,256]{3,2,1,0:T(2,128)(2,1)S(1)} fusion(bf16[24,128,2,256]{3,2,1,0:T(2,128)(2,1)S(1)} %gather.7, pred[24]{0:T(512)(128)(4,1)} %compare_and_fusion), kind=kLoop, calls=%fused_computation.29 | loop fusion | flops 1572864 | bytes 6291480 | tf_op jit(solution)/shard_map/jit(_take)/select_n | solution.py:56
  71.5 2.3 %fusion.21 = (bf16[24,128,2,128]{3,2,1,0:T(2,128)(2,1)S(1)}, f32[24,128,2,128]{3,2,1,0:T(2,128)S(1)}) fusion(bf16[24,128,2,256]{3,2,1,0:T(2,128)(2,1)S(1)} %broadcast_select_fusion), kind=kLoop, calls=%fused_computation.71 | loop fusion | flops 786432 | bytes 7864320 | tf_op jit(solution)/shard_map/slice | solution.py:63
  73.8 4.4 %subtract_convert_fusion = (bf16[24,128,2,64]{3,2,1,0:T(2,128)(2,1)S(1)}, bf16[24,128,2,64]{3,2,1,0:T(2,128)(2,1)S(1)}) fusion(f32[24,128,2,128]{3,2,1,0:T(2,128)S(1)} %get-tuple-element.106, f32[24,64]{1,0:T(8,128)S(1)} %copy-done.4, f32[24,64]{1,0:T(8,128)S(1)} %copy-done.3), kind=kLoop, calls=%fused_computation.32 | loop fusion | flops 3145728 | bytes 4730880 | tf_op jit(solution)/shard_map/convert.6
  78.2 4.3 %pad_maximum_fusion = bf16[3072,2,128]{2,1,0:T(2,128)(2,1)S(1)} fusion(bf16[3072,2,64]{2,1,0:T(2,128)(2,1)S(1)} %bitcast.92, bf16[3072,2,64]{2,1,0:T(2,128)(2,1)S(1)} %bitcast.91), kind=kLoop, calls=%fused_computation.38 | loop fusion | flops 3145728 | bytes 3145728 | tf_op jit(solution)/shard_map/concatenate | solution.py:18
  82.5 12.3 %scatter_fusion = bf16[3072,2,128]{2,1,0:T(2,128)(2,1)S(1)} fusion(bf16[3072,2,128]{2,1,0:T(2,128)(2,1)S(1)} %pad_maximum_fusion, s32[384]{0:T(512)} %fusion.17, bf16[384,2,128]{2,1,0:T(2,128)(2,1)S(1)} %pad_maximum_fusion.3), kind=kCustom, calls=%fused_computation.1 | custom fusion | bytes 591360 | tf_op jit(solution)/shard_map/scatter | solution.py:70
  94.8 3.4 %fusion.24 = (bf16[3072,1,128]{2,1,0:T(2,128)(2,1)}, bf16[3072,1,128]{2,1,0:T(2,128)(2,1)}) fusion(bf16[3072,2,128]{2,1,0:T(2,128)(2,1)S(1)} %scatter_fusion), kind=kLoop, calls=%fused_computation.74 | loop fusion | bytes 3145728 | tf_op jit(solution)/shard_map/slice | solution.py:82
  98.3 12.2 %scatter_fusion.1 = bf16[3072,2,128]{2,1,0:T(2,128)(2,1)S(1)} fusion(bf16[3072,2,128]{2,1,0:T(2,128)(2,1)S(1)} %bitcast.90, s32[384]{0:T(512)S(1)} %copy-done.5, bf16[384,2,128]{2,1,0:T(2,128)(2,1)S(1)} %get-tuple-element.115), kind=kCustom, calls=%fused_computation.2 | custom fusion | bytes 591360 | tf_op jit(solution)/shard_map/scatter | solution.py:71
  110.4 2.5 %fusion.23 = (bf16[3072,1,128]{2,1,0:T(2,128)(2,1)S(1)}, bf16[3072,1,128]{2,1,0:T(2,128)(2,1)S(1)}) fusion(bf16[3072,2,128]{2,1,0:T(2,128)(2,1)S(1)} %scatter_fusion.1), kind=kLoop, calls=%fused_computation.73 | loop fusion | bytes 3145728 | tf_op jit(solution)/shard_map/slice | solution.py:83
  114.3 27.9 %while.21 = (s32[]{:T(128)}, bf16[6,512,128]{2,1,0:T(8,128)(2,1)S(1)}, s32[6,512]{1,0:T(8,128)S(1)}, bf16[6,512,128]{2,1,0:T(8,128)(2,1)}, bf16[3072,128]{1,0:T(...) while((s32[]{:T(128)}, bf16[6,512,128]{2,1,0:T(8,128)(2,1)S(1)}, s32[6,512]{1,0:T(8,128)S(1)}, ...), condition=%wide.region_11.12_spmd, body=%wide.region_8.11_spmd.sunk | while | flops 819526656 | bytes 23871612 | solution.py:89
  114.4 2.2 %fusion.47 = (f32[512]{0:T(512)S(1)}, f32[512,3072]{1,0:T(8,128)S(1)}) fusion(bf16[3072,128]{1,0:T(8,128)(2,1)S(1)} %get-tuple-element.225, bf16[6,512,128]{2,1,0:T(8,128)(2,1)} %get-tuple-element.224, s32[]{:T(128)S(6)} %copy.53, s32[512]{0:T(512)S(1)} %bitcast.98), kind=kOutput, calls=%fused_computation.70.clone.1 | convolution fusion | flops 408944128 | bytes 7213060 | tf_op jit(solution)/shard_map/while/body/eval_jaxpr/dot_general | solution.py:33
  119.0 2.2 %fusion.47 = (f32[512]{0:T(512)S(1)}, f32[512,3072]{1,0:T(8,128)S(1)}) fusion(bf16[3072,128]{1,0:T(8,128)(2,1)S(1)} %get-tuple-element.225, bf16[6,512,128]{2,1,0:T(8,128)(2,1)} %get-tuple-element.224, s32[]{:T(128)S(6)} %copy.53, s32[512]{0:T(512)S(1)} %bitcast.98), kind=kOutput, calls=%fused_computation.70.clone.1 | convolution fusion | flops 408944128 | bytes 7213060 | tf_op jit(solution)/shard_map/while/body/eval_jaxpr/dot_general | solution.py:33
  128.3 2.2 %fusion.47 = (f32[512]{0:T(512)S(1)}, f32[512,3072]{1,0:T(8,128)S(1)}) fusion(bf16[3072,128]{1,0:T(8,128)(2,1)S(1)} %get-tuple-element.225, bf16[6,512,128]{2,1,0:T(8,128)(2,1)} %get-tuple-element.224, s32[]{:T(128)S(6)} %copy.53, s32[512]{0:T(512)S(1)} %bitcast.98), kind=kOutput, calls=%fused_computation.70.clone.1 | convolution fusion | flops 408944128 | bytes 7213060 | tf_op jit(solution)/shard_map/while/body/eval_jaxpr/dot_general | solution.py:33
  132.9 2.2 %fusion.47 = (f32[512]{0:T(512)S(1)}, f32[512,3072]{1,0:T(8,128)S(1)}) fusion(bf16[3072,128]{1,0:T(8,128)(2,1)S(1)} %get-tuple-element.225, bf16[6,512,128]{2,1,0:T(8,128)(2,1)} %get-tuple-element.224, s32[]{:T(128)S(6)} %copy.53, s32[512]{0:T(512)S(1)} %bitcast.98), kind=kOutput, calls=%fused_computation.70.clone.1 | convolution fusion | flops 408944128 | bytes 7213060 | tf_op jit(solution)/shard_map/while/body/eval_jaxpr/dot_general | solution.py:33
  137.6 2.2 %fusion.47 = (f32[512]{0:T(512)S(1)}, f32[512,3072]{1,0:T(8,128)S(1)}) fusion(bf16[3072,128]{1,0:T(8,128)(2,1)S(1)} %get-tuple-element.225, bf16[6,512,128]{2,1,0:T(8,128)(2,1)} %get-tuple-element.224, s32[]{:T(128)S(6)} %copy.53, s32[512]{0:T(512)S(1)} %bitcast.98), kind=kOutput, calls=%fused_computation.70.clone.1 | convolution fusion | flops 408944128 | bytes 7213060 | tf_op jit(solution)/shard_map/while/body/eval_jaxpr/dot_general | solution.py:33
  142.3 27.2 %while.20 = (s32[]{:T(128)}, bf16[6,512,128]{2,1,0:T(8,128)(2,1)S(1)}, s32[6,512]{1,0:T(8,128)S(1)}, bf16[6,512,128]{2,1,0:T(8,128)(2,1)}, bf16[3072,128]{1,0:T(...) while((s32[]{:T(128)}, bf16[6,512,128]{2,1,0:T(8,128)(2,1)S(1)}, s32[6,512]{1,0:T(8,128)S(1)}, ...), condition=%wide.region_7.8_spmd, body=%wide.region_4.7_spmd.sunk | while | flops 819526656 | bytes 20725856 | solution.py:89
  142.3 2.2 %fusion.42 = (f32[512]{0:T(512)S(1)}, f32[512,3072]{1,0:T(8,128)S(1)}) fusion(bf16[3072,128]{1,0:T(8,128)(2,1)S(1)} %get-tuple-element.246, bf16[6,512,128]{2,1,0:T(8,128)(2,1)} %get-tuple-element.245, s32[]{:T(128)S(6)} %copy.59, s32[512]{0:T(512)S(1)} %bitcast.99), kind=kOutput, calls=%fused_computation.69.clone.1 | convolution fusion | flops 408944128 | bytes 7213060 | tf_op jit(solution)/shard_map/while/body/eval_jaxpr/dot_general | solution.py:33
  146.9 2.2 %fusion.42 = (f32[512]{0:T(512)S(1)}, f32[512,3072]{1,0:T(8,128)S(1)}) fusion(bf16[3072,128]{1,0:T(8,128)(2,1)S(1)} %get-tuple-element.246, bf16[6,512,128]{2,1,0:T(8,128)(2,1)} %get-tuple-element.245, s32[]{:T(128)S(6)} %copy.59, s32[512]{0:T(512)S(1)} %bitcast.99), kind=kOutput, calls=%fused_computation.69.clone.1 | convolution fusion | flops 408944128 | bytes 7213060 | tf_op jit(solution)/shard_map/while/body/eval_jaxpr/dot_general | solution.py:33
  151.4 2.2 %fusion.42 = (f32[512]{0:T(512)S(1)}, f32[512,3072]{1,0:T(8,128)S(1)}) fusion(bf16[3072,128]{1,0:T(8,128)(2,1)S(1)} %get-tuple-element.246, bf16[6,512,128]{2,1,0:T(8,128)(2,1)} %get-tuple-element.245, s32[]{:T(128)S(6)} %copy.59, s32[512]{0:T(512)S(1)} %bitcast.99), kind=kOutput, calls=%fused_computation.69.clone.1 | convolution fusion | flops 408944128 | bytes 7213060 | tf_op jit(solution)/shard_map/while/body/eval_jaxpr/dot_general | solution.py:33
  155.9 2.2 %fusion.42 = (f32[512]{0:T(512)S(1)}, f32[512,3072]{1,0:T(8,128)S(1)}) fusion(bf16[3072,128]{1,0:T(8,128)(2,1)S(1)} %get-tuple-element.246, bf16[6,512,128]{2,1,0:T(8,128)(2,1)} %get-tuple-element.245, s32[]{:T(128)S(6)} %copy.59, s32[512]{0:T(512)S(1)} %bitcast.99), kind=kOutput, calls=%fused_computation.69.clone.1 | convolution fusion | flops 408944128 | bytes 7213060 | tf_op jit(solution)/shard_map/while/body/eval_jaxpr/dot_general | solution.py:33
  160.5 2.2 %fusion.42 = (f32[512]{0:T(512)S(1)}, f32[512,3072]{1,0:T(8,128)S(1)}) fusion(bf16[3072,128]{1,0:T(8,128)(2,1)S(1)} %get-tuple-element.246, bf16[6,512,128]{2,1,0:T(8,128)(2,1)} %get-tuple-element.245, s32[]{:T(128)S(6)} %copy.59, s32[512]{0:T(512)S(1)} %bitcast.99), kind=kOutput, calls=%fused_computation.69.clone.1 | convolution fusion | flops 408944128 | bytes 7213060 | tf_op jit(solution)/shard_map/while/body/eval_jaxpr/dot_general | solution.py:33
  165.0 2.2 %fusion.42 = (f32[512]{0:T(512)S(1)}, f32[512,3072]{1,0:T(8,128)S(1)}) fusion(bf16[3072,128]{1,0:T(8,128)(2,1)S(1)} %get-tuple-element.246, bf16[6,512,128]{2,1,0:T(8,128)(2,1)} %get-tuple-element.245, s32[]{:T(128)S(6)} %copy.59, s32[512]{0:T(512)S(1)} %bitcast.99), kind=kOutput, calls=%fused_computation.69.clone.1 | convolution fusion | flops 408944128 | bytes 7213060 | tf_op jit(solution)/shard_map/while/body/eval_jaxpr/dot_general | solution.py:33
  (105 shorter events, 52.1 us)
Async XLA Ops:
  6.5 51.0 %all-gather.3.cloned.1.call-start = ((), (), s32[]{:S(2)}) async-start(), calls=%async_computation | async-start | bytes 2621440 | tf_op jit(solution)/shard_map/all_gather | solution.py:54
  12.2 0.7 copy-start.8
  12.2 0.7 copy-start.10
  12.3 1.3 copy-start.7
  12.3 1.5 copy-start.6
  19.6 2.0 %copy-start.9 = (s32[1,24]{1,0:T(1,128)S(1)}, s32[1,24]{1,0:T(1,128)}, u32[]{:S(2)}) copy-start(s32[1,24]{1,0:T(1,128)} %param.13) | copy-start | bytes 292
  19.6 2.0 %copy-start.11 = (s32[1,24,1]{1,2,0:T(1,128)S(1)}, s32[1,24,1]{1,2,0:T(1,128)}, u32[]{:S(2)}) copy-start(s32[1,24,1]{1,2,0:T(1,128)} %param.12) | copy-start | bytes 292
  71.4 2.3 %copy-start.3 = (f32[24,64]{1,0:T(8,128)S(1)}, f32[24,64]{1,0:T(8,128)}, u32[]{:S(2)}) copy-start(f32[24,64]{1,0:T(8,128)} %get-tuple-element.119) | copy-start | bytes 18436
  71.5 2.3 %copy-start.4 = (f32[24,64]{1,0:T(8,128)S(1)}, f32[24,64]{1,0:T(8,128)}, u32[]{:S(2)}) copy-start(f32[24,64]{1,0:T(8,128)} %get-tuple-element.120) | copy-start | bytes 18436
  94.8 3.4 %copy-start.5 = (s32[384]{0:T(512)S(1)}, s32[384]{0:T(512)}, u32[]{:S(2)}) copy-start(s32[384]{0:T(512)} %fusion.17) | copy-start | bytes 4612
  110.4 2.5 %copy-start = (bf16[3072,1,128]{2,1,0:T(2,128)(2,1)S(1)}, bf16[3072,1,128]{2,1,0:T(2,128)(2,1)}, u32[]{:S(2)}) copy-start(bf16[3072,1,128]{2,1,0:T(2,128)(2,1)} %get-tuple-element.111) | copy-start | bytes 2359300
  110.4 2.5 %copy-start.1 = (bf16[3072,1,128]{2,1,0:T(2,128)(2,1)S(1)}, bf16[3072,1,128]{2,1,0:T(2,128)(2,1)}, u32[]{:S(2)}) copy-start(bf16[3072,1,128]{2,1,0:T(2,128)(2,1)} %get-tuple-element.112) | copy-start | bytes 2359300
  116.6 1.1 copy-start.2
  121.2 1.1 copy-start.2
  125.9 1.1 copy-start.2
  130.5 1.1 copy-start.2
  135.2 1.1 copy-start.2
  139.8 1.1 copy-start.2
Sparse Core Ops, SparseCore 0:
  8.9 48.5 all-gather.2
where the time goes:
time: 180 us; the launch traced here: 179 us
  local copies, waits for them, and re-layouts  49.4 us (27%)
  matrix products  41.8 us (23%)
  other arithmetic  38.7 us (22%)
  waiting for transfers between devices  34.6 us (19%)
  between operations  13.7 us (8%)
    all_gather x1, waiting for transfers between devices, on_device(): everything = lax.all_gather(store_flat, 'req', axis=0, tiled=True)  34.6 us
    dot_general x12, matrix products, attend_head(): lax.dot_general(query_rows, key_rows, (((1,), (1,)), ((), ())), preferred...  26.7 us
    dot_general x12, matrix products, attend_head(): jnp.dot(probs, value_rows, preferred_element_type=jnp.float32)  15.1 us
    scatter x1, local copies, waits for them, and re-layouts, on_device(): key_rows = key_rows.at[row_pos].set(fresh_keys)  12.3 us
    scatter x1, local copies, waits for them, and re-layouts, on_device(): value_rows = value_rows.at[row_pos].set(fresh[..., head_dim:])  12.2 us
    reduce_sum x12, other arithmetic, attend_head(): jnp.sum(weights, axis=1, keepdims=True)  11.9 us
    gather x2, local copies, waits for them, and re-layouts, on_device(): cached = jnp.take(everything, wanted, axis=0)  8.58 us
    concatenate x3, other arithmetic, rotate(): jnp.concatenate([first_half * cosine - second * sine_part, second * cosin...  6.86 us
  transfers between devices with their start and end apart: 1, of which 1 were waited for; matrix products, arithmetic and copies ran while one was open for 8% of the time, Pallas kernels for 0%

commit v1 on v0

v1 whole, which is shorter than its diff:
```python
import functools
import math

import jax
import jax.numpy as jnp
from jax import lax
from jax.experimental import pallas as pl
from jax.experimental.pallas import tpu as pltpu
from jax.sharding import PartitionSpec as P

rope_base = 500000.0
tile_rows = 32
low = -1e30
far = 1 << 20
vmem = pl.BlockSpec(memory_space=pltpu.VMEM)
smem = pl.BlockSpec(memory_space=pltpu.SMEM)
anywhere = pl.BlockSpec(memory_space=pl.ANY)
params = pltpu.CompilerParams(vmem_limit_bytes=56 << 20)


def tables(position, head_dim):
    half_dim = head_dim // 2
    pair_index = jnp.arange(half_dim, dtype=jnp.float32)
    inv_freq = jnp.exp(pair_index * (-2.0 / head_dim) * jnp.log(jnp.float32(rope_base)))
    angles = position[:, None] * inv_freq
    cosine = jnp.cos(angles)
    sine = jnp.sin(angles)
    return (
        jnp.concatenate([cosine, cosine], axis=1),
        jnp.concatenate([-sine, sine], axis=1),
    )


def span_offsets(lengths, block_count, block_len):
    starts = jnp.cumsum(lengths) - lengths
    block_ids = jnp.arange(block_count, dtype=jnp.int32)
    began = jnp.where(starts[None, :] <= block_ids[:, None], starts[None, :], 0)
    return jnp.max(began, axis=1) * block_len


def turn(field, cosine, sine):
    return field * cosine + pltpu.roll(field, field.shape[1] // 2, 1) * sine


def prepare(query_ref, fresh_ref, cos_ref, sin_ref, pos_ref, turned_ref, placed_ref, wide_ref, all_ref):
    heads, tiles, lanes_rows, dim = turned_ref.shape
    group = lanes_rows // tile_rows
    blocks, block_len, _ = placed_ref.shape
    rows = cos_ref.shape[0]

    def turn_tile(tile, carry):
        at = pl.ds(pl.multiple_of(tile * tile_rows, tile_rows), tile_rows)
        cosine = cos_ref[at, :]
        sine = sin_ref[at, :]
        for head in range(heads):
            for member in range(group):
                column = (head * group + member) * dim
                field = query_ref[at, column : column + dim].astype(jnp.float32)
                turned_ref[head, tile, member * tile_rows : (member + 1) * tile_rows, :] = turn(
                    field, cosine, sine
                ).astype(jnp.bfloat16)
        return carry

    lax.fori_loop(0, tiles, turn_tile, 0)
    wide_ref[...] = fresh_ref[...].astype(jnp.float32)
    for head in range(heads):
        key = wide_ref[pl.ds(head, rows, stride=2 * heads), :]
        value = wide_ref[pl.ds(heads + head, rows, stride=2 * heads), :]
        all_ref[:, head * 2 * dim : head * 2 * dim + dim] = turn(
            key, cos_ref[...], sin_ref[...]
        ).astype(jnp.bfloat16)
        all_ref[:, head * 2 * dim + dim : (head + 1) * 2 * dim] = value.astype(jnp.bfloat16)
    all_ref[:, heads * 2 * dim :] = jnp.ones((rows, dim), jnp.bfloat16)

    def place(block, carry):
        spot = lax.broadcasted_iota(jnp.int32, (block_len, rows), 0) + block * block_len
        chosen = jnp.where(spot == pos_ref[...], 1.0, 0.0).astype(jnp.bfloat16)
        placed_ref[block] = jnp.dot(
            chosen, all_ref[...], preferred_element_type=jnp.float32
        ).astype(jnp.bfloat16)
        return carry

    lax.fori_loop(0, blocks, place, 0)


def attend(counts, blocks, slots, first, last, *refs):
    given = len(counts)
    sources = refs[:given]
    meta_ref, turned_ref, placed_ref, cos_ref, sin_ref, row_ref = refs[given : given + 6]
    refs = refs[given + 6 :]
    if not first:
        most_in, sum_in, acc_in = refs[:3]
        refs = refs[3:]
    if last:
        out_ref = refs[0]
        refs = refs[1:]
    else:
        most_out, sum_out, acc_out = refs[:3]
        refs = refs[3:]
    raw_ref, wide_ref, key_ref, value_ref, score_ref, list_ref, sems = refs
    heads, tiles, lanes_rows, dim = turned_ref.shape
    group = lanes_rows // tile_rows
    block_len = placed_ref.shape[1]
    stride = 2 * heads
    raw_rows = block_len * stride
    scale = dim**-0.5 * math.log2(math.e)
    bounds_at = 2 * blocks
    first_at = bounds_at + blocks + 1

    def find(block, found):
        owner = meta_ref[block]
        slot = meta_ref[blocks + block]
        hit = owner < 0
        for number in range(given):
            lowest = meta_ref[first_at + number]
            here = (owner >= lowest) & (owner < lowest + counts[number])
            hit = hit | here

            @pl.when(here)
            def _(number=number, lowest=lowest):
                start = pl.multiple_of(((owner - lowest) * slots + slot) * raw_rows, raw_rows)
                pltpu.make_async_copy(
                    sources[number].at[pl.ds(start, raw_rows), :], raw_ref.at[found], sems.at[found]
                ).start()

        list_ref[found] = block
        return found + hit.astype(jnp.int32)

    found = lax.fori_loop(0, blocks, find, jnp.int32(0))

    def load(spot, carry):
        block = list_ref[spot]
        pltpu.make_async_copy(
            sources[0].at[pl.ds(0, raw_rows), :], raw_ref.at[spot], sems.at[spot]
        ).wait()
        wide_ref[...] = raw_ref[spot].astype(jnp.float32)
        cosine = cos_ref[pl.ds(block, 1), :]
        sine = sin_ref[pl.ds(block, 1), :]
        fresh = placed_ref[block].astype(jnp.float32)
        renewed = fresh[:, heads * 2 * dim :] > 0.5
        at = pl.ds(pl.multiple_of(spot * block_len, block_len), block_len)
        for head in range(heads):
            key = turn(wide_ref[pl.ds(head, block_len, stride=stride), :], cosine, sine)
            value = wide_ref[pl.ds(heads + head, block_len, stride=stride), :]
            begin = head * 2 * dim
            key_ref[head, at, :] = jnp.where(renewed, fresh[:, begin : begin + dim], key).astype(
                jnp.bfloat16
            )
            value_ref[head, at, :] = jnp.where(
                renewed, fresh[:, begin + dim : begin + 2 * dim], value
            ).astype(jnp.bfloat16)
        return carry

    lax.fori_loop(0, found, load, 0)
    list_ref[found] = far

    @pl.when(found % 2 == 1)
    def _():
        at = pl.ds(pl.multiple_of(found * block_len, block_len), block_len)
        for head in range(heads):
            key_ref[head, at, :] = jnp.zeros((block_len, dim), jnp.bfloat16)
            value_ref[head, at, :] = jnp.zeros((block_len, dim), jnp.bfloat16)

    pairs = (found + 1) // 2

    def per_tile(tile, carry):
        def reach(pair, tally):
            early = list_ref[2 * pair]
            late = list_ref[2 * pair + 1]
            begins = meta_ref[bounds_at + early] < (tile + 1) * tile_rows
            past = (late < blocks) & (
                meta_ref[bounds_at + jnp.minimum(late, blocks - 1) + 1] <= tile * tile_rows
            )
            return tally[0] + begins.astype(jnp.int32), tally[1] + past.astype(jnp.int32)

        active, clear = lax.fori_loop(0, pairs, reach, (jnp.int32(0), jnp.int32(0)))
        clear = jnp.minimum(clear, active)

        def score(pair, masked, most):
            at = pl.ds(pl.multiple_of(pair * 2 * block_len, 2 * block_len), 2 * block_len)
            if masked:
                row_at = pl.ds(pl.multiple_of(tile * tile_rows, tile_rows), tile_rows)
                lane = lax.broadcasted_iota(jnp.int32, (tile_rows, block_len), 1)
                row_pos = row_ref[row_at, :]
                seen = jnp.concatenate(
                    [
                        lane + list_ref[2 * pair + side] * block_len <= row_pos
                        for side in range(2)
                    ],
                    axis=1,
                )
            after = []
            for head in range(heads):
                scores = lax.dot_general(
                    turned_ref[head, tile],
                    key_ref[head, at, :],
                    (((1,), (1,)), ((), ())),
                    preferred_element_type=jnp.float32,
                )
                if masked:
                    scores = jnp.where(
                        seen[None], scores.reshape(group, tile_rows, 2 * block_len), 2 * low
                    ).reshape(lanes_rows, 2 * block_len)
                score_ref[head, pair] = scores
                after.append(
                    jnp.maximum(
                        most[head],
                        jnp.maximum(scores[:, :block_len], scores[:, block_len:]),
                    )
                )
            return tuple(after)

        start = tuple(jnp.full((lanes_rows, block_len), low, jnp.float32) for _ in range(heads))
        most = lax.fori_loop(0, clear, lambda pair, now: score(pair, False, now), start)
        most = lax.fori_loop(clear, active, lambda pair, now: score(pair, True, now), most)
        tops = []
        begun = []
        for head in range(heads):
            top = jnp.broadcast_to(jnp.max(most[head], axis=1, keepdims=True), (lanes_rows, dim))
            if first:
                begun.append(jnp.zeros((lanes_rows, dim), jnp.float32))
                begun.append(jnp.zeros((lanes_rows, dim), jnp.float32))
            else:
                before = most_in[head, tile]
                top = jnp.maximum(top, before)
                shrink = jnp.exp2((before - top) * scale)
                begun.append(sum_in[head, tile] * shrink)
                begun.append(acc_in[head, tile] * shrink)
            tops.append(top)

        def gather(pair, now):
            at = pl.ds(pl.multiple_of(pair * 2 * block_len, 2 * block_len), 2 * block_len)
            after = []
            for head in range(heads):
                scores = score_ref[head, pair]
                left = jnp.exp2((scores[:, :block_len] - tops[head]) * scale)
                right = jnp.exp2((scores[:, block_len:] - tops[head]) * scale)
                after.append(now[2 * head] + (left + right))
                weights = jnp.concatenate(
                    [left.astype(jnp.bfloat16), right.astype(jnp.bfloat16)], axis=1
                )
                after.append(
                    now[2 * head + 1]
                    + jnp.dot(
                        weights, value_ref[head, at, :], preferred_element_type=jnp.float32
                    )
                )
            return tuple(after)

        ended = lax.fori_loop(0, active, gather, tuple(begun))
        for head in range(heads):
            if last:
                total = jnp.sum(ended[2 * head], axis=1, keepdims=True)
                result = (ended[2 * head + 1] / total).astype(jnp.bfloat16)
                row_at = pl.ds(pl.multiple_of(tile * tile_rows, tile_rows), tile_rows)
                for member in range(group):
                    column = (head * group + member) * dim
                    out_ref[row_at, column : column + dim] = result[
                        member * tile_rows : (member + 1) * tile_rows
                    ]
            else:
                most_out[head, tile] = tops[head]
                sum_out[head, tile] = ended[2 * head]
                acc_out[head, tile] = ended[2 * head + 1]
        return carry

    lax.fori_loop(0, tiles, per_tile, 0)


def on_device(count, store_kv, block_owner, block_slot, span_len, row_index, fresh_q, fresh_kv):
    stored, block_len, heads, pair_width = store_kv.shape
    dim = pair_width // 2
    blocks = block_slot.shape[1]
    rows = row_index.shape[1]
    group = fresh_q.shape[2] // (heads * dim)
    tiles = rows // tile_rows
    lanes_rows = tile_rows * group
    raw_rows = block_len * 2 * heads

    def flat(array):
        lead = math.prod(array.shape[:-2])
        split = array.reshape(lead, heads, 2, dim)
        return split.transpose(0, 2, 1, 3).reshape(lead * 2 * heads, dim)

    place = lax.axis_index("req")
    store = flat(store_kv)
    none = jnp.int32(-(1 << 16))
    if count == 4:
        outer = [(0, 1), (1, 0), (2, 3), (3, 2)]
        inner = [(1, 2), (2, 1)]
        outward = [(1, 0), (2, 3)]
        send = lambda array, pairs: lax.ppermute(array, "req", pairs)
        beside = send(store, outer)
        across = send(store, inner)
        second = send(across, outward)
        third_in = send(beside, inner)
        third = send(third_in, outward)
        middle = (place == 1) | (place == 2)
        far_two = jnp.where(place == 0, 2, 1)
        far_three = jnp.where(place == 0, 3, 0)
        phases = [
            ((store, place, 1), (beside, place ^ 1, 1)),
            (
                (second, jnp.where(middle, none, far_two), 1),
                (across, jnp.where(middle, 3 - place, none), 1),
            ),
            (
                (third, jnp.where(middle, none, far_three), 1),
                (third_in, jnp.where(middle, (3 - place) ^ 1, none), 1),
            ),
        ]
    else:
        everything = lax.all_gather(store, "req", axis=0, tiled=True)
        phases = [((everything, jnp.int32(0), count),)]

    row_pos = row_index[0]
    bounds = jnp.sum(
        row_pos[None, :] < block_len * jnp.arange(blocks + 1, dtype=jnp.int32)[:, None],
        axis=1,
        dtype=jnp.int32,
    )
    row_cos, row_sin = tables(row_pos.astype(jnp.float32), dim)
    offset = span_offsets(span_len[0], blocks, block_len)
    cos, sin = tables(offset.astype(jnp.float32), dim)
    row_lanes = jnp.broadcast_to(row_pos[:, None], (rows, block_len))
    turned, placed = pl.pallas_call(
        prepare,
        out_shape=(
            jax.ShapeDtypeStruct((heads, tiles, lanes_rows, dim), jnp.bfloat16),
            jax.ShapeDtypeStruct((blocks, block_len, heads * 2 * dim + dim), jnp.bfloat16),
        ),
        in_specs=[vmem] * 5,
        out_specs=(vmem, vmem),
        scratch_shapes=[
            pltpu.VMEM((rows * 2 * heads, dim), jnp.float32),
            pltpu.VMEM((rows, heads * 2 * dim + dim), jnp.bfloat16),
        ],
        compiler_params=params,
        name="prepare",
    )(fresh_q[0], flat(fresh_kv), row_cos, row_sin, row_pos[None])
    state_shape = jax.ShapeDtypeStruct((heads, tiles, lanes_rows, dim), jnp.float32)
    state = ()
    for number, phase in enumerate(phases):
        begin = number == 0
        end = number == len(phases) - 1
        meta = jnp.concatenate(
            [block_owner[0, :, 0], block_slot[0], bounds, jnp.stack([entry[1] for entry in phase])]
        )
        inputs = [entry[0] for entry in phase] + [meta, turned, placed, cos, sin, row_lanes]
        specs = [anywhere] * len(phase) + [smem] + [vmem] * 5
        most = blocks if len(phases) == 1 else min(blocks, 24)
        state = pl.pallas_call(
            functools.partial(
                attend, tuple(entry[2] for entry in phase), blocks, stored, begin, end
            ),
            out_shape=jax.ShapeDtypeStruct((rows, heads * group * dim), jnp.bfloat16)
            if end
            else (state_shape,) * 3,
            in_specs=specs + [vmem] * len(state),
            out_specs=vmem if end else (vmem,) * 3,
            scratch_shapes=[
                pltpu.VMEM((most, raw_rows, dim), jnp.bfloat16),
                pltpu.VMEM((raw_rows, dim), jnp.float32),
                pltpu.VMEM((heads, (most + 2) * block_len, dim), jnp.bfloat16),
                pltpu.VMEM((heads, (most + 2) * block_len, dim), jnp.bfloat16),
                pltpu.VMEM((heads, most // 2 + 1, lanes_rows, 2 * block_len), jnp.float32),
                pltpu.SMEM((most + 2,), jnp.int32),
                pltpu.SemaphoreType.DMA((most,)),
            ],
            compiler_params=params,
            name=f"attend_{number}",
        )(*inputs, *state)
    return state[None]


def solution(mesh):
    placed = (
        P(("grp", "req"), None, "kvh", None),
        P(("grp", "req"), None, None),
        P(("grp", "req"), None),
        P(("grp", "req"), None),
        P(("grp", "req"), None),
        P(("grp", "req"), None, "kvh"),
        P(("grp", "req"), None, "kvh", None),
    )
    return jax.shard_map(
        functools.partial(on_device, mesh.shape["req"]),
        mesh=mesh,
        in_specs=placed,
        out_specs=P(("grp", "req"), None, "kvh"),
        check_vma=False,
    )
```

time: 180 us -> 132 us (0.73)
  the two profiles are of different devices: /device:TPU:0 before, /device:TPU:14 now
where the time goes in v1:
time: 132 us
  Pallas kernels  104 us (79%)
  starting transfers between devices  11.2 us (8%)
  waiting for transfers between devices  6.49 us (5%)
  local copies, waits for them, and re-layouts  6.2 us (5%)
  other arithmetic  4.33 us (3%)
    pallas_call x3, Pallas kernels, on_device(): pl.pallas_call(functools.partial(attend, tuple((entry[2] for entry in pha...  91.8 us
    pallas_call x1, Pallas kernels, on_device(): pl.pallas_call(prepare, out_shape=(jax.ShapeDtypeStruct((heads, tiles, la...  11.7 us
    ppermute x5, starting transfers between devices, on_device(): send = lambda array, pairs: lax.ppermute(array, 'req', pairs)  11.2 us
    ppermute x5, waiting for transfers between devices, on_device(): send = lambda array, pairs: lax.ppermute(array, 'req', pairs)  6.49 us
    concatenate x3, local copies, waits for them, and re-layouts, on_device(): jnp.concatenate([block_owner[0, :, 0], block_slot[0], bounds, jnp.stack([...  3.82 us
  transfers between devices with their start and end apart: 5, of which 1 were waited for; matrix products, arithmetic and copies ran while one was open for 7% of the time, Pallas kernels for 56%

profile of v1, /device:TPU:14, one launch (start us, length us, event | category | flops | bytes accessed | tf_op | source)
XLA Modules:
  0.0 131.9 jit_solution(3402036898932674)
XLA Ops:
  0.0 0.4 collective-permute-start
  0.5 4.6 %collective-permute-start.3 = (bf16[2048,128]{1,0:T(8,128)(2,1)}, bf16[2048,128]{1,0:T(8,128)(2,1)S(1)}, u32[]{:S(2)}, u32[]{:S(2)}) collective-permute-start(bf16[2048,128]{1,0:T(8,128)(2,1)} %bitcast.24), channel_id=1, source_target_pairs={{4,8},{8,4},{5,9},{9,5},{6,10},{10,6},{7,11},{11,7},{20,24},{24,20... | collective-permute-start | bytes 1572872 | tf_op jit(solution)/shard_map/ppermute | solution.py:292
  5.1 0.7 reduce
  5.8 0.8 reduce-window_clone.1
  6.6 0.8 fusion
  7.4 6.5 %collective-permute-done.refs_1_ = bf16[2048,128]{1,0:T(8,128)(2,1)S(1)} collective-permute-done((bf16[2048,128]{1,0:T(8,128)(2,1)}, bf16[2048,128]{1,0:T(8,128)(2,1)S(1)}, u32[]{:S(2)}, u32[]{:S(2)}) %collective-permute-start) | collective-permute-done | bytes 524320 | tf_op jit(solution)/shard_map/ppermute | solution.py:292
  13.9 3.5 %collective-permute-start.1 = (bf16[2048,128]{1,0:T(8,128)(2,1)S(1)}, bf16[2048,128]{1,0:T(8,128)(2,1)S(1)}, u32[]{:S(2)}, u32[]{:S(2)}) collective-permute-start(bf16[2048,128]{1,0:T(8,128)(2,1)S(1)} %collective-permute-done.refs_1_), channel_id=1, source_target_pairs={{4,8},{8,4},{5,9},{9,5},{6,10},{10,6},{7,11},{11,7},{20,24},{24,20... | collective-permute-start | bytes 1572872 | tf_op jit(solution)/shard_map/ppermute | solution.py:292
  17.4 0.2 convert_reduce_fusion
  17.5 1.2 concatenate.27.refs_2_
  18.8 1.3 concatenate.26.refs_2_
  20.1 1.3 concatenate.21.refs_2_
  21.4 0.9 pad_maximum_fusion
  22.3 11.7 %prepare.1 = (bf16[2,12,256,128]{3,2,1,0:T(8,128)(2,1)}, bf16[24,128,640]{2,1,0:T(8,128)(2,1)}) custom-call(bf16[384,2048]{1,0:T(8,128)(2,1)} %bitcast.22, bf16[1536,128]{1,0:T(8,128)(2,1)} %bitcast.26, f32[384,128]{1,0:T(8,128)} %get-tuple-element.27.cos_ref, f32[384,128]{1,0:T(8,128)} %get-tuple-element.28.sin_ref, s32[1,384]{1,0:T(1,128)} %pos_ref.1), custom_call_target="tpu_custom_call" | custom-call | tf_op jit(solution)/shard_map/prepare/pallas_call | solution.py:326
  34.0 0.1 select_reduce_fusion
  34.1 1.3 %collective-permute-start.4 = (bf16[2048,128]{1,0:T(8,128)(2,1)S(1)}, bf16[2048,128]{1,0:T(8,128)(2,1)S(1)}, u32[]{:S(2)}, u32[]{:S(2)}) collective-permute-start(bf16[2048,128]{1,0:T(8,128)(2,1)S(1)} %collective-permute-done.3.refs_1_), channel_id=1, source_target_pairs={{4,0},{8,12},{5,1},{9,13},{6,2},{10,14},{7,3},{11,15},{20,16},{24,... | collective-permute-start | bytes 1572872 | tf_op jit(solution)/shard_map/ppermute | solution.py:292
  35.5 1.3 %collective-permute-start.2 = (bf16[2048,128]{1,0:T(8,128)(2,1)S(1)}, bf16[2048,128]{1,0:T(8,128)(2,1)S(1)}, u32[]{:S(2)}, u32[]{:S(2)}) collective-permute-start(bf16[2048,128]{1,0:T(8,128)(2,1)S(1)} %collective-permute-done.1.refs_1_), channel_id=1, source_target_pairs={{4,0},{8,12},{5,1},{9,13},{6,2},{10,14},{7,3},{11,15},{20,16},{24,... | collective-permute-start | bytes 1572872 | tf_op jit(solution)/shard_map/ppermute | solution.py:292
  36.8 0.1 fusion.1
  36.9 0.7 pad_maximum_fusion.2
  37.6 0.8 broadcast_in_dim.15.refs_7_
  38.4 36.0 %attend_0.1 = (f32[2,12,256,128]{3,2,1,0:T(8,128)}, f32[2,12,256,128]{3,2,1,0:T(8,128)}, f32[2,12,256,128]{3,2,1,0:T(8,128)}) custom-call(bf16[2048,128]{1,0:T(8,128)(2,1)} %bitcast.25, bf16[2048,128]{1,0:T(8,128)(2,1)} %copy-done.4, s32[75]{0:T(128)} %concatenate.27.refs_2_, bf16[2,12,256,128]{3,2,1,0:T(8,128)(2,1)} %get-tuple-element.13.refs_3_, ...), custom_call_target="tpu_custom_call" | custom-call | tf_op jit(solution)/shard_map/attend_0/pallas_call | solution.py:352
  74.4 0.8 copy-done.3
  75.2 26.6 %attend_1.1 = (f32[2,12,256,128]{3,2,1,0:T(8,128)}, f32[2,12,256,128]{3,2,1,0:T(8,128)}, f32[2,12,256,128]{3,2,1,0:T(8,128)}) custom-call(bf16[2048,128]{1,0:T(8,128)(2,1)} %copy-done.3, bf16[2048,128]{1,0:T(8,128)(2,1)} %copy-done, s32[75]{0:T(128)} %concatenate.26.refs_2_, bf16[2,12,256,128]{3,2,1,0:T(8,128)(2,1)} %get-tuple-element.13.refs_3_, ...), custom_call_target="tpu_custom_call" | custom-call | tf_op jit(solution)/shard_map/attend_1/pallas_call | solution.py:352
  101.9 0.8 copy-done.2
  102.7 29.2 %attend_2.1 = bf16[384,2048]{1,0:T(8,128)(2,1)} custom-call(bf16[2048,128]{1,0:T(8,128)(2,1)} %copy-done.2, bf16[2048,128]{1,0:T(8,128)(2,1)} %copy-done.1, s32[75]{0:T(128)} %concatenate.21.refs_2_, bf16[2,12,256,128]{3,2,1,0:T(8,128)(2,1)} %get-tuple-element.13.refs_3_, bf16[24,128,640]{2,1,0:T(8,128)(2,1)} %get-tuple-element.14.refs_4_, ...), custom_call_target="tpu_custom_call" | custom-call | tf_op jit(solution)/shard_map/attend_2/pallas_call | solution.py:352
  (19 shorter events, 0.1 us)
Async XLA Ops:
  0.0 34.0 %copy-start.5 = (s32[1,4]{1,0:T(1,128)S(1)}, s32[1,4]{1,0:T(1,128)}, u32[]{:S(2)}) copy-start(s32[1,4]{1,0:T(1,128)} %param.10) | copy-start | bytes 52
  0.0 13.9 %collective-permute-start = (bf16[2048,128]{1,0:T(8,128)(2,1)}, bf16[2048,128]{1,0:T(8,128)(2,1)S(1)}, u32[]{:S(2)}, u32[]{:S(2)}) collective-permute-start(bf16[2048,128]{1,0:T(8,128)(2,1)} %bitcast.23), channel_id=1, source_target_pairs={{0,4},{4,0},{8,12},{12,8},{1,5},{5,1},{9,13},{13,9},{2,6},{6,2},{1... | collective-permute-start | bytes 1572872 | tf_op jit(solution)/shard_map/ppermute | solution.py:292
  0.5 33.6 %collective-permute-start.3 = (bf16[2048,128]{1,0:T(8,128)(2,1)}, bf16[2048,128]{1,0:T(8,128)(2,1)S(1)}, u32[]{:S(2)}, u32[]{:S(2)}) collective-permute-start(bf16[2048,128]{1,0:T(8,128)(2,1)} %bitcast.24), channel_id=1, source_target_pairs={{4,8},{8,4},{5,9},{9,5},{6,10},{10,6},{7,11},{11,7},{20,24},{24,20... | collective-permute-start | bytes 1572872 | tf_op jit(solution)/shard_map/ppermute | solution.py:292
  13.9 24.5 %copy-start.4 = (bf16[2048,128]{1,0:T(8,128)(2,1)}, bf16[2048,128]{1,0:T(8,128)(2,1)S(1)}, u32[]{:S(2)}) copy-start(bf16[2048,128]{1,0:T(8,128)(2,1)S(1)} %collective-permute-done.refs_1_) | copy-start | bytes 1572868
  13.9 21.6 %collective-permute-start.1 = (bf16[2048,128]{1,0:T(8,128)(2,1)S(1)}, bf16[2048,128]{1,0:T(8,128)(2,1)S(1)}, u32[]{:S(2)}, u32[]{:S(2)}) collective-permute-start(bf16[2048,128]{1,0:T(8,128)(2,1)S(1)} %collective-permute-done.refs_1_), channel_id=1, source_target_pairs={{4,8},{8,4},{5,9},{9,5},{6,10},{10,6},{7,11},{11,7},{20,24},{24,20... | collective-permute-start | bytes 1572872 | tf_op jit(solution)/shard_map/ppermute | solution.py:292
  34.1 40.3 %copy-start = (bf16[2048,128]{1,0:T(8,128)(2,1)}, bf16[2048,128]{1,0:T(8,128)(2,1)S(1)}, u32[]{:S(2)}) copy-start(bf16[2048,128]{1,0:T(8,128)(2,1)S(1)} %collective-permute-done.3.refs_1_) | copy-start | bytes 1572868
  34.1 40.3 %collective-permute-start.4 = (bf16[2048,128]{1,0:T(8,128)(2,1)S(1)}, bf16[2048,128]{1,0:T(8,128)(2,1)S(1)}, u32[]{:S(2)}, u32[]{:S(2)}) collective-permute-start(bf16[2048,128]{1,0:T(8,128)(2,1)S(1)} %collective-permute-done.3.refs_1_), channel_id=1, source_target_pairs={{4,0},{8,12},{5,1},{9,13},{6,2},{10,14},{7,3},{11,15},{20,16},{24,... | collective-permute-start | bytes 1572872 | tf_op jit(solution)/shard_map/ppermute | solution.py:292
  35.5 39.0 %copy-start.1 = (bf16[2048,128]{1,0:T(8,128)(2,1)}, bf16[2048,128]{1,0:T(8,128)(2,1)S(1)}, u32[]{:S(2)}) copy-start(bf16[2048,128]{1,0:T(8,128)(2,1)S(1)} %collective-permute-done.1.refs_1_) | copy-start | bytes 1572868
  35.5 66.4 %collective-permute-start.2 = (bf16[2048,128]{1,0:T(8,128)(2,1)S(1)}, bf16[2048,128]{1,0:T(8,128)(2,1)S(1)}, u32[]{:S(2)}, u32[]{:S(2)}) collective-permute-start(bf16[2048,128]{1,0:T(8,128)(2,1)S(1)} %collective-permute-done.1.refs_1_), channel_id=1, source_target_pairs={{4,0},{8,12},{5,1},{9,13},{6,2},{10,14},{7,3},{11,15},{20,16},{24,... | collective-permute-start | bytes 1572872 | tf_op jit(solution)/shard_map/ppermute | solution.py:292
  74.4 0.8 copy-start.3
  101.9 0.8 copy-start.2

commit v2 on v0

v2 whole, which is shorter than its diff:
```python
import functools
import math

import jax
import jax.numpy as jnp
from jax import lax
from jax.experimental import pallas as pl
from jax.experimental.pallas import tpu as pltpu
from jax.sharding import PartitionSpec as P

rope_base = 500000.0
tile_rows = 64
unit_blocks = 6
low = -1e30
vmem = pl.BlockSpec(memory_space=pltpu.VMEM)
smem = pl.BlockSpec(memory_space=pltpu.SMEM)
params = pltpu.CompilerParams(vmem_limit_bytes=28 << 20)


def near(array):
    return pltpu.with_memory_space_constraint(array, pltpu.VMEM)


def tables(position, head_dim):
    lane = lax.broadcasted_iota(jnp.int32, (position.shape[0], head_dim), 1)
    half_dim = head_dim // 2
    pair_index = (lane % half_dim).astype(jnp.float32)
    inv_freq = jnp.exp(pair_index * (-2.0 / head_dim) * jnp.log(jnp.float32(rope_base)))
    angles = position[:, None] * inv_freq
    sine = jnp.sin(angles)
    return jnp.cos(angles), jnp.where(lane < half_dim, -sine, sine)


def turn(field, cosine, sine):
    return field * cosine + pltpu.roll(field, field.shape[1] // 2, 1) * sine


def prepare(query_ref, fresh_ref, cos_ref, sin_ref, pos_ref, turned_ref, placed_ref, wide_ref, all_ref):
    heads, tiles, lanes_rows, dim = turned_ref.shape
    group = lanes_rows // tile_rows
    placed_rows = placed_ref.shape[0]
    rows = cos_ref.shape[0]

    def turn_tile(tile, carry):
        at = pl.ds(pl.multiple_of(tile * tile_rows, tile_rows), tile_rows)
        cosine = cos_ref[at, :]
        sine = sin_ref[at, :]
        for head in range(heads):
            for member in range(group):
                column = (head * group + member) * dim
                field = query_ref[at, column : column + dim].astype(jnp.float32)
                turned_ref[head, tile, member * tile_rows : (member + 1) * tile_rows, :] = turn(
                    field, cosine, sine
                ).astype(jnp.bfloat16)
        return carry

    lax.fori_loop(0, tiles, turn_tile, 0)
    wide_ref[...] = fresh_ref[...].astype(jnp.float32)
    for head in range(heads):
        key = wide_ref[pl.ds(head, rows, stride=2 * heads), :]
        value = wide_ref[pl.ds(heads + head, rows, stride=2 * heads), :]
        all_ref[:, head * 2 * dim : head * 2 * dim + dim] = turn(
            key, cos_ref[...], sin_ref[...]
        ).astype(jnp.bfloat16)
        all_ref[:, head * 2 * dim + dim : (head + 1) * 2 * dim] = value.astype(jnp.bfloat16)
    all_ref[:, heads * 2 * dim :] = jnp.ones((rows, dim), jnp.bfloat16)
    step = 512

    def place(number, carry):
        at = pl.ds(pl.multiple_of(number * step, step), step)
        spot = lax.broadcasted_iota(jnp.int32, (step, rows), 0) + number * step
        chosen = jnp.where(spot == pos_ref[...], 1.0, 0.0).astype(jnp.bfloat16)
        placed_ref[at, :] = jnp.dot(
            chosen, all_ref[...], preferred_element_type=jnp.float32
        ).astype(jnp.bfloat16)
        return carry

    lax.fori_loop(0, placed_rows // step, place, 0)


def attend(spans, shards, pick, units, first, last, *refs):
    given = len(pick)
    sources = refs[:given]
    place_ref, owner_ref, slot_ref, span_ref, pos_ref = refs[given : given + 5]
    turned_ref, placed_ref, cos_ref, sin_ref, row_ref = refs[given + 5 : given + 10]
    refs = refs[given + 10 :]
    if not first:
        most_in, sum_in, acc_in = refs[:3]
        refs = refs[3:]
    if last:
        out_ref = refs[0]
        refs = refs[1:]
    else:
        most_out, sum_out, acc_out = refs[:3]
        refs = refs[3:]
    wide_ref, key_ref, value_ref, list_ref = refs[:4]
    if last and units > 1:
        most_out, sum_out, acc_out = refs[4:]
    heads, tiles, lanes_rows, dim = turned_ref.shape
    group = lanes_rows // tile_rows
    blocks = slot_ref.shape[1]
    block_len = placed_ref.shape[0] // blocks
    stride = 2 * heads
    raw_rows = block_len * stride
    slots = sources[0].shape[0] // raw_rows // shards
    scale = dim**-0.5 * math.log2(math.e)
    lowest = [choose(place_ref[0]) for choose in pick]

    def find(block, found):
        owner = owner_ref[0, block]
        hit = jnp.bool_(False)
        for base in lowest:
            hit = hit | ((owner >= base) & (owner < base + shards))
        list_ref[found] = block
        return found + hit.astype(jnp.int32)

    lax.fori_loop(0, blocks, find, jnp.int32(0))

    def load(spot, carry):
        block = list_ref[spot]
        owner = owner_ref[0, block]
        for source, base in zip(sources, lowest):

            @pl.when((owner >= base) & (owner < base + shards))
            def _(source=source, base=base):
                start = ((owner - base) * slots + slot_ref[0, block]) * raw_rows
                wide_ref[...] = source[pl.ds(pl.multiple_of(start, raw_rows), raw_rows), :].astype(
                    jnp.float32
                )

        began = jnp.int32(0)
        start = jnp.int32(0)
        for span in range(spans):
            began = jnp.where(start <= block, start, began)
            start = start + span_ref[0, span]
        cosine = cos_ref[pl.ds(began, 1), :]
        sine = sin_ref[pl.ds(began, 1), :]
        fresh = placed_ref[
            pl.ds(pl.multiple_of(block * block_len, block_len), block_len), :
        ].astype(jnp.float32)
        renewed = fresh[:, heads * 2 * dim :] > 0.5
        at = pl.ds(pl.multiple_of(spot * block_len, block_len), block_len)
        for head in range(heads):
            key = turn(wide_ref[pl.ds(head, block_len, stride=stride), :], cosine, sine)
            value = wide_ref[pl.ds(heads + head, block_len, stride=stride), :]
            begin = head * 2 * dim
            key_ref[head, at, :] = jnp.where(renewed, fresh[:, begin : begin + dim], key).astype(
                jnp.bfloat16
            )
            value_ref[head, at, :] = jnp.where(
                renewed, fresh[:, begin + dim : begin + 2 * dim], value
            ).astype(jnp.bfloat16)
        return carry

    lax.fori_loop(0, units * unit_blocks, load, 0)

    def write(head, tile, state):
        most, total, acc = state
        most_out[head, tile] = most
        sum_out[head, tile] = total
        acc_out[head, tile] = acc

    def extend(tile, unit, count, before, after):
        row_at = pl.ds(pl.multiple_of(tile * tile_rows, tile_rows), tile_rows)
        row_pos = row_ref[row_at, :]
        lane = lax.broadcasted_iota(jnp.int32, (tile_rows, block_len), 1)
        first_spot = unit * unit_blocks
        seen = [
            lane + list_ref[first_spot + spot] * block_len <= row_pos for spot in range(count)
        ]
        at = pl.ds(first_spot * block_len, count * block_len)
        for head in range(heads):
            scores = lax.dot_general(
                turned_ref[head, tile],
                key_ref[head, at, :],
                (((1,), (1,)), ((), ())),
                preferred_element_type=jnp.float32,
            )
            parts = [
                jnp.where(
                    seen[spot][None],
                    scores[:, spot * block_len : (spot + 1) * block_len].reshape(
                        group, tile_rows, block_len
                    ),
                    2 * low,
                ).reshape(lanes_rows, block_len)
                for spot in range(count)
            ]
            most = functools.reduce(jnp.maximum, parts)
            most = jnp.broadcast_to(
                jnp.maximum(jnp.max(most, axis=1, keepdims=True), low), (lanes_rows, block_len)
            )
            if before is not None:
                was_most, was_sum, was_acc = [ref[head, tile] for ref in before]
                most = jnp.maximum(most, was_most)
            parts = [jnp.exp2((part - most) * scale) for part in parts]
            total = functools.reduce(jnp.add, parts)
            acc = jnp.dot(
                jnp.concatenate([part.astype(jnp.bfloat16) for part in parts], axis=1),
                value_ref[head, at, :],
                preferred_element_type=jnp.float32,
            )
            if before is not None:
                shrink = jnp.exp2((was_most - most) * scale)
                total = was_sum * shrink + total
                acc = was_acc * shrink + acc
            after(head, tile, (most, total, acc))

    def finish(head, tile, state):
        most, total, acc = state
        result = (acc / jnp.sum(total, axis=1, keepdims=True)).astype(jnp.bfloat16)
        row_at = pl.ds(pl.multiple_of(tile * tile_rows, tile_rows), tile_rows)
        for member in range(group):
            column = (head * group + member) * dim
            out_ref[row_at, column : column + dim] = result[
                member * tile_rows : (member + 1) * tile_rows
            ]

    def keep(tile, before, after):
        for head in range(heads):
            if before is None:
                nothing = jnp.zeros((lanes_rows, dim), jnp.float32)
                after(head, tile, (nothing + low, nothing, nothing))
            else:
                after(head, tile, tuple(ref[head, tile] for ref in before))

    def per_tile(tile, carry):
        furthest = pos_ref[0, (tile + 1) * tile_rows - 1]
        for unit in range(units):
            ends = last and unit == units - 1
            fresh = first and unit == 0
            if fresh:
                before = None
            elif unit == 0:
                before = (most_in, sum_in, acc_in)
            else:
                before = (most_out, sum_out, acc_out)
            active = jnp.int32(0)
            for spot in range(unit_blocks):
                begins = list_ref[unit * unit_blocks + spot] * block_len
                active = active + (begins <= furthest).astype(jnp.int32)
            after = finish if ends else write
            for count in range(0, unit_blocks + 1, 2):

                @pl.when((active + 1) // 2 == count // 2)
                def _(count=count):
                    if count:
                        extend(tile, unit, count, before, after)
                    elif fresh or ends:
                        keep(tile, before, after)

        return carry

    lax.fori_loop(0, tiles, per_tile, 0)


def on_device(count, store_kv, block_owner, block_slot, span_len, row_index, fresh_q, fresh_kv):
    stored, block_len, heads, pair_width = store_kv.shape
    dim = pair_width // 2
    blocks = block_slot.shape[1]
    rows = row_index.shape[1]
    group = fresh_q.shape[2] // (heads * dim)
    tiles = rows // tile_rows
    lanes_rows = tile_rows * group
    raw_rows = block_len * 2 * heads

    def flat(array):
        lead = math.prod(array.shape[:-2])
        split = array.reshape(lead, heads, 2, dim)
        return split.transpose(0, 2, 1, 3).reshape(lead * 2 * heads, dim)

    store = flat(store_kv)
    place = lax.axis_index("req").reshape(1)
    row_pos = row_index[0]
    row_cos, row_sin = tables(row_pos.astype(jnp.float32), dim)
    cos, sin = tables(block_len * jnp.arange(blocks, dtype=jnp.float32), dim)
    row_lanes = jnp.broadcast_to(row_pos[:, None], (rows, block_len))
    turned, placed = pl.pallas_call(
        prepare,
        out_shape=(
            pltpu.VMEM((heads, tiles, lanes_rows, dim), jnp.bfloat16),
            pltpu.VMEM((blocks * block_len, heads * 2 * dim + dim), jnp.bfloat16),
        ),
        in_specs=[vmem] * 5,
        out_specs=(vmem, vmem),
        scratch_shapes=[
            pltpu.VMEM((rows * 2 * heads, dim), jnp.float32),
            pltpu.VMEM((rows, heads * 2 * dim + dim), jnp.bfloat16),
        ],
        compiler_params=params,
        name="prepare",
    )(fresh_q[0], flat(fresh_kv), row_cos, row_sin, row_index)

    def attention(number, last, sources, pick, shards, units, state):
        first = not state
        state_shape = pltpu.VMEM((heads, tiles, lanes_rows, dim), jnp.float32)
        inputs = [near(source) for source in sources]
        inputs += [place, block_owner[:, :, 0], block_slot, span_len, row_index]
        inputs += [near(turned), near(placed), cos, sin, row_lanes]
        specs = [vmem] * len(sources) + [smem] * 5 + [vmem] * 5
        spots = units * unit_blocks
        return pl.pallas_call(
            functools.partial(attend, span_len.shape[1], shards, pick, units, first, last),
            out_shape=jax.ShapeDtypeStruct((rows, heads * group * dim), jnp.bfloat16)
            if last
            else (state_shape,) * 3,
            in_specs=specs + [vmem] * len(state),
            out_specs=vmem if last else (vmem,) * 3,
            input_output_aliases={}
            if last or first
            else {len(specs) + entry: entry for entry in range(3)},
            scratch_shapes=[
                pltpu.VMEM((raw_rows, dim), jnp.float32),
                pltpu.VMEM((heads, spots * block_len, dim), jnp.bfloat16),
                pltpu.VMEM((heads, spots * block_len, dim), jnp.bfloat16),
                pltpu.SMEM((blocks + 1,), jnp.int32),
            ]
            + ([pltpu.VMEM((heads, tiles, lanes_rows, dim), jnp.float32)] * 3 if last and units > 1 else []),
            compiler_params=params,
            name=f"attend_{number}",
        )(*inputs, *[near(entry) for entry in state])

    if count != 4:
        everything = lax.all_gather(store, "req", axis=0, tiled=True)
        units = blocks // unit_blocks
        state = ()
        result = attention(0, True, [everything], [lambda at: 0], count, units, state)
        return result[None]
    outer = [(0, 1), (1, 0), (2, 3), (3, 2)]
    inner = [(1, 2), (2, 1)]
    outward = [(1, 0), (2, 3)]
    none = -(1 << 16)
    is_end = lambda at: (at == 0) | (at == 3)

    def send(array, pairs):
        return lax.ppermute(array, "req", pairs)

    beside = send(store, outer)
    across = send(store, inner)
    state = attention(0, False, [store], [lambda at: at], 1, 1, ())
    beside, across, state = lax.optimization_barrier((beside, across, state))
    second = send(across, outward)
    third_in = send(beside, inner)
    state = attention(1, False, [beside], [lambda at: at ^ 1], 1, 1, state)
    second, third_in, state = lax.optimization_barrier((second, third_in, state))
    third = send(third_in, outward)
    state = attention(
        2,
        False,
        [second, across],
        [
            lambda at: jnp.where(is_end(at), jnp.where(at == 0, 2, 1), none),
            lambda at: jnp.where(is_end(at), none, 3 - at),
        ],
        1,
        1,
        state,
    )
    third, state = lax.optimization_barrier((third, state))
    result = attention(
        3,
        True,
        [third, third_in],
        [
            lambda at: jnp.where(is_end(at), 3 - at, none),
            lambda at: jnp.where(is_end(at), none, (3 - at) ^ 1),
        ],
        1,
        1,
        state,
    )
    return result[None]


def solution(mesh):
    placed = (
        P(("grp", "req"), None, "kvh", None),
        P(("grp", "req"), None, None),
        P(("grp", "req"), None),
        P(("grp", "req"), None),
        P(("grp", "req"), None),
        P(("grp", "req"), None, "kvh"),
        P(("grp", "req"), None, "kvh", None),
    )
    return jax.shard_map(
        functools.partial(on_device, mesh.shape["req"]),
        mesh=mesh,
        in_specs=placed,
        out_specs=P(("grp", "req"), None, "kvh"),
        check_vma=False,
    )
```

time: 180 us -> 68.8 us (0.38); the launches traced: 179 us -> 70.1 us
  local copies, waits for them, and re-layouts: 49.4 us -> 6.21 us
  matrix products: 41.8 us -> 0 us
  Pallas kernels: 0 us -> 41.1 us
  other arithmetic: 38.7 us -> 1.62 us
  waiting for transfers between devices: 34.6 us -> 10.9 us
  between operations: 13.7 us -> 0.16 us
  starting transfers between devices: 0.01 us -> 10 us
    dot_general x24 -> x0, matrix products: 41.8 us -> none  [the longest x12 26.7 us: attend_head(): lax.dot_general(query_rows, key_rows, (((1,), (1,)), ((), ())), preferred...]
    pallas_call x0 -> x5, Pallas kernels: none -> 41.1 us  [the longest x4 36.8 us: attention(): pl.pallas_call(functools.partial(attend, span_len.shape[1], shards, pick,...]
    all_gather x1 -> x0, waiting for transfers between devices: 34.6 us -> none  [on_device(): everything = lax.all_gather(store_flat, 'req', axis=0, tiled=True)]
    scatter x2 -> x0, local copies, waits for them, and re-layouts: 24.4 us -> none  [the longest x1 12.3 us: on_device(): key_rows = key_rows.at[row_pos].set(fresh_keys)]
    reduce_sum x12 -> x0, other arithmetic: 11.9 us -> none  [attend_head(): jnp.sum(weights, axis=1, keepdims=True)]
    ppermute x0 -> x5, waiting for transfers between devices: none -> 10.9 us  [send(): return lax.ppermute(array, 'req', pairs)]
    ppermute x0 -> x5, starting transfers between devices: none -> 10 us  [send(): return lax.ppermute(array, 'req', pairs)]
    gather x2 -> x0, local copies, waits for them, and re-layouts: 8.58 us -> none  [on_device(): cached = jnp.take(everything, wanted, axis=0)]
  transfers between devices with their start and end apart: 1 -> 5, of which waited for: 1 -> 2; matrix products, arithmetic and copies ran while one was open for 8% -> 2% of each run, Pallas kernels for 0% -> 43%
where the time goes in v2:
time: 68.8 us; the launch traced here: 70.1 us
  Pallas kernels  41.1 us (60%)
  waiting for transfers between devices  10.9 us (16%)
  starting transfers between devices  10 us (15%)
  local copies, waits for them, and re-layouts  6.21 us (9%)
  other arithmetic  1.62 us (2%)
    pallas_call x4, Pallas kernels, attention(): pl.pallas_call(functools.partial(attend, span_len.shape[1], shards, pick,...  36.8 us
    ppermute x5, waiting for transfers between devices, send(): return lax.ppermute(array, 'req', pairs)  10.9 us
    ppermute x5, starting transfers between devices, send(): return lax.ppermute(array, 'req', pairs)  10 us
    unnamed x18, local copies, waits for them, and re-layouts  6.1 us
    pallas_call x1, Pallas kernels, on_device(): pl.pallas_call(prepare, out_shape=(pltpu.VMEM((heads, tiles, lanes_rows,...  4.34 us
  transfers between devices with their start and end apart: 5, of which 2 were waited for; matrix products, arithmetic and copies ran while one was open for 2% of the time, Pallas kernels for 43%

profile of v2, /device:TPU:0, one launch (start us, length us, event | category | flops | bytes accessed | tf_op | source)
XLA Modules:
  0.0 70.1 jit_solution(15334462851191046866)
XLA Ops:
  0.0 0.7 collective-permute-start.1
  0.7 5.9 %collective-permute-start = (bf16[2048,128]{1,0:T(8,128)(2,1)}, bf16[2048,128]{1,0:T(8,128)(2,1)S(1)}, u32[]{:S(2)}, u32[]{:S(2)}) collective-permute-start(bf16[2048,128]{1,0:T(8,128)(2,1)} %bitcast.16), channel_id=1, source_target_pairs={{0,4},{4,0},{8,12},{12,8},{1,5},{5,1},{9,13},{13,9},{2,6},{6,2},{1... | collective-permute-start | bytes 1572872 | tf_op jit(solution)/shard_map/ppermute | solution.py:336
  6.6 0.7 reduce
  7.3 0.8 %negate_select_fusion = (f32[384,128]{1,0:T(8,128)S(1)}, f32[384,128]{1,0:T(8,128)S(1)}) fusion(s32[128]{0:T(128)S(1)} %get-tuple-element.61, s32[128]{0:T(128)S(1)} %get-tuple-element.62, f32[384]{0:T(512)S(1)} %convert_element_type.27, pred[128]{0:T(512)(128)(4,1)S(1)} %get-tuple-element.60, pred[128]{0:T(512)(128)(4,1)S(1)} %get-tuple-element.59), kind=kLoop, calls=%fused_computation | loop fusion | flops 294912 | bytes 396032 | tf_op jit(solution)/shard_map/jit(_where)/select_n | solution.py:31
  8.1 1.4 %copy-done = bf16[1,384,2048]{2,1,0:T(8,128)(2,1)S(1)} copy-done((bf16[1,384,2048]{2,1,0:T(8,128)(2,1)S(1)}, bf16[1,384,2048]{2,1,0:T(8,128)(2,1)}, u32[]{:S(2)}) %copy-start) | copy-done | bytes 1572888
  9.5 1.0 %copy-done.2 = bf16[1,384,2,256]{3,2,1,0:T(2,128)(2,1)S(1)} copy-done((bf16[1,384,2,256]{3,2,1,0:T(2,128)(2,1)S(1)}, bf16[1,384,2,256]{3,2,1,0:T(2,128)(2,1)}, u32[]{:S(2)}) %copy-start.2) | copy-done | bytes 393240
  10.5 0.7 copy-done.3
  11.2 4.3 %prepare.1 = (bf16[2,6,512,128]{3,2,1,0:T(8,128)(2,1)S(1)}, bf16[3072,640]{1,0:T(8,128)(2,1)S(1)}) custom-call(bf16[384,2048]{1,0:T(8,128)(2,1)S(1)} %bitcast.14, bf16[1536,128]{1,0:T(8,128)(2,1)S(1)} %bitcast.18, f32[384,128]{1,0:T(8,128)S(1)} %get-tuple-element.56.cos_ref, f32[384,128]{1,0:T(8,128)S(1)} %get-tuple-element.55.sin_ref, s32[1,384]{1,0:T(1,128)S(1)} %copy-done.3), custom_call_target="tpu_custom_call" | custom-call | tf_op jit(solution)/shard_map/prepare/pallas_call | solution.py:278
  15.5 0.1 negate_select_fusion.1
  15.7 0.1 broadcast_in_dim.4.refs_10_.refs_11_
  15.8 0.0 copy-start.1
  15.8 1.0 %copy-done.1 = bf16[4,128,2,256]{3,2,1,0:T(2,128)(2,1)S(1)} copy-done((bf16[4,128,2,256]{3,2,1,0:T(2,128)(2,1)S(1)}, bf16[4,128,2,256]{3,2,1,0:T(2,128)(2,1)}, u32[]{:S(2)}) %copy-start.1) | copy-done | bytes 524312
  16.8 0.7 copy-done.4
  17.5 0.7 copy-done.6
  18.2 0.7 copy-done.8
  18.8 10.4 %attend_0.1 = (f32[2,6,512,128]{3,2,1,0:T(8,128)S(1)}, f32[2,6,512,128]{3,2,1,0:T(8,128)S(1)}, f32[2,6,512,128]{3,2,1,0:T(8,128)S(1)}) custom-call(bf16[2048,128]{1,0:T(8,128)(2,1)S(1)} %bitcast.17, s32[1]{0:T(128)} %bitcast.5.refs_1_.refs_2_, s32[1,24]{1,0:T(1,128)S(1)} %bitcast.19, s32[1,24]{1,0:T(1,128)S(1)} %copy-done.6, s32[1,4]{1,0:T(1,128)S(1)} %copy-done.8, ...), custom_call_target="tpu_custom_call" | custom-call | tf_op jit(solution)/shard_map/attend_0/pallas_call | solution.py:302
  29.3 1.3 %collective-permute-start.2 = (bf16[2048,128]{1,0:T(8,128)(2,1)S(1)}, bf16[2048,128]{1,0:T(8,128)(2,1)S(1)}, u32[]{:S(2)}, u32[]{:S(2)}) collective-permute-start(bf16[2048,128]{1,0:T(8,128)(2,1)S(1)} %collective-permute-done.1.refs_1_), channel_id=1, source_target_pairs={{4,0},{8,12},{5,1},{9,13},{6,2},{10,14},{7,3},{11,15},{20,16},{24,... | collective-permute-start | bytes 1572872 | tf_op jit(solution)/shard_map/ppermute | solution.py:336
  30.6 0.7 collective-permute-start.3
  31.3 7.6 %attend_1.1 = (f32[2,6,512,128]{3,2,1,0:T(8,128)S(1)}, f32[2,6,512,128]{3,2,1,0:T(8,128)S(1)}, f32[2,6,512,128]{3,2,1,0:T(8,128)S(1)}) custom-call(bf16[2048,128]{1,0:T(8,128)(2,1)S(1)} %collective-permute-done.refs_0_, s32[1]{0:T(128)} %bitcast.5.refs_1_.refs_2_, ...), custom_call_target="tpu_custom_call", output_to_operand_aliasing={{0}: (11, {}), {1}: (12, {}), {2}: (13, {})} | custom-call | tf_op jit(solution)/shard_map/attend_1/pallas_call | solution.py:302
  38.9 5.3 %collective-permute-done.2.refs_0_ = bf16[2048,128]{1,0:T(8,128)(2,1)S(1)} collective-permute-done((bf16[2048,128]{1,0:T(8,128)(2,1)S(1)}, bf16[2048,128]{1,0:T(8,128)(2,1)S(1)}, u32[]{:S(2)}, u32[]{:S(2)}) %collective-permute-start.2) | collective-permute-done | bytes 524320 | tf_op jit(solution)/shard_map/ppermute | solution.py:336
  44.3 1.5 %collective-permute-start.4 = (bf16[2048,128]{1,0:T(8,128)(2,1)S(1)}, bf16[2048,128]{1,0:T(8,128)(2,1)S(1)}, u32[]{:S(2)}, u32[]{:S(2)}) collective-permute-start(bf16[2048,128]{1,0:T(8,128)(2,1)S(1)} %collective-permute-done.3.refs_1_), channel_id=1, source_target_pairs={{4,0},{8,12},{5,1},{9,13},{6,2},{10,14},{7,3},{11,15},{20,16},{24,... | collective-permute-start | bytes 1572872 | tf_op jit(solution)/shard_map/ppermute | solution.py:336
  45.7 8.1 %attend_2.1 = (f32[2,6,512,128]{3,2,1,0:T(8,128)S(1)}, f32[2,6,512,128]{3,2,1,0:T(8,128)S(1)}, f32[2,6,512,128]{3,2,1,0:T(8,128)S(1)}) custom-call(bf16[2048,128]{1,0:T(8,128)(2,1)S(1)} %collective-permute-done.2.refs_0_, bf16[2048,128]{1,0:T(8,128)(2,1)S(1)} %collective-permute-done.1.refs_1_, ...), custom_call_target="tpu_custom_call", output_to_operand_aliasing={{0}: (12, {}), {1}: (13, {}), {2}: (14, {})} | custom-call | tf_op jit(solution)/shard_map/attend_2/pallas_call | solution.py:302
  53.8 5.6 %collective-permute-done.4.refs_0_ = bf16[2048,128]{1,0:T(8,128)(2,1)S(1)} collective-permute-done((bf16[2048,128]{1,0:T(8,128)(2,1)S(1)}, bf16[2048,128]{1,0:T(8,128)(2,1)S(1)}, u32[]{:S(2)}, u32[]{:S(2)}) %collective-permute-start.4) | collective-permute-done | bytes 524320 | tf_op jit(solution)/shard_map/ppermute | solution.py:336
  59.4 10.7 %attend_3.1 = bf16[384,2048]{1,0:T(8,128)(2,1)} custom-call(bf16[2048,128]{1,0:T(8,128)(2,1)S(1)} %collective-permute-done.4.refs_0_, bf16[2048,128]{1,0:T(8,128)(2,1)S(1)} %collective-permute-done.3.refs_1_, s32[1]{0:T(128)} %bitcast.5.refs_1_.refs_2_, s32[1,24]{1,0:T(1,128)S(1)} %bitcast.22, s32[1,24]{1,0:T(1,128)S(1)} %copy-done.7, s32[1,4]{1,0:T(1,128)S(1)} %copy-done.8, ...), custom_call_target="tpu_custom_call" | custom-call | tf_op jit(solution)/shard_map/attend_3/pallas_call | solution.py:302
  (17 shorter events, 0.1 us)
Async XLA Ops:
  0.0 29.3 %collective-permute-start.1 = (bf16[2048,128]{1,0:T(8,128)(2,1)}, bf16[2048,128]{1,0:T(8,128)(2,1)S(1)}, u32[]{:S(2)}, u32[]{:S(2)}) collective-permute-start(bf16[2048,128]{1,0:T(8,128)(2,1)} %bitcast.15), channel_id=1, source_target_pairs={{4,8},{8,4},{5,9},{9,5},{6,10},{10,6},{7,11},{11,7},{20,24},{24,20... | collective-permute-start | bytes 1572872 | tf_op jit(solution)/shard_map/ppermute | solution.py:336
  0.7 28.6 %collective-permute-start = (bf16[2048,128]{1,0:T(8,128)(2,1)}, bf16[2048,128]{1,0:T(8,128)(2,1)S(1)}, u32[]{:S(2)}, u32[]{:S(2)}) collective-permute-start(bf16[2048,128]{1,0:T(8,128)(2,1)} %bitcast.16), channel_id=1, source_target_pairs={{0,4},{4,0},{8,12},{12,8},{1,5},{5,1},{9,13},{13,9},{2,6},{6,2},{1... | collective-permute-start | bytes 1572872 | tf_op jit(solution)/shard_map/ppermute | solution.py:336
  8.1 1.4 %copy-start = (bf16[1,384,2048]{2,1,0:T(8,128)(2,1)S(1)}, bf16[1,384,2048]{2,1,0:T(8,128)(2,1)}, u32[]{:S(2)}) copy-start(bf16[1,384,2048]{2,1,0:T(8,128)(2,1)} %param.12) | copy-start | bytes 4718596
  9.5 1.0 %copy-start.2 = (bf16[1,384,2,256]{3,2,1,0:T(2,128)(2,1)S(1)}, bf16[1,384,2,256]{3,2,1,0:T(2,128)(2,1)}, u32[]{:S(2)}) copy-start(bf16[1,384,2,256]{3,2,1,0:T(2,128)(2,1)} %param.13) | copy-start | bytes 1179652
  10.5 0.7 copy-start.3
  15.8 15.5 %copy-start.5 = (s32[1,24,1]{1,2,0:T(1,128)S(1)}, s32[1,24,1]{1,2,0:T(1,128)}, u32[]{:S(2)}) copy-start(s32[1,24,1]{1,2,0:T(1,128)} %param.8) | copy-start | bytes 292
  15.8 15.5 %copy-start.7 = (s32[1,24]{1,0:T(1,128)S(1)}, s32[1,24]{1,0:T(1,128)}, u32[]{:S(2)}) copy-start(s32[1,24]{1,0:T(1,128)} %refs_4_.7) | copy-start | bytes 292
  15.8 1.1 %copy-start.1 = (bf16[4,128,2,256]{3,2,1,0:T(2,128)(2,1)S(1)}, bf16[4,128,2,256]{3,2,1,0:T(2,128)(2,1)}, u32[]{:S(2)}) copy-start(bf16[4,128,2,256]{3,2,1,0:T(2,128)(2,1)} %param.7) | copy-start | bytes 1572868
  16.8 0.7 copy-start.4
  17.5 0.7 copy-start.6
  18.2 0.7 copy-start.8
  29.3 15.0 %collective-permute-start.2 = (bf16[2048,128]{1,0:T(8,128)(2,1)S(1)}, bf16[2048,128]{1,0:T(8,128)(2,1)S(1)}, u32[]{:S(2)}, u32[]{:S(2)}) collective-permute-start(bf16[2048,128]{1,0:T(8,128)(2,1)S(1)} %collective-permute-done.1.refs_1_), channel_id=1, source_target_pairs={{4,0},{8,12},{5,1},{9,13},{6,2},{10,14},{7,3},{11,15},{20,16},{24,... | collective-permute-start | bytes 1572872 | tf_op jit(solution)/shard_map/ppermute | solution.py:336
  30.6 13.7 %collective-permute-start.3 = (bf16[2048,128]{1,0:T(8,128)(2,1)S(1)}, bf16[2048,128]{1,0:T(8,128)(2,1)S(1)}, u32[]{:S(2)}, u32[]{:S(2)}) collective-permute-start(bf16[2048,128]{1,0:T(8,128)(2,1)S(1)} %collective-permute-done.refs_0_), channel_id=1, source_target_pairs={{4,8},{8,4},{5,9},{9,5},{6,10},{10,6},{7,11},{11,7},{20,24},{24,20... | collective-permute-start | bytes 1572872 | tf_op jit(solution)/shard_map/ppermute | solution.py:336
  44.3 15.1 %collective-permute-start.4 = (bf16[2048,128]{1,0:T(8,128)(2,1)S(1)}, bf16[2048,128]{1,0:T(8,128)(2,1)S(1)}, u32[]{:S(2)}, u32[]{:S(2)}) collective-permute-start(bf16[2048,128]{1,0:T(8,128)(2,1)S(1)} %collective-permute-done.3.refs_1_), channel_id=1, source_target_pairs={{4,0},{8,12},{5,1},{9,13},{6,2},{10,14},{7,3},{11,15},{20,16},{24,... | collective-permute-start | bytes 1572872 | tf_op jit(solution)/shard_map/ppermute | solution.py:336

commit v3 on v2

v3 whole, which is shorter than its diff:
```python
import functools
import math

import jax
import jax.numpy as jnp
from jax import lax
from jax.experimental import pallas as pl
from jax.experimental.pallas import tpu as pltpu
from jax.sharding import PartitionSpec as P

rope_base = 500000.0
tile_rows = 64
unit_blocks = 6
low = -1e30
bound = 105.0
grain = 2
chunk = 3
vmem = pl.BlockSpec(memory_space=pltpu.VMEM)
smem = pl.BlockSpec(memory_space=pltpu.SMEM)
anywhere = pl.BlockSpec(memory_space=pl.ANY)
params = pltpu.CompilerParams(vmem_limit_bytes=28 << 20)


def near(array):
    return pltpu.with_memory_space_constraint(array, pltpu.VMEM)


def held(array):
    return pltpu.with_memory_space_constraint(array, pltpu.SMEM)


def away(array):
    return pltpu.with_memory_space_constraint(array, pltpu.HBM)


def tables(position, head_dim):
    lane = lax.broadcasted_iota(jnp.int32, (position.shape[0], head_dim), 1)
    half_dim = head_dim // 2
    pair_index = (lane % half_dim).astype(jnp.float32)
    inv_freq = jnp.exp(pair_index * (-2.0 / head_dim) * jnp.log(jnp.float32(rope_base)))
    angles = position[:, None] * inv_freq
    sine = jnp.sin(angles)
    return jnp.cos(angles), jnp.where(lane < half_dim, -sine, sine)


def turn(field, cosine, sine):
    return field * cosine + pltpu.roll(field, field.shape[1] // 2, 1) * sine


def prepare(
    query_ref, fresh_ref, store_ref, owner_ref, slot_ref, span_ref, pos_ref, place_ref, cos_ref, sin_ref,
    turned_ref, placed_ref, near_ref, table_ref, peak_ref,
    raw_ref, flat_ref, wide_ref, all_ref, lanes_ref, row_smem, owner_smem, slot_smem, span_smem, sems,
):
    heads, tiles, lanes_rows, dim = turned_ref.shape
    group = lanes_rows // tile_rows
    placed_rows = placed_ref.shape[0]
    rows = cos_ref.shape[0]
    blocks = slot_ref.shape[1]

    def load_query(tile):
        at = pl.ds(pl.multiple_of(tile * tile_rows, tile_rows), tile_rows)
        return pltpu.make_async_copy(query_ref.at[at, :], raw_ref.at[at, :], sems.at[tile])

    small = [
        pltpu.make_async_copy(source, target, sems.at[tiles + number])
        for number, (source, target) in enumerate(
            (
                (pos_ref, lanes_ref),
                (fresh_ref, flat_ref),
                (pos_ref, row_smem),
                (owner_ref, owner_smem),
                (slot_ref, slot_smem),
                (span_ref, span_smem),
                (store_ref, near_ref),
            )
        )
    ]
    for copy in small[:-1]:
        copy.start()
    for tile in range(tiles):
        load_query(tile).start()
    small[-1].start()
    for copy in small[:-1]:
        copy.wait()
    wide_ref[...] = flat_ref[...].astype(jnp.float32)
    for head in range(heads):
        key = wide_ref[pl.ds(head, rows, stride=2 * heads), :]
        value = wide_ref[pl.ds(heads + head, rows, stride=2 * heads), :]
        all_ref[:, head * 2 * dim : head * 2 * dim + dim] = turn(
            key, cos_ref[...], sin_ref[...]
        ).astype(jnp.bfloat16)
        all_ref[:, head * 2 * dim + dim : (head + 1) * 2 * dim] = value.astype(jnp.bfloat16)
    all_ref[:, heads * 2 * dim :] = jnp.ones((rows, dim), jnp.bfloat16)
    step = 512

    def place(number, carry):
        at = pl.ds(pl.multiple_of(number * step, step), step)
        spot = lax.broadcasted_iota(jnp.int32, (step, rows), 0) + number * step
        chosen = jnp.where(spot == lanes_ref[...], 1.0, 0.0).astype(jnp.bfloat16)
        placed_ref[at, :] = jnp.dot(
            chosen, all_ref[...], preferred_element_type=jnp.float32
        ).astype(jnp.bfloat16)
        return carry

    lax.fori_loop(0, placed_rows // step, place, 0)

    def note(block, carry):
        began = jnp.int32(0)
        start = jnp.int32(0)
        for span in range(span_ref.shape[1]):
            began = jnp.where(start <= block, start, began)
            start = start + span_smem[0, span]
        table_ref[block] = owner_smem[0, block]
        table_ref[blocks + block] = slot_smem[0, block]
        table_ref[2 * blocks + block] = began
        return carry

    lax.fori_loop(0, blocks, note, 0)
    for tile in range(tiles):
        table_ref[3 * blocks + tile] = row_smem[0, (tile + 1) * tile_rows - 1]
    table_ref[3 * blocks + tiles] = place_ref[0]
    ones = jnp.ones((dim, dim), jnp.bfloat16)

    def turn_tile(tile, peak):
        load_query(tile).wait()
        at = pl.ds(pl.multiple_of(tile * tile_rows, tile_rows), tile_rows)
        cosine = cos_ref[at, :]
        sine = sin_ref[at, :]
        for head in range(heads):
            squares = []
            for member in range(group):
                column = (head * group + member) * dim
                field = raw_ref[at, column : column + dim].astype(jnp.float32)
                turned_ref[head, tile, member * tile_rows : (member + 1) * tile_rows, :] = turn(
                    field, cosine, sine
                ).astype(jnp.bfloat16)
                squares.append((field * field).astype(jnp.bfloat16))
            lengths = jnp.dot(
                jnp.concatenate(squares, axis=0), ones, preferred_element_type=jnp.float32
            )
            peak = jnp.maximum(peak, jnp.max(lengths.reshape(-1, 8, dim), axis=0))
        return peak

    peak = lax.fori_loop(0, tiles, turn_tile, jnp.zeros((8, dim), jnp.float32))
    peak_ref[0] = jnp.max(peak)
    small[-1].wait()


def attend(shards, pick, units, first, last, *refs):
    given = len(pick)
    sources = refs[:given]
    table_ref, calm_in, turned_ref, placed_ref, cos_ref, sin_ref, row_ref = refs[given : given + 7]
    refs = refs[given + 7 :]
    if not first:
        most_in, sum_in, acc_in = refs[:3]
        refs = refs[3:]
    most_out, sum_out, acc_out, calm_out = refs[:4]
    refs = refs[4:]
    if last:
        out_ref = refs[0]
        refs = refs[1:]
    wide_ref, key_ref, value_ref, list_ref = refs
    heads, tiles, lanes_rows, dim = turned_ref.shape
    group = lanes_rows // tile_rows
    blocks = cos_ref.shape[0]
    block_len = placed_ref.shape[0] // blocks
    stride = 2 * heads
    raw_rows = block_len * stride
    slots = sources[0].shape[0] // raw_rows // shards
    scale = dim**-0.5 * math.log2(math.e)
    lowest = [choose(table_ref[3 * blocks + tiles]) for choose in pick]
    spots = units * unit_blocks

    def find(block, found):
        owner = table_ref[block]
        hit = jnp.bool_(False)
        for base in lowest:
            hit = hit | ((owner >= base) & (owner < base + shards))
        list_ref[found] = block
        return found + hit.astype(jnp.int32)

    lax.fori_loop(0, blocks, find, jnp.int32(0))
    ones = jnp.ones((dim, dim), jnp.bfloat16)

    def load(turn_number, peak):
        for lane in range(chunk):
            spot = turn_number * chunk + lane
            block = list_ref[spot]
            owner = table_ref[block]
            raw = None
            for source, base in zip(sources, lowest):
                here = (owner >= base) & (owner < base + shards)
                start = ((owner - base) * slots + table_ref[blocks + block]) * raw_rows
                start = pl.multiple_of(jnp.where(here, start, 0), raw_rows)
                found = source[pl.ds(start, raw_rows), :].astype(jnp.float32)
                raw = found if raw is None else jnp.where(here, found, raw)
            wide_ref[lane] = raw
            began = table_ref[2 * blocks + block]
            cosine = cos_ref[pl.ds(began, 1), :]
            sine = sin_ref[pl.ds(began, 1), :]
            fresh = placed_ref[
                pl.ds(pl.multiple_of(block * block_len, block_len), block_len), :
            ].astype(jnp.float32)
            renewed = fresh[:, heads * 2 * dim :] > 0.5
            at = pl.ds(pl.multiple_of(spot * block_len, block_len), block_len)
            for head in range(heads):
                key = turn(wide_ref[lane, pl.ds(head, block_len, stride=stride), :], cosine, sine)
                value = wide_ref[lane, pl.ds(heads + head, block_len, stride=stride), :]
                begin = head * 2 * dim
                key = jnp.where(renewed, fresh[:, begin : begin + dim], key)
                key_ref[head, at, :] = key.astype(jnp.bfloat16)
                value_ref[head, at, :] = jnp.where(
                    renewed, fresh[:, begin + dim : begin + 2 * dim], value
                ).astype(jnp.bfloat16)
                lengths = jnp.dot(
                    (key * key).astype(jnp.bfloat16), ones, preferred_element_type=jnp.float32
                )
                peak = jnp.maximum(peak, jnp.max(lengths.reshape(-1, 8, dim), axis=0))
        return peak

    peak = lax.fori_loop(0, spots // chunk, load, jnp.zeros((8, dim), jnp.float32))
    room = (calm_in[0] < 1e38) & (calm_in[0] * jnp.max(peak) <= (bound / scale) ** 2)
    calm = room.astype(jnp.float32)
    calm_out[0] = jnp.where(room, calm_in[0], jnp.float32(3e38))

    def query_mask(tile):
        row_at = pl.ds(pl.multiple_of(tile * tile_rows, tile_rows), tile_rows)
        row_pos = row_ref[row_at, :]
        lane = lax.broadcasted_iota(jnp.int32, (tile_rows, block_len), 1)
        return lambda spot: (lane + list_ref[spot] * block_len <= row_pos)[None]

    def scored(head, tile, first_spot, count, seen):
        at = pl.ds(pl.multiple_of(first_spot * block_len, block_len), count * block_len)
        scores = lax.dot_general(
            turned_ref[head, tile],
            key_ref[head, at, :],
            (((1,), (1,)), ((), ())),
            preferred_element_type=jnp.float32,
        )
        return at, [
            jnp.where(
                seen[spot],
                scores[:, spot * block_len : (spot + 1) * block_len].reshape(
                    group, tile_rows, block_len
                ),
                2 * low,
            ).reshape(lanes_rows, block_len)
            for spot in range(count)
        ]

    def weighed(head, at, parts):
        return functools.reduce(jnp.add, parts), jnp.dot(
            jnp.concatenate([part.astype(jnp.bfloat16) for part in parts], axis=1),
            value_ref[head, at, :],
            preferred_element_type=jnp.float32,
        )

    def write(head, tile, total, acc):
        sum_out[head, tile] = total
        acc_out[head, tile] = acc

    def finish(head, tile, total, acc):
        result = (acc / jnp.sum(total, axis=1, keepdims=True)).astype(jnp.bfloat16)
        row_at = pl.ds(pl.multiple_of(tile * tile_rows, tile_rows), tile_rows)
        for member in range(group):
            column = (head * group + member) * dim
            out_ref[row_at, column : column + dim] = result[
                member * tile_rows : (member + 1) * tile_rows
            ]

    def quick(tile, carry):
        furthest = table_ref[3 * blocks + tile]
        visible = query_mask(tile)
        for unit in range(units):
            fresh = first and unit == 0
            ends = last and unit == units - 1
            before = (sum_in, acc_in) if unit == 0 and not first else (sum_out, acc_out)
            first_spot = unit * unit_blocks
            active = jnp.int32(0)
            for spot in range(unit_blocks):
                begins = list_ref[first_spot + spot] * block_len
                active = active + (begins <= furthest).astype(jnp.int32)
            after = finish if ends else write
            for count in range(0, unit_blocks + 1, grain):

                @pl.when((active + grain - 1) // grain == count // grain)
                def _(count=count):
                    if not count and not fresh and not ends:
                        return
                    seen = [visible(first_spot + spot) for spot in range(count)]
                    for head in range(heads):
                        total = acc = jnp.zeros((lanes_rows, dim), jnp.float32)
                        if count:
                            at, parts = scored(head, tile, first_spot, count, seen)
                            parts = [jnp.exp2(part * scale) for part in parts]
                            total, acc = weighed(head, at, parts)
                        if not fresh:
                            total = before[0][head, tile] + total
                            acc = before[1][head, tile] + acc
                        after(head, tile, total, acc)

        return carry

    def careful(tile, carry):
        furthest = table_ref[3 * blocks + tile]
        visible = query_mask(tile)

        def begin(head, ignored):
            if first:
                nothing = jnp.zeros((lanes_rows, dim), jnp.float32)
                most_out[head, tile] = nothing + low
                write(head, tile, nothing, nothing)
            else:
                total = sum_in[head, tile]
                most_out[head, tile] = jnp.where(
                    calm_in[0] < 1e38,
                    jnp.where(jnp.max(total, axis=1, keepdims=True) > 0, 0.0, low),
                    most_in[head, tile],
                )
                write(head, tile, total, acc_in[head, tile])
            return ignored

        lax.fori_loop(0, heads, begin, 0)

        def one(step, ignored):
            head = step % heads
            spot = step // heads

            @pl.when(list_ref[spot] * block_len <= furthest)
            def _():
                at, parts = scored(head, tile, spot, 1, [visible(spot)])
                was = most_out[head, tile]
                most = jnp.maximum(was, jnp.max(parts[0], axis=1, keepdims=True))
                total, acc = weighed(head, at, [jnp.exp2((parts[0] - most) * scale)])
                shrink = jnp.exp2((was - most) * scale)
                most_out[head, tile] = most
                write(
                    head,
                    tile,
                    sum_out[head, tile] * shrink + total,
                    acc_out[head, tile] * shrink + acc,
                )

            return ignored

        lax.fori_loop(0, spots * heads, one, 0)
        if last:
            for head in range(heads):
                finish(head, tile, sum_out[head, tile], acc_out[head, tile])
        return carry

    @pl.when(calm > 0.5)
    def _():
        lax.fori_loop(0, tiles, quick, 0)

    @pl.when(calm < 0.5)
    def _():
        lax.fori_loop(0, tiles, careful, 0)


def on_device(count, store_kv, block_owner, block_slot, span_len, row_index, fresh_q, fresh_kv):
    stored, block_len, heads, pair_width = store_kv.shape
    dim = pair_width // 2
    blocks = block_slot.shape[1]
    rows = row_index.shape[1]
    group = fresh_q.shape[2] // (heads * dim)
    tiles = rows // tile_rows
    lanes_rows = tile_rows * group
    raw_rows = block_len * 2 * heads

    def flat(array):
        lead = math.prod(array.shape[:-2])
        split = array.reshape(lead, heads, 2, dim)
        return split.transpose(0, 2, 1, 3).reshape(lead * 2 * heads, dim)

    store = flat(store_kv)
    place = lax.axis_index("req").reshape(1)
    row_pos = row_index[0]
    row_cos, row_sin = tables(row_pos.astype(jnp.float32), dim)
    cos, sin = tables(block_len * jnp.arange(blocks, dtype=jnp.float32), dim)
    row_lanes = jnp.broadcast_to(row_pos[:, None], (rows, block_len))
    wide = heads * 2 * dim + dim
    turned, placed, close, table, peak = pl.pallas_call(
        prepare,
        out_shape=(
            pltpu.VMEM((heads, tiles, lanes_rows, dim), jnp.bfloat16),
            pltpu.VMEM((blocks * block_len, wide), jnp.bfloat16),
            pltpu.VMEM(store.shape, jnp.bfloat16),
            pltpu.SMEM((3 * blocks + tiles + 1,), jnp.int32),
            pltpu.SMEM((1,), jnp.float32),
        ),
        in_specs=[anywhere] * 7 + [smem, vmem, vmem],
        out_specs=(vmem, vmem, vmem, smem, smem),
        scratch_shapes=[
            pltpu.VMEM((rows, heads * group * dim), jnp.bfloat16),
            pltpu.VMEM((rows * 2 * heads, dim), jnp.bfloat16),
            pltpu.VMEM((rows * 2 * heads, dim), jnp.float32),
            pltpu.VMEM((rows, wide), jnp.bfloat16),
            pltpu.VMEM((1, rows), jnp.int32),
            pltpu.SMEM((1, rows), jnp.int32),
            pltpu.SMEM((1, blocks), jnp.int32),
            pltpu.SMEM((1, blocks), jnp.int32),
            pltpu.SMEM(span_len.shape, jnp.int32),
            pltpu.SemaphoreType.DMA((tiles + 7,)),
        ],
        compiler_params=params,
        name="prepare",
    )(
        away(fresh_q[0]), away(flat(fresh_kv)), away(store), away(block_owner[:, :, 0]),
        away(block_slot), away(span_len), away(row_index), place, near(row_cos), near(row_sin),
    )

    def attention(number, last, sources, pick, shards, units, state):
        first = len(state) == 1
        state_shape = pltpu.VMEM((heads, tiles, lanes_rows, dim), jnp.float32)
        inputs = [near(source) for source in sources]
        inputs += [held(table), held(state[-1])]
        inputs += [near(array) for array in (turned, placed, cos, sin, row_lanes)]
        specs = [vmem] * len(sources) + [smem] * 2 + [vmem] * 5
        spots = units * unit_blocks
        result = [jax.ShapeDtypeStruct((rows, heads * group * dim), jnp.bfloat16)] if last else []
        return pl.pallas_call(
            functools.partial(attend, shards, pick, units, first, last),
            out_shape=[state_shape] * 3 + [pltpu.SMEM((1,), jnp.float32)] + result,
            in_specs=specs + [vmem] * (len(state) - 1),
            out_specs=[vmem] * 3 + [smem] + [vmem] * len(result),
            input_output_aliases={}
            if first
            else {len(specs) + entry: entry for entry in range(3)},
            scratch_shapes=[
                pltpu.VMEM((chunk, raw_rows, dim), jnp.float32),
                pltpu.VMEM((heads, spots * block_len, dim), jnp.bfloat16),
                pltpu.VMEM((heads, spots * block_len, dim), jnp.bfloat16),
                pltpu.SMEM((blocks + 1,), jnp.int32),
            ],
            compiler_params=params,
            name=f"attend_{number}",
        )(*inputs, *[near(entry) for entry in state[:-1]])

    if count != 4:
        everything = lax.all_gather(store, "req", axis=0, tiled=True)
        return attention(
            0, True, [everything], [lambda at: 0], count, blocks // unit_blocks, (peak,)
        )[-1][None]
    outer = [(0, 1), (1, 0), (2, 3), (3, 2)]
    inner = [(1, 2), (2, 1)]
    outward = [(1, 0), (2, 3)]
    none = -(1 << 16)
    is_end = lambda at: (at == 0) | (at == 3)

    def send(array, pairs):
        return lax.ppermute(array, "req", pairs)

    beside = send(store, outer)
    across = send(store, inner)
    beside, across, close, turned = lax.optimization_barrier((beside, across, close, turned))
    second = send(across, outward)
    third_in = send(beside, inner)
    state = attention(0, False, [close, beside], [lambda at: at, lambda at: at ^ 1], 1, 2, (peak,))
    second, third_in, state = lax.optimization_barrier((second, third_in, state))
    third = send(third_in, outward)
    state = attention(
        1,
        False,
        [second, across],
        [
            lambda at: jnp.where(is_end(at), jnp.where(at == 0, 2, 1), none),
            lambda at: jnp.where(is_end(at), none, 3 - at),
        ],
        1,
        1,
        state,
    )
    third, state = lax.optimization_barrier((third, state))
    return attention(
        2,
        True,
        [third, third_in],
        [
            lambda at: jnp.where(is_end(at), 3 - at, none),
            lambda at: jnp.where(is_end(at), none, (3 - at) ^ 1),
        ],
        1,
        1,
        state,
    )[-1][None]


def solution(mesh):
    placed = (
        P(("grp", "req"), None, "kvh", None),
        P(("grp", "req"), None, None),
        P(("grp", "req"), None),
        P(("grp", "req"), None),
        P(("grp", "req"), None),
        P(("grp", "req"), None, "kvh"),
        P(("grp", "req"), None, "kvh", None),
    )
    return jax.shard_map(
        functools.partial(on_device, mesh.shape["req"]),
        mesh=mesh,
        in_specs=placed,
        out_specs=P(("grp", "req"), None, "kvh"),
        check_vma=False,
    )
```

time: 68.8 us -> 119 us (1.73)
  the two profiles are of different devices: /device:TPU:0 before, /device:TPU:8 now
where the time goes in v3:
time: 119 us; the launch traced here: 122 us
  Pallas kernels  99.4 us (84%)
  starting transfers between devices  14.6 us (12%)
  waiting for transfers between devices  5.7 us (5%)
  other arithmetic  1.62 us (1%)
    pallas_call x3, Pallas kernels, attention(): pl.pallas_call(functools.partial(attend, shards, pick, units, first, last...  93 us
    ppermute x5, starting transfers between devices, send(): return lax.ppermute(array, 'req', pairs)  14.6 us
    pallas_call x1, Pallas kernels, on_device(): pl.pallas_call(prepare, out_shape=(pltpu.VMEM((heads, tiles, lanes_rows,...  6.37 us
    ppermute x5, waiting for transfers between devices, send(): return lax.ppermute(array, 'req', pairs)  5.7 us
  transfers between devices with their start and end apart: 5, of which 2 were waited for; matrix products, arithmetic and copies ran while one was open for 1% of the time, Pallas kernels for 60%

profile of v3, /device:TPU:8, one launch (start us, length us, event | category | flops | bytes accessed | tf_op | source)
XLA Modules:
  0.0 121.5 jit_solution(6757677623941482350)
XLA Ops:
  0.0 3.5 %collective-permute-start.1 = (bf16[2048,128]{1,0:T(8,128)(2,1)}, bf16[2048,128]{1,0:T(8,128)(2,1)S(1)}, u32[]{:S(2)}, u32[]{:S(2)}) collective-permute-start(bf16[2048,128]{1,0:T(8,128)(2,1)} %bitcast.15), channel_id=1, source_target_pairs={{4,8},{8,4},{5,9},{9,5},{6,10},{10,6},{7,11},{11,7},{20,24},{24,20... | collective-permute-start | bytes 1572872 | tf_op jit(solution)/shard_map/ppermute | solution.py:453
  3.5 0.1 collective-permute-start
  3.6 0.7 reduce
  4.3 0.8 negate_select_fusion
  5.1 6.4 %prepare.1 = (bf16[2,6,512,128]{3,2,1,0:T(8,128)(2,1)S(1)}, bf16[3072,640]{1,0:T(8,128)(2,1)S(1)}, bf16[2048,128]{1,0:T(8,128)(2,1)S(1)}, s32[79]{0:T(128)S(4)}, f32[1]{0:T(128)S(4)}) custom-call(bf16[384,2048]{1,0:T(8,128)(2,1)} %bitcast.14, bf16[1536,128]{1,0:T(8,128)(2,1)} %bitcast.18, bf16[2048,128]{1,0:T(8,128)(2,1)} %bitcast.17, s32[1,24]{1,0:T(1,128)} %bitcast.19, ...), custom_call_target="tpu_custom_call" | custom-call | tf_op jit(solution)/shard_map/prepare/pallas_call | solution.py:384
  11.5 4.3 %collective-permute-done.1.refs_1_ = bf16[2048,128]{1,0:T(8,128)(2,1)S(1)} collective-permute-done((bf16[2048,128]{1,0:T(8,128)(2,1)}, bf16[2048,128]{1,0:T(8,128)(2,1)S(1)}, u32[]{:S(2)}, u32[]{:S(2)}) %collective-permute-start.1) | collective-permute-done | bytes 524320 | tf_op jit(solution)/shard_map/ppermute | solution.py:453
  15.8 1.4 %collective-permute-done.refs_1_ = bf16[2048,128]{1,0:T(8,128)(2,1)S(1)} collective-permute-done((bf16[2048,128]{1,0:T(8,128)(2,1)}, bf16[2048,128]{1,0:T(8,128)(2,1)S(1)}, u32[]{:S(2)}, u32[]{:S(2)}) %collective-permute-start) | collective-permute-done | bytes 524320 | tf_op jit(solution)/shard_map/ppermute | solution.py:453
  17.1 2.2 %collective-permute-start.2 = (bf16[2048,128]{1,0:T(8,128)(2,1)S(1)}, bf16[2048,128]{1,0:T(8,128)(2,1)S(1)}, u32[]{:S(2)}, u32[]{:S(2)}) collective-permute-start(bf16[2048,128]{1,0:T(8,128)(2,1)S(1)} %collective-permute-done.1.refs_1_), channel_id=1, source_target_pairs={{4,0},{8,12},{5,1},{9,13},{6,2},{10,14},{7,3},{11,15},{20,16},{24,... | collective-permute-start | bytes 1572872 | tf_op jit(solution)/shard_map/ppermute | solution.py:453
  19.4 2.4 %collective-permute-start.3 = (bf16[2048,128]{1,0:T(8,128)(2,1)S(1)}, bf16[2048,128]{1,0:T(8,128)(2,1)S(1)}, u32[]{:S(2)}, u32[]{:S(2)}) collective-permute-start(bf16[2048,128]{1,0:T(8,128)(2,1)S(1)} %collective-permute-done.refs_1_), channel_id=1, source_target_pairs={{4,8},{8,4},{5,9},{9,5},{6,10},{10,6},{7,11},{11,7},{20,24},{24,20... | collective-permute-start | bytes 1572872 | tf_op jit(solution)/shard_map/ppermute | solution.py:453
  21.7 0.1 negate_select_fusion.1
  21.9 0.1 broadcast_in_dim.4.refs_8_
  22.0 38.2 %attend_0.1 = (f32[2,6,512,128]{3,2,1,0:T(8,128)S(1)}, f32[2,6,512,128]{3,2,1,0:T(8,128)S(1)}, f32[2,6,512,128]{3,2,1,0:T(8,128)S(1)}, f32[1]{0:T(128)S(4)}) custom-call(bf16[2048,128]{1,0:T(8,128)(2,1)S(1)} %get-tuple-element.38.refs_0_, bf16[2048,128]{1,0:T(8,128)(2,1)S(1)} %collective-permute-done.refs_1_, s32[79]{0:T(128)S(4)} %get-tuple-element.39.refs_2_, ...), custom_call_target="tpu_custom_call" | custom-call | tf_op jit(solution)/shard_map/attend_0/pallas_call | solution.py:423
  60.2 0.0 collective-permute-done.2.refs_0_
  60.2 0.0 collective-permute-done.3.refs_1_
  60.2 6.5 %collective-permute-start.4 = (bf16[2048,128]{1,0:T(8,128)(2,1)S(1)}, bf16[2048,128]{1,0:T(8,128)(2,1)S(1)}, u32[]{:S(2)}, u32[]{:S(2)}) collective-permute-start(bf16[2048,128]{1,0:T(8,128)(2,1)S(1)} %collective-permute-done.3.refs_1_), channel_id=1, source_target_pairs={{4,0},{8,12},{5,1},{9,13},{6,2},{10,14},{7,3},{11,15},{20,16},{24,... | collective-permute-start | bytes 1572872 | tf_op jit(solution)/shard_map/ppermute | solution.py:453
  66.7 28.7 %attend_1.1 = (f32[2,6,512,128]{3,2,1,0:T(8,128)S(1)}, f32[2,6,512,128]{3,2,1,0:T(8,128)S(1)}, f32[2,6,512,128]{3,2,1,0:T(8,128)S(1)}, f32[1]{0:T(128)S(4)}) custom-call(bf16[2048,128]{1,0:T(8,128)(2,1)S(1)} %collective-permute-done.2.refs_0_, ...), custom_call_target="tpu_custom_call", output_to_operand_aliasing={{0}: (9, {}), {1}: (10, {}), {2}: (11, {})} | custom-call | tf_op jit(solution)/shard_map/attend_1/pallas_call | solution.py:423
  95.4 0.0 collective-permute-done.4.refs_0_
  95.4 26.1 %attend_2.1 = (f32[2,6,512,128]{3,2,1,0:T(8,128)S(1)}, f32[2,6,512,128]{3,2,1,0:T(8,128)S(1)}, f32[2,6,512,128]{3,2,1,0:T(8,128)S(1)}, f32[1]{0:T(128)S(4)}, bf16[384,2048]{1,0:T(8,128)(2,1)}) custom-call(bf16[2048,128]{1,0:T(8,128)(2,1)S(1)} %collective-permute-done.4.refs_0_, ...), custom_call_target="tpu_custom_call", output_to_operand_aliasing={{0}: (9, {}), {1}: (10, {}), {2}: (11, {})} | custom-call | tf_op jit(solution)/shard_map/attend_2/pallas_call | solution.py:423
  (4 shorter events, 0.0 us)
Async XLA Ops:
  0.0 15.8 %collective-permute-start.1 = (bf16[2048,128]{1,0:T(8,128)(2,1)}, bf16[2048,128]{1,0:T(8,128)(2,1)S(1)}, u32[]{:S(2)}, u32[]{:S(2)}) collective-permute-start(bf16[2048,128]{1,0:T(8,128)(2,1)} %bitcast.15), channel_id=1, source_target_pairs={{4,8},{8,4},{5,9},{9,5},{6,10},{10,6},{7,11},{11,7},{20,24},{24,20... | collective-permute-start | bytes 1572872 | tf_op jit(solution)/shard_map/ppermute | solution.py:453
  3.5 13.7 %collective-permute-start = (bf16[2048,128]{1,0:T(8,128)(2,1)}, bf16[2048,128]{1,0:T(8,128)(2,1)S(1)}, u32[]{:S(2)}, u32[]{:S(2)}) collective-permute-start(bf16[2048,128]{1,0:T(8,128)(2,1)} %bitcast.16), channel_id=1, source_target_pairs={{0,4},{4,0},{8,12},{12,8},{1,5},{5,1},{9,13},{13,9},{2,6},{6,2},{1... | collective-permute-start | bytes 1572872 | tf_op jit(solution)/shard_map/ppermute | solution.py:453
  17.1 43.0 %collective-permute-start.2 = (bf16[2048,128]{1,0:T(8,128)(2,1)S(1)}, bf16[2048,128]{1,0:T(8,128)(2,1)S(1)}, u32[]{:S(2)}, u32[]{:S(2)}) collective-permute-start(bf16[2048,128]{1,0:T(8,128)(2,1)S(1)} %collective-permute-done.1.refs_1_), channel_id=1, source_target_pairs={{4,0},{8,12},{5,1},{9,13},{6,2},{10,14},{7,3},{11,15},{20,16},{24,... | collective-permute-start | bytes 1572872 | tf_op jit(solution)/shard_map/ppermute | solution.py:453
  19.4 40.8 %collective-permute-start.3 = (bf16[2048,128]{1,0:T(8,128)(2,1)S(1)}, bf16[2048,128]{1,0:T(8,128)(2,1)S(1)}, u32[]{:S(2)}, u32[]{:S(2)}) collective-permute-start(bf16[2048,128]{1,0:T(8,128)(2,1)S(1)} %collective-permute-done.refs_1_), channel_id=1, source_target_pairs={{4,8},{8,4},{5,9},{9,5},{6,10},{10,6},{7,11},{11,7},{20,24},{24,20... | collective-permute-start | bytes 1572872 | tf_op jit(solution)/shard_map/ppermute | solution.py:453
  60.2 35.2 %collective-permute-start.4 = (bf16[2048,128]{1,0:T(8,128)(2,1)S(1)}, bf16[2048,128]{1,0:T(8,128)(2,1)S(1)}, u32[]{:S(2)}, u32[]{:S(2)}) collective-permute-start(bf16[2048,128]{1,0:T(8,128)(2,1)S(1)} %collective-permute-done.3.refs_1_), channel_id=1, source_target_pairs={{4,0},{8,12},{5,1},{9,13},{6,2},{10,14},{7,3},{11,15},{20,16},{24,... | collective-permute-start | bytes 1572872 | tf_op jit(solution)/shard_map/ppermute | solution.py:453

commit v4 on v3

--- a/solution.py
+++ b/solution.py
@@ -12,6 +12,8 @@
 tile_rows = 64
 unit_blocks = 6
 low = -1e30
+far = 1 << 20
+cut = 2
 bound = 105.0
 grain = 2
 chunk = 3
@@ -147,7 +149,7 @@
     small[-1].wait()
 
 
-def attend(shards, pick, units, first, last, *refs):
+def attend(shards, pick, parts_of, units, first, last, *refs):
     given = len(pick)
     sources = refs[:given]
     table_ref, calm_in, turned_ref, placed_ref, cos_ref, sin_ref, row_ref = refs[given : given + 7]
@@ -167,32 +169,49 @@
     block_len = placed_ref.shape[0] // blocks
     stride = 2 * heads
     raw_rows = block_len * stride
-    slots = sources[0].shape[0] // raw_rows // shards
+    slots = sources[0].shape[0] // raw_rows // shards if parts_of is None else None
     scale = dim**-0.5 * math.log2(math.e)
     lowest = [choose(table_ref[3 * blocks + tiles]) for choose in pick]
     spots = units * unit_blocks
+
+    whole = parts_of is None
+    low_slot, high_slot = (0, slots) if whole else parts_of
 
     def find(block, found):
         owner = table_ref[block]
         hit = jnp.bool_(False)
         for base in lowest:
             hit = hit | ((owner >= base) & (owner < base + shards))
+        if not whole:
+            slot = table_ref[blocks + block]
+            hit = hit & (slot >= low_slot) & (slot < high_slot)
         list_ref[found] = block
         return found + hit.astype(jnp.int32)
 
-    lax.fori_loop(0, blocks, find, jnp.int32(0))
+    found = lax.fori_loop(0, blocks, find, jnp.int32(0))
+    if not whole:
+
+        def clear(spot, carry):
+            list_ref[spot] = far
+            return carry
+
+        lax.fori_loop(found, spots, clear, 0)
     ones = jnp.ones((dim, dim), jnp.bfloat16)
 
     def load(turn_number, peak):
         for lane in range(chunk):
             spot = turn_number * chunk + lane
-            block = list_ref[spot]
+            block = list_ref[spot] if whole else jnp.minimum(list_ref[spot], blocks - 1)
             owner = table_ref[block]
             raw = None
             for source, base in zip(sources, lowest):
                 here = (owner >= base) & (owner < base + shards)
-                start = ((owner - base) * slots + table_ref[blocks + block]) * raw_rows
-                start = pl.multiple_of(jnp.where(here, start, 0), raw_rows)
+                slot = table_ref[blocks + block]
+                if whole:
+                    start = jnp.where(here, (owner - base) * slots + slot, 0)
+                else:
+                    start = jnp.clip(slot - low_slot, 0, high_slot - low_slot - 1)
+                start = pl.multiple_of(start * raw_rows, raw_rows)
                 found = source[pl.ds(start, raw_rows), :].astype(jnp.float32)
                 raw = found if raw is None else jnp.where(here, found, raw)
             wide_ref[lane] = raw
@@ -219,7 +238,8 @@
                 peak = jnp.maximum(peak, jnp.max(lengths.reshape(-1, 8, dim), axis=0))
         return peak
 
-    peak = lax.fori_loop(0, spots // chunk, load, jnp.zeros((8, dim), jnp.float32))
+    turns = spots // chunk if whole else (found + chunk - 1) // chunk
+    peak = lax.fori_loop(0, turns, load, jnp.zeros((8, dim), jnp.float32))
     room = (calm_in[0] < 1e38) & (calm_in[0] * jnp.max(peak) <= (bound / scale) ** 2)
     calm = room.astype(jnp.float32)
     calm_out[0] = jnp.where(room, calm_in[0], jnp.float32(3e38))
@@ -378,6 +398,18 @@
     place = lax.axis_index("req").reshape(1)
     row_pos = row_index[0]
     row_cos, row_sin = tables(row_pos.astype(jnp.float32), dim)
+    outer = [(0, 1), (1, 0), (2, 3), (3, 2)]
+    inner = [(1, 2), (2, 1)]
+    outward = [(1, 0), (2, 3)]
+    none = -(1 << 16)
+    is_end = lambda at: (at == 0) | (at == 3)
+
+    def send(array, pairs):
+        return lax.ppermute(array, "req", pairs)
+
+    if count == 4:
+        beside = send(store, outer)
+        across = send(store, inner)
     cos, sin = tables(block_len * jnp.arange(blocks, dtype=jnp.float32), dim)
     row_lanes = jnp.broadcast_to(row_pos[:, None], (rows, block_len))
     wide = heads * 2 * dim + dim
@@ -411,7 +443,7 @@
         away(block_slot), away(span_len), away(row_index), place, near(row_cos), near(row_sin),
     )
 
-    def attention(number, last, sources, pick, shards, units, state):
+    def attention(number, last, sources, pick, shards, units, state, parts_of=None):
         first = len(state) == 1
         state_shape = pltpu.VMEM((heads, tiles, lanes_rows, dim), jnp.float32)
         inputs = [near(source) for source in sources]
@@ -421,7 +453,7 @@
         spots = units * unit_blocks
         result = [jax.ShapeDtypeStruct((rows, heads * group * dim), jnp.bfloat16)] if last else []
         return pl.pallas_call(
-            functools.partial(attend, shards, pick, units, first, last),
+            functools.partial(attend, shards, pick, parts_of, units, first, last),
             out_shape=[state_shape] * 3 + [pltpu.SMEM((1,), jnp.float32)] + result,
             in_specs=specs + [vmem] * (len(state) - 1),
             out_specs=[vmem] * 3 + [smem] + [vmem] * len(result),
@@ -443,23 +475,17 @@
         return attention(
             0, True, [everything], [lambda at: 0], count, blocks // unit_blocks, (peak,)
         )[-1][None]
-    outer = [(0, 1), (1, 0), (2, 3), (3, 2)]
-    inner = [(1, 2), (2, 1)]
-    outward = [(1, 0), (2, 3)]
-    none = -(1 << 16)
-    is_end = lambda at: (at == 0) | (at == 3)
-
-    def send(array, pairs):
-        return lax.ppermute(array, "req", pairs)
-
-    beside = send(store, outer)
-    across = send(store, inner)
     beside, across, close, turned = lax.optimization_barrier((beside, across, close, turned))
     second = send(across, outward)
-    third_in = send(beside, inner)
+    halves = ((0, cut), (cut, stored))
+    third_in = [send(beside[begin * raw_rows : end * raw_rows], inner) for begin, end in halves]
     state = attention(0, False, [close, beside], [lambda at: at, lambda at: at ^ 1], 1, 2, (peak,))
-    second, third_in, state = lax.optimization_barrier((second, third_in, state))
-    third = send(third_in, outward)
+    third = []
+    for number in range(2):
+        third_in[number], second, state = lax.optimization_barrier(
+            (third_in[number], second, state)
+        )
+        third.append(send(third_in[number], outward))
     state = attention(
         1,
         False,
@@ -472,19 +498,22 @@
         1,
         state,
     )
-    third, state = lax.optimization_barrier((third, state))
-    return attention(
-        2,
-        True,
-        [third, third_in],
-        [
-            lambda at: jnp.where(is_end(at), 3 - at, none),
-            lambda at: jnp.where(is_end(at), none, (3 - at) ^ 1),
-        ],
-        1,
-        1,
-        state,
-    )[-1][None]
+    for number in range(2):
+        third[number], state = lax.optimization_barrier((third[number], state))
+        state = attention(
+            2 + number,
+            number == 1,
+            [third[number], third_in[number]],
+            [
+                lambda at: jnp.where(is_end(at), 3 - at, none),
+                lambda at: jnp.where(is_end(at), none, (3 - at) ^ 1),
+            ],
+            1,
+            1,
+            state,
+            halves[number],
+        )
+    return state[-1][None]
 
 
 def solution(mesh):

time: 119 us -> 126 us (1.059); the launches traced: 122 us -> 124 us
  Pallas kernels: 99.4 us -> 102 us
    pallas_call x3 -> x4, Pallas kernels: 93 us -> 95.5 us  [attention(): pl.pallas_call(functools.partial(attend, shards, pick, parts_of, units, f...]
    ppermute x5 -> x7, starting transfers between devices: 14.6 us -> 14.2 us  [send(): return lax.ppermute(array, 'req', pairs)]
    ppermute x5 -> x7, waiting for transfers between devices: 5.7 us -> 5.7 us  [send(): return lax.ppermute(array, 'req', pairs)]
  transfers between devices with their start and end apart: 5 -> 7, of which waited for: 2 -> 2; matrix products, arithmetic and copies ran while one was open for 1% -> 1% of each run, Pallas kernels for 60% -> 72%
where the time goes in v4:
time: 126 us; the launch traced here: 124 us
  Pallas kernels  102 us (81%)
  starting transfers between devices  14.2 us (11%)
  waiting for transfers between devices  5.7 us (5%)
  other arithmetic  1.62 us (1%)
    pallas_call x4, Pallas kernels, attention(): pl.pallas_call(functools.partial(attend, shards, pick, parts_of, units, f...  95.5 us
    ppermute x7, starting transfers between devices, send(): return lax.ppermute(array, 'req', pairs)  14.2 us
    pallas_call x1, Pallas kernels, on_device(): pl.pallas_call(prepare, out_shape=(pltpu.VMEM((heads, tiles, lanes_rows,...  6.37 us
    ppermute x7, waiting for transfers between devices, send(): return lax.ppermute(array, 'req', pairs)  5.7 us
  transfers between devices with their start and end apart: 7, of which 2 were waited for; matrix products, arithmetic and copies ran while one was open for 1% of the time, Pallas kernels for 72%

profile of v4, /device:TPU:8, one launch (start us, length us, event | category | flops | bytes accessed | tf_op | source)
XLA Modules:
  0.0 123.7 jit_solution(10687157723760310975)
XLA Ops:
  0.0 3.5 %collective-permute-start.1 = (bf16[2048,128]{1,0:T(8,128)(2,1)}, bf16[2048,128]{1,0:T(8,128)(2,1)S(1)}, u32[]{:S(2)}, u32[]{:S(2)}) collective-permute-start(bf16[2048,128]{1,0:T(8,128)(2,1)} %bitcast.15), channel_id=1, source_target_pairs={{4,8},{8,4},{5,9},{9,5},{6,10},{10,6},{7,11},{11,7},{20,24},{24,20... | collective-permute-start | bytes 1572872 | tf_op jit(solution)/shard_map/ppermute | solution.py:408
  3.5 0.1 collective-permute-start
  3.6 0.7 reduce
  4.3 0.8 negate_select_fusion
  5.1 6.4 %prepare.1 = (bf16[2,6,512,128]{3,2,1,0:T(8,128)(2,1)S(1)}, bf16[3072,640]{1,0:T(8,128)(2,1)S(1)}, bf16[2048,128]{1,0:T(8,128)(2,1)S(1)}, s32[79]{0:T(128)S(4)}, f32[1]{0:T(128)S(4)}) custom-call(bf16[384,2048]{1,0:T(8,128)(2,1)} %bitcast.14, bf16[1536,128]{1,0:T(8,128)(2,1)} %bitcast.18, bf16[2048,128]{1,0:T(8,128)(2,1)} %bitcast.17, s32[1,24]{1,0:T(1,128)} %bitcast.19, ...), custom_call_target="tpu_custom_call" | custom-call | tf_op jit(solution)/shard_map/prepare/pallas_call | solution.py:416
  11.5 4.3 %collective-permute-done.1.refs_1_ = bf16[2048,128]{1,0:T(8,128)(2,1)S(1)} collective-permute-done((bf16[2048,128]{1,0:T(8,128)(2,1)}, bf16[2048,128]{1,0:T(8,128)(2,1)S(1)}, u32[]{:S(2)}, u32[]{:S(2)}) %collective-permute-start.1) | collective-permute-done | bytes 524320 | tf_op jit(solution)/shard_map/ppermute | solution.py:408
  15.8 1.4 %collective-permute-done.refs_1_ = bf16[2048,128]{1,0:T(8,128)(2,1)S(1)} collective-permute-done((bf16[2048,128]{1,0:T(8,128)(2,1)}, bf16[2048,128]{1,0:T(8,128)(2,1)S(1)}, u32[]{:S(2)}, u32[]{:S(2)}) %collective-permute-start) | collective-permute-done | bytes 524320 | tf_op jit(solution)/shard_map/ppermute | solution.py:408
  17.1 2.2 %collective-permute-start.4 = (bf16[2048,128]{1,0:T(8,128)(2,1)S(1)}, bf16[2048,128]{1,0:T(8,128)(2,1)S(1)}, u32[]{:S(2)}, u32[]{:S(2)}) collective-permute-start(bf16[2048,128]{1,0:T(8,128)(2,1)S(1)} %collective-permute-done.1.refs_1_), channel_id=1, source_target_pairs={{4,0},{8,12},{5,1},{9,13},{6,2},{10,14},{7,3},{11,15},{20,16},{24,... | collective-permute-start | bytes 1572872 | tf_op jit(solution)/shard_map/ppermute | solution.py:408
  19.4 2.4 %collective-permute-start.3 = (bf16[1024,128]{1,0:T(8,128)(2,1)S(1)}, bf16[1024,128]{1,0:T(8,128)(2,1)S(1)}, u32[]{:S(2)}, u32[]{:S(2)}) collective-permute-start(bf16[1024,128]{1,0:T(8,128)(2,1)S(1)} %get-tuple-element.93), channel_id=1, source_target_pairs={{4,8},{8,4},{5,9},{9,5},{6,10},{10,6},{7,11},{11,7},{20,24},{24,20... | collective-permute-start | bytes 786440 | tf_op jit(solution)/shard_map/ppermute | solution.py:408
  21.8 3.5 %collective-permute-start.2 = (bf16[1024,128]{1,0:T(8,128)(2,1)S(1)}, bf16[1024,128]{1,0:T(8,128)(2,1)S(1)}, u32[]{:S(2)}, u32[]{:S(2)}) collective-permute-start(bf16[1024,128]{1,0:T(8,128)(2,1)S(1)} %get-tuple-element.94), channel_id=1, source_target_pairs={{4,8},{8,4},{5,9},{9,5},{6,10},{10,6},{7,11},{11,7},{20,24},{24,20... | collective-permute-start | bytes 786440 | tf_op jit(solution)/shard_map/ppermute | solution.py:408
  25.3 0.1 negate_select_fusion.1
  25.4 0.1 broadcast_in_dim.4.refs_8_
  25.5 44.8 %attend_0.1 = (f32[2,6,512,128]{3,2,1,0:T(8,128)S(1)}, f32[2,6,512,128]{3,2,1,0:T(8,128)S(1)}, f32[2,6,512,128]{3,2,1,0:T(8,128)S(1)}, f32[1]{0:T(128)S(4)}) custom-call(bf16[2048,128]{1,0:T(8,128)(2,1)S(1)} %get-tuple-element.53.refs_0_, bf16[2048,128]{1,0:T(8,128)(2,1)S(1)} %collective-permute-done.refs_1_, s32[79]{0:T(128)S(4)} %get-tuple-element.54.refs_2_, ...), custom_call_target="tpu_custom_call" | custom-call | tf_op jit(solution)/shard_map/attend_0/pallas_call | solution.py:455
  70.4 0.0 collective-permute-done.3.refs_1_
  70.4 0.0 collective-permute-done.4.refs_0_
  70.4 1.3 %collective-permute-start.6 = (bf16[1024,128]{1,0:T(8,128)(2,1)S(1)}, bf16[1024,128]{1,0:T(8,128)(2,1)S(1)}, u32[]{:S(2)}, u32[]{:S(2)}) collective-permute-start(bf16[1024,128]{1,0:T(8,128)(2,1)S(1)} %collective-permute-done.3.refs_1_), channel_id=1, source_target_pairs={{4,0},{8,12},{5,1},{9,13},{6,2},{10,14},{7,3},{11,15},{20,16},{24,... | collective-permute-start | bytes 786440 | tf_op jit(solution)/shard_map/ppermute | solution.py:408
  71.7 0.0 collective-permute-done.2.refs_1_
  71.7 1.3 %collective-permute-start.5 = (bf16[1024,128]{1,0:T(8,128)(2,1)S(1)}, bf16[1024,128]{1,0:T(8,128)(2,1)S(1)}, u32[]{:S(2)}, u32[]{:S(2)}) collective-permute-start(bf16[1024,128]{1,0:T(8,128)(2,1)S(1)} %collective-permute-done.2.refs_1_), channel_id=1, source_target_pairs={{4,0},{8,12},{5,1},{9,13},{6,2},{10,14},{7,3},{11,15},{20,16},{24,... | collective-permute-start | bytes 786440 | tf_op jit(solution)/shard_map/ppermute | solution.py:408
  73.0 23.5 %attend_1.1 = (f32[2,6,512,128]{3,2,1,0:T(8,128)S(1)}, f32[2,6,512,128]{3,2,1,0:T(8,128)S(1)}, f32[2,6,512,128]{3,2,1,0:T(8,128)S(1)}, f32[1]{0:T(128)S(4)}) custom-call(bf16[2048,128]{1,0:T(8,128)(2,1)S(1)} %collective-permute-done.4.refs_0_, ...), custom_call_target="tpu_custom_call", output_to_operand_aliasing={{0}: (9, {}), {1}: (10, {}), {2}: (11, {})} | custom-call | tf_op jit(solution)/shard_map/attend_1/pallas_call | solution.py:455
  96.5 0.0 collective-permute-done.6.refs_0_
  96.5 14.4 %attend_2.1 = (f32[2,6,512,128]{3,2,1,0:T(8,128)S(1)}, f32[2,6,512,128]{3,2,1,0:T(8,128)S(1)}, f32[2,6,512,128]{3,2,1,0:T(8,128)S(1)}, f32[1]{0:T(128)S(4)}) custom-call(bf16[1024,128]{1,0:T(8,128)(2,1)S(1)} %collective-permute-done.6.refs_0_, ...), custom_call_target="tpu_custom_call", output_to_operand_aliasing={{0}: (9, {}), {1}: (10, {}), {2}: (11, {})} | custom-call | tf_op jit(solution)/shard_map/attend_2/pallas_call | solution.py:455
  110.9 0.0 collective-permute-done.5.refs_0_
  110.9 12.8 %attend_3.1 = (f32[2,6,512,128]{3,2,1,0:T(8,128)S(1)}, f32[2,6,512,128]{3,2,1,0:T(8,128)S(1)}, f32[2,6,512,128]{3,2,1,0:T(8,128)S(1)}, f32[1]{0:T(128)S(4)}, bf16[384,2048]{1,0:T(8,128)(2,1)}) custom-call(bf16[1024,128]{1,0:T(8,128)(2,1)S(1)} %collective-permute-done.5.refs_0_, ...), custom_call_target="tpu_custom_call", output_to_operand_aliasing={{0}: (9, {}), {1}: (10, {}), {2}: (11, {})} | custom-call | tf_op jit(solution)/shard_map/attend_3/pallas_call | solution.py:455
  (5 shorter events, 0.1 us)
Async XLA Ops:
  0.0 15.8 %collective-permute-start.1 = (bf16[2048,128]{1,0:T(8,128)(2,1)}, bf16[2048,128]{1,0:T(8,128)(2,1)S(1)}, u32[]{:S(2)}, u32[]{:S(2)}) collective-permute-start(bf16[2048,128]{1,0:T(8,128)(2,1)} %bitcast.15), channel_id=1, source_target_pairs={{4,8},{8,4},{5,9},{9,5},{6,10},{10,6},{7,11},{11,7},{20,24},{24,20... | collective-permute-start | bytes 1572872 | tf_op jit(solution)/shard_map/ppermute | solution.py:408
  3.5 13.7 %collective-permute-start = (bf16[2048,128]{1,0:T(8,128)(2,1)}, bf16[2048,128]{1,0:T(8,128)(2,1)S(1)}, u32[]{:S(2)}, u32[]{:S(2)}) collective-permute-start(bf16[2048,128]{1,0:T(8,128)(2,1)} %bitcast.16), channel_id=1, source_target_pairs={{0,4},{4,0},{8,12},{12,8},{1,5},{5,1},{9,13},{13,9},{2,6},{6,2},{1... | collective-permute-start | bytes 1572872 | tf_op jit(solution)/shard_map/ppermute | solution.py:408
  17.1 53.3 %collective-permute-start.4 = (bf16[2048,128]{1,0:T(8,128)(2,1)S(1)}, bf16[2048,128]{1,0:T(8,128)(2,1)S(1)}, u32[]{:S(2)}, u32[]{:S(2)}) collective-permute-start(bf16[2048,128]{1,0:T(8,128)(2,1)S(1)} %collective-permute-done.1.refs_1_), channel_id=1, source_target_pairs={{4,0},{8,12},{5,1},{9,13},{6,2},{10,14},{7,3},{11,15},{20,16},{24,... | collective-permute-start | bytes 1572872 | tf_op jit(solution)/shard_map/ppermute | solution.py:408
  19.4 51.0 %collective-permute-start.3 = (bf16[1024,128]{1,0:T(8,128)(2,1)S(1)}, bf16[1024,128]{1,0:T(8,128)(2,1)S(1)}, u32[]{:S(2)}, u32[]{:S(2)}) collective-permute-start(bf16[1024,128]{1,0:T(8,128)(2,1)S(1)} %get-tuple-element.93), channel_id=1, source_target_pairs={{4,8},{8,4},{5,9},{9,5},{6,10},{10,6},{7,11},{11,7},{20,24},{24,20... | collective-permute-start | bytes 786440 | tf_op jit(solution)/shard_map/ppermute | solution.py:408
  21.8 49.9 %collective-permute-start.2 = (bf16[1024,128]{1,0:T(8,128)(2,1)S(1)}, bf16[1024,128]{1,0:T(8,128)(2,1)S(1)}, u32[]{:S(2)}, u32[]{:S(2)}) collective-permute-start(bf16[1024,128]{1,0:T(8,128)(2,1)S(1)} %get-tuple-element.94), channel_id=1, source_target_pairs={{4,8},{8,4},{5,9},{9,5},{6,10},{10,6},{7,11},{11,7},{20,24},{24,20... | collective-permute-start | bytes 786440 | tf_op jit(solution)/shard_map/ppermute | solution.py:408
  70.4 26.1 %collective-permute-start.6 = (bf16[1024,128]{1,0:T(8,128)(2,1)S(1)}, bf16[1024,128]{1,0:T(8,128)(2,1)S(1)}, u32[]{:S(2)}, u32[]{:S(2)}) collective-permute-start(bf16[1024,128]{1,0:T(8,128)(2,1)S(1)} %collective-permute-done.3.refs_1_), channel_id=1, source_target_pairs={{4,0},{8,12},{5,1},{9,13},{6,2},{10,14},{7,3},{11,15},{20,16},{24,... | collective-permute-start | bytes 786440 | tf_op jit(solution)/shard_map/ppermute | solution.py:408
  71.7 39.2 %collective-permute-start.5 = (bf16[1024,128]{1,0:T(8,128)(2,1)S(1)}, bf16[1024,128]{1,0:T(8,128)(2,1)S(1)}, u32[]{:S(2)}, u32[]{:S(2)}) collective-permute-start(bf16[1024,128]{1,0:T(8,128)(2,1)S(1)} %collective-permute-done.2.refs_1_), channel_id=1, source_target_pairs={{4,0},{8,12},{5,1},{9,13},{6,2},{10,14},{7,3},{11,15},{20,16},{24,... | collective-permute-start | bytes 786440 | tf_op jit(solution)/shard_map/ppermute | solution.py:408

commit v5 on v3

--- a/solution.py
+++ b/solution.py
@@ -454,9 +454,10 @@
 
     beside = send(store, outer)
     across = send(store, inner)
+    store, close, turned = lax.optimization_barrier((store, close, turned))
+    third_in = send(store, [(0, 2), (3, 1)])
     beside, across, close, turned = lax.optimization_barrier((beside, across, close, turned))
     second = send(across, outward)
-    third_in = send(beside, inner)
     state = attention(0, False, [close, beside], [lambda at: at, lambda at: at ^ 1], 1, 2, (peak,))
     second, third_in, state = lax.optimization_barrier((second, third_in, state))
     third = send(third_in, outward)

time: 119 us -> 121 us (1.017)
  the two profiles are of different devices: /device:TPU:8 before, /device:TPU:20 now
where the time goes in v5:
time: 121 us; the launch traced here: 120 us
  Pallas kernels  95.9 us (79%)
  starting transfers between devices  17.1 us (14%)
  waiting for transfers between devices  4.93 us (4%)
  other arithmetic  1.62 us (1%)
    pallas_call x3, Pallas kernels, attention(): pl.pallas_call(functools.partial(attend, shards, pick, units, first, last...  89.6 us
    ppermute x5, starting transfers between devices, send(): return lax.ppermute(array, 'req', pairs)  17.1 us
    pallas_call x1, Pallas kernels, on_device(): pl.pallas_call(prepare, out_shape=(pltpu.VMEM((heads, tiles, lanes_rows,...  6.37 us
    ppermute x5, waiting for transfers between devices, send(): return lax.ppermute(array, 'req', pairs)  4.93 us
  transfers between devices with their start and end apart: 5, of which 2 were waited for; matrix products, arithmetic and copies ran while one was open for 1% of the time, Pallas kernels for 55%

profile of v5, /device:TPU:20, one launch (start us, length us, event | category | flops | bytes accessed | tf_op | source)
XLA Modules:
  0.0 119.8 jit_solution(11487219448745703264)
XLA Ops:
  0.0 0.0 copy-start
  0.0 2.5 %collective-permute-start.1 = (bf16[2048,128]{1,0:T(8,128)(2,1)}, bf16[2048,128]{1,0:T(8,128)(2,1)S(1)}, u32[]{:S(2)}, u32[]{:S(2)}) collective-permute-start(bf16[2048,128]{1,0:T(8,128)(2,1)} %bitcast.15), channel_id=1, source_target_pairs={{4,8},{8,4},{5,9},{9,5},{6,10},{10,6},{7,11},{11,7},{20,24},{24,20... | collective-permute-start | bytes 1572872 | tf_op jit(solution)/shard_map/ppermute | solution.py:453
  2.5 0.1 collective-permute-start
  2.6 0.7 reduce
  3.3 0.8 negate_select_fusion
  4.1 6.4 %prepare.1 = (bf16[2,6,512,128]{3,2,1,0:T(8,128)(2,1)S(1)}, bf16[3072,640]{1,0:T(8,128)(2,1)S(1)}, bf16[2048,128]{1,0:T(8,128)(2,1)S(1)}, s32[79]{0:T(128)S(4)}, f32[1]{0:T(128)S(4)}) custom-call(bf16[384,2048]{1,0:T(8,128)(2,1)} %bitcast.14, bf16[1536,128]{1,0:T(8,128)(2,1)} %bitcast.19, bf16[2048,128]{1,0:T(8,128)(2,1)} %bitcast.17, s32[1,24]{1,0:T(1,128)} %bitcast.20, ...), custom_call_target="tpu_custom_call" | custom-call | tf_op jit(solution)/shard_map/prepare/pallas_call | solution.py:384
  10.5 0.0 copy-done
  10.5 1.3 %collective-permute-start.3 = (bf16[2048,128]{1,0:T(8,128)(2,1)S(1)}, bf16[2048,128]{1,0:T(8,128)(2,1)S(1)}, u32[]{:S(2)}, u32[]{:S(2)}) collective-permute-start(bf16[2048,128]{1,0:T(8,128)(2,1)S(1)} %bitcast.18), channel_id=1, source_target_pairs={{0,8},{12,4},{1,9},{13,5},{2,10},{14,6},{3,11},{15,7},{16,24},{28,... | collective-permute-start | bytes 1572872 | tf_op jit(solution)/shard_map/ppermute | solution.py:453
  11.8 4.3 %collective-permute-done.1.refs_1_ = bf16[2048,128]{1,0:T(8,128)(2,1)S(1)} collective-permute-done((bf16[2048,128]{1,0:T(8,128)(2,1)}, bf16[2048,128]{1,0:T(8,128)(2,1)S(1)}, u32[]{:S(2)}, u32[]{:S(2)}) %collective-permute-start.1) | collective-permute-done | bytes 524320 | tf_op jit(solution)/shard_map/ppermute | solution.py:453
  16.1 0.6 collective-permute-done.refs_1_
  16.7 1.7 %collective-permute-start.2 = (bf16[2048,128]{1,0:T(8,128)(2,1)S(1)}, bf16[2048,128]{1,0:T(8,128)(2,1)S(1)}, u32[]{:S(2)}, u32[]{:S(2)}) collective-permute-start(bf16[2048,128]{1,0:T(8,128)(2,1)S(1)} %collective-permute-done.1.refs_1_), channel_id=1, source_target_pairs={{4,0},{8,12},{5,1},{9,13},{6,2},{10,14},{7,3},{11,15},{20,16},{24,... | collective-permute-start | bytes 1572872 | tf_op jit(solution)/shard_map/ppermute | solution.py:453
  18.4 0.1 negate_select_fusion.1
  18.5 0.1 broadcast_in_dim.4.refs_8_
  18.6 37.3 %attend_0.1 = (f32[2,6,512,128]{3,2,1,0:T(8,128)S(1)}, f32[2,6,512,128]{3,2,1,0:T(8,128)S(1)}, f32[2,6,512,128]{3,2,1,0:T(8,128)S(1)}, f32[1]{0:T(128)S(4)}) custom-call(bf16[2048,128]{1,0:T(8,128)(2,1)S(1)} %get-tuple-element.43.refs_0_, bf16[2048,128]{1,0:T(8,128)(2,1)S(1)} %collective-permute-done.refs_1_, s32[79]{0:T(128)S(4)} %get-tuple-element.45.refs_2_, ...), custom_call_target="tpu_custom_call" | custom-call | tf_op jit(solution)/shard_map/attend_0/pallas_call | solution.py:423
  56.0 0.0 collective-permute-done.3.refs_1_
  56.0 0.0 collective-permute-done.2.refs_0_
  56.0 11.6 %collective-permute-start.4 = (bf16[2048,128]{1,0:T(8,128)(2,1)S(1)}, bf16[2048,128]{1,0:T(8,128)(2,1)S(1)}, u32[]{:S(2)}, u32[]{:S(2)}) collective-permute-start(bf16[2048,128]{1,0:T(8,128)(2,1)S(1)} %collective-permute-done.3.refs_1_), channel_id=1, source_target_pairs={{4,0},{8,12},{5,1},{9,13},{6,2},{10,14},{7,3},{11,15},{20,16},{24,... | collective-permute-start | bytes 1572872 | tf_op jit(solution)/shard_map/ppermute | solution.py:453
  67.5 22.7 %attend_1.1 = (f32[2,6,512,128]{3,2,1,0:T(8,128)S(1)}, f32[2,6,512,128]{3,2,1,0:T(8,128)S(1)}, f32[2,6,512,128]{3,2,1,0:T(8,128)S(1)}, f32[1]{0:T(128)S(4)}) custom-call(bf16[2048,128]{1,0:T(8,128)(2,1)S(1)} %collective-permute-done.2.refs_0_, ...), custom_call_target="tpu_custom_call", output_to_operand_aliasing={{0}: (9, {}), {1}: (10, {}), {2}: (11, {})} | custom-call | tf_op jit(solution)/shard_map/attend_1/pallas_call | solution.py:423
  90.2 0.0 collective-permute-done.4.refs_0_
  90.3 29.6 %attend_2.1 = (f32[2,6,512,128]{3,2,1,0:T(8,128)S(1)}, f32[2,6,512,128]{3,2,1,0:T(8,128)S(1)}, f32[2,6,512,128]{3,2,1,0:T(8,128)S(1)}, f32[1]{0:T(128)S(4)}, bf16[384,2048]{1,0:T(8,128)(2,1)}) custom-call(bf16[2048,128]{1,0:T(8,128)(2,1)S(1)} %collective-permute-done.4.refs_0_, ...), custom_call_target="tpu_custom_call", output_to_operand_aliasing={{0}: (9, {}), {1}: (10, {}), {2}: (11, {})} | custom-call | tf_op jit(solution)/shard_map/attend_2/pallas_call | solution.py:423
  (4 shorter events, 0.0 us)
Async XLA Ops:
  0.0 10.5 %copy-start = (bf16[4,128,2,256]{3,2,1,0:T(2,128)(2,1)S(1)}, bf16[4,128,2,256]{3,2,1,0:T(2,128)(2,1)}, u32[]{:S(2)}) copy-start(bf16[4,128,2,256]{3,2,1,0:T(2,128)(2,1)} %param.7) | copy-start | bytes 1572868
  0.0 16.1 %collective-permute-start.1 = (bf16[2048,128]{1,0:T(8,128)(2,1)}, bf16[2048,128]{1,0:T(8,128)(2,1)S(1)}, u32[]{:S(2)}, u32[]{:S(2)}) collective-permute-start(bf16[2048,128]{1,0:T(8,128)(2,1)} %bitcast.15), channel_id=1, source_target_pairs={{4,8},{8,4},{5,9},{9,5},{6,10},{10,6},{7,11},{11,7},{20,24},{24,20... | collective-permute-start | bytes 1572872 | tf_op jit(solution)/shard_map/ppermute | solution.py:453
  2.5 14.2 %collective-permute-start = (bf16[2048,128]{1,0:T(8,128)(2,1)}, bf16[2048,128]{1,0:T(8,128)(2,1)S(1)}, u32[]{:S(2)}, u32[]{:S(2)}) collective-permute-start(bf16[2048,128]{1,0:T(8,128)(2,1)} %bitcast.16), channel_id=1, source_target_pairs={{0,4},{4,0},{8,12},{12,8},{1,5},{5,1},{9,13},{13,9},{2,6},{6,2},{1... | collective-permute-start | bytes 1572872 | tf_op jit(solution)/shard_map/ppermute | solution.py:453
  10.5 45.5 %collective-permute-start.3 = (bf16[2048,128]{1,0:T(8,128)(2,1)S(1)}, bf16[2048,128]{1,0:T(8,128)(2,1)S(1)}, u32[]{:S(2)}, u32[]{:S(2)}) collective-permute-start(bf16[2048,128]{1,0:T(8,128)(2,1)S(1)} %bitcast.18), channel_id=1, source_target_pairs={{0,8},{12,4},{1,9},{13,5},{2,10},{14,6},{3,11},{15,7},{16,24},{28,... | collective-permute-start | bytes 1572872 | tf_op jit(solution)/shard_map/ppermute | solution.py:453
  16.7 39.3 %collective-permute-start.2 = (bf16[2048,128]{1,0:T(8,128)(2,1)S(1)}, bf16[2048,128]{1,0:T(8,128)(2,1)S(1)}, u32[]{:S(2)}, u32[]{:S(2)}) collective-permute-start(bf16[2048,128]{1,0:T(8,128)(2,1)S(1)} %collective-permute-done.1.refs_1_), channel_id=1, source_target_pairs={{4,0},{8,12},{5,1},{9,13},{6,2},{10,14},{7,3},{11,15},{20,16},{24,... | collective-permute-start | bytes 1572872 | tf_op jit(solution)/shard_map/ppermute | solution.py:453
  56.0 34.3 %collective-permute-start.4 = (bf16[2048,128]{1,0:T(8,128)(2,1)S(1)}, bf16[2048,128]{1,0:T(8,128)(2,1)S(1)}, u32[]{:S(2)}, u32[]{:S(2)}) collective-permute-start(bf16[2048,128]{1,0:T(8,128)(2,1)S(1)} %collective-permute-done.3.refs_1_), channel_id=1, source_target_pairs={{4,0},{8,12},{5,1},{9,13},{6,2},{10,14},{7,3},{11,15},{20,16},{24,... | collective-permute-start | bytes 1572872 | tf_op jit(solution)/shard_map/ppermute | solution.py:453

commit v6 on v3

--- a/solution.py
+++ b/solution.py
@@ -13,8 +13,8 @@
 unit_blocks = 6
 low = -1e30
 bound = 105.0
-grain = 2
-chunk = 3
+grain = 1
+chunk = 6
 vmem = pl.BlockSpec(memory_space=pltpu.VMEM)
 smem = pl.BlockSpec(memory_space=pltpu.SMEM)
 anywhere = pl.BlockSpec(memory_space=pl.ANY)
@@ -454,9 +454,10 @@
 
     beside = send(store, outer)
     across = send(store, inner)
-    beside, across, close, turned = lax.optimization_barrier((beside, across, close, turned))
+    beside, close, turned = lax.optimization_barrier((beside, close, turned))
+    third_in = send(beside, inner)
+    across, close, turned = lax.optimization_barrier((across, close, turned))
     second = send(across, outward)
-    third_in = send(beside, inner)
     state = attention(0, False, [close, beside], [lambda at: at, lambda at: at ^ 1], 1, 2, (peak,))
     second, third_in, state = lax.optimization_barrier((second, third_in, state))
     third = send(third_in, outward)

time: 119 us -> 118 us (level)
  the two profiles are of different devices: /device:TPU:8 before, /device:TPU:22 now
where the time goes in v6:
time: 118 us; the launch traced here: 120 us
  Pallas kernels  94.4 us (80%)
  starting transfers between devices  18 us (15%)
  waiting for transfers between devices  5.67 us (5%)
  other arithmetic  1.62 us (1%)
    pallas_call x3, Pallas kernels, attention(): pl.pallas_call(functools.partial(attend, shards, pick, units, first, last...  88 us
    ppermute x5, starting transfers between devices, send(): return lax.ppermute(array, 'req', pairs)  18 us
    pallas_call x1, Pallas kernels, on_device(): pl.pallas_call(prepare, out_shape=(pltpu.VMEM((heads, tiles, lanes_rows,...  6.38 us
    ppermute x5, waiting for transfers between devices, send(): return lax.ppermute(array, 'req', pairs)  5.67 us
  transfers between devices with their start and end apart: 5, of which 2 were waited for; matrix products, arithmetic and copies ran while one was open for 1% of the time, Pallas kernels for 54%

profile of v6, /device:TPU:22, one launch (start us, length us, event | category | flops | bytes accessed | tf_op | source)
XLA Modules:
  0.0 119.9 jit_solution(10860200554874000236)
XLA Ops:
  0.0 1.6 %collective-permute-start.1 = (bf16[2048,128]{1,0:T(8,128)(2,1)}, bf16[2048,128]{1,0:T(8,128)(2,1)S(1)}, u32[]{:S(2)}, u32[]{:S(2)}) collective-permute-start(bf16[2048,128]{1,0:T(8,128)(2,1)} %bitcast.15), channel_id=1, source_target_pairs={{0,4},{4,0},{8,12},{12,8},{1,5},{5,1},{9,13},{13,9},{2,6},{6,2},{1... | collective-permute-start | bytes 1572872 | tf_op jit(solution)/shard_map/ppermute | solution.py:453
  1.6 1.9 %collective-permute-start = (bf16[2048,128]{1,0:T(8,128)(2,1)}, bf16[2048,128]{1,0:T(8,128)(2,1)S(1)}, u32[]{:S(2)}, u32[]{:S(2)}) collective-permute-start(bf16[2048,128]{1,0:T(8,128)(2,1)} %bitcast.16), channel_id=1, source_target_pairs={{4,8},{8,4},{5,9},{9,5},{6,10},{10,6},{7,11},{11,7},{20,24},{24,20... | collective-permute-start | bytes 1572872 | tf_op jit(solution)/shard_map/ppermute | solution.py:453
  3.5 0.7 reduce
  4.2 0.8 negate_select_fusion
  5.0 6.4 %prepare.1 = (bf16[2,6,512,128]{3,2,1,0:T(8,128)(2,1)S(1)}, bf16[3072,640]{1,0:T(8,128)(2,1)S(1)}, bf16[2048,128]{1,0:T(8,128)(2,1)S(1)}, s32[79]{0:T(128)S(4)}, f32[1]{0:T(128)S(4)}) custom-call(bf16[384,2048]{1,0:T(8,128)(2,1)} %bitcast.14, bf16[1536,128]{1,0:T(8,128)(2,1)} %bitcast.18, bf16[2048,128]{1,0:T(8,128)(2,1)} %bitcast.17, s32[1,24]{1,0:T(1,128)} %bitcast.19, ...), custom_call_target="tpu_custom_call" | custom-call | tf_op jit(solution)/shard_map/prepare/pallas_call | solution.py:384
  11.4 2.5 %collective-permute-done.1.refs_1_ = bf16[2048,128]{1,0:T(8,128)(2,1)S(1)} collective-permute-done((bf16[2048,128]{1,0:T(8,128)(2,1)}, bf16[2048,128]{1,0:T(8,128)(2,1)S(1)}, u32[]{:S(2)}, u32[]{:S(2)}) %collective-permute-start.1) | collective-permute-done | bytes 524320 | tf_op jit(solution)/shard_map/ppermute | solution.py:453
  13.9 3.2 %collective-permute-done.refs_1_ = bf16[2048,128]{1,0:T(8,128)(2,1)S(1)} collective-permute-done((bf16[2048,128]{1,0:T(8,128)(2,1)}, bf16[2048,128]{1,0:T(8,128)(2,1)S(1)}, u32[]{:S(2)}, u32[]{:S(2)}) %collective-permute-start) | collective-permute-done | bytes 524320 | tf_op jit(solution)/shard_map/ppermute | solution.py:453
  17.1 1.3 %collective-permute-start.2 = (bf16[2048,128]{1,0:T(8,128)(2,1)S(1)}, bf16[2048,128]{1,0:T(8,128)(2,1)S(1)}, u32[]{:S(2)}, u32[]{:S(2)}) collective-permute-start(bf16[2048,128]{1,0:T(8,128)(2,1)S(1)} %collective-permute-done.refs_1_), channel_id=1, source_target_pairs={{4,0},{8,12},{5,1},{9,13},{6,2},{10,14},{7,3},{11,15},{20,16},{24,... | collective-permute-start | bytes 1572872 | tf_op jit(solution)/shard_map/ppermute | solution.py:453
  18.4 2.2 %collective-permute-start.3 = (bf16[2048,128]{1,0:T(8,128)(2,1)S(1)}, bf16[2048,128]{1,0:T(8,128)(2,1)S(1)}, u32[]{:S(2)}, u32[]{:S(2)}) collective-permute-start(bf16[2048,128]{1,0:T(8,128)(2,1)S(1)} %collective-permute-done.1.refs_1_), channel_id=1, source_target_pairs={{4,8},{8,4},{5,9},{9,5},{6,10},{10,6},{7,11},{11,7},{20,24},{24,20... | collective-permute-start | bytes 1572872 | tf_op jit(solution)/shard_map/ppermute | solution.py:453
  20.6 0.1 negate_select_fusion.1
  20.7 0.1 broadcast_in_dim.4.refs_8_
  20.8 36.2 %attend_0.1 = (f32[2,6,512,128]{3,2,1,0:T(8,128)S(1)}, f32[2,6,512,128]{3,2,1,0:T(8,128)S(1)}, f32[2,6,512,128]{3,2,1,0:T(8,128)S(1)}, f32[1]{0:T(128)S(4)}) custom-call(bf16[2048,128]{1,0:T(8,128)(2,1)S(1)} %get-tuple-element.42.refs_0_, bf16[2048,128]{1,0:T(8,128)(2,1)S(1)} %collective-permute-done.1.refs_1_, s32[79]{0:T(128)S(4)} %get-tuple-element.43.refs_2_, ...), custom_call_target="tpu_custom_call" | custom-call | tf_op jit(solution)/shard_map/attend_0/pallas_call | solution.py:423
  57.1 0.0 collective-permute-done.2.refs_0_
  57.1 0.0 collective-permute-done.3.refs_1_
  57.1 11.0 %collective-permute-start.4 = (bf16[2048,128]{1,0:T(8,128)(2,1)S(1)}, bf16[2048,128]{1,0:T(8,128)(2,1)S(1)}, u32[]{:S(2)}, u32[]{:S(2)}) collective-permute-start(bf16[2048,128]{1,0:T(8,128)(2,1)S(1)} %collective-permute-done.3.refs_1_), channel_id=1, source_target_pairs={{4,0},{8,12},{5,1},{9,13},{6,2},{10,14},{7,3},{11,15},{20,16},{24,... | collective-permute-start | bytes 1572872 | tf_op jit(solution)/shard_map/ppermute | solution.py:453
  68.1 22.5 %attend_1.1 = (f32[2,6,512,128]{3,2,1,0:T(8,128)S(1)}, f32[2,6,512,128]{3,2,1,0:T(8,128)S(1)}, f32[2,6,512,128]{3,2,1,0:T(8,128)S(1)}, f32[1]{0:T(128)S(4)}) custom-call(bf16[2048,128]{1,0:T(8,128)(2,1)S(1)} %collective-permute-done.2.refs_0_, ...), custom_call_target="tpu_custom_call", output_to_operand_aliasing={{0}: (9, {}), {1}: (10, {}), {2}: (11, {})} | custom-call | tf_op jit(solution)/shard_map/attend_1/pallas_call | solution.py:423
  90.6 0.0 collective-permute-done.4.refs_0_
  90.6 29.2 %attend_2.1 = (f32[2,6,512,128]{3,2,1,0:T(8,128)S(1)}, f32[2,6,512,128]{3,2,1,0:T(8,128)S(1)}, f32[2,6,512,128]{3,2,1,0:T(8,128)S(1)}, f32[1]{0:T(128)S(4)}, bf16[384,2048]{1,0:T(8,128)(2,1)}) custom-call(bf16[2048,128]{1,0:T(8,128)(2,1)S(1)} %collective-permute-done.4.refs_0_, ...), custom_call_target="tpu_custom_call", output_to_operand_aliasing={{0}: (9, {}), {1}: (10, {}), {2}: (11, {})} | custom-call | tf_op jit(solution)/shard_map/attend_2/pallas_call | solution.py:423
  (4 shorter events, 0.0 us)
Async XLA Ops:
  0.0 13.9 %collective-permute-start.1 = (bf16[2048,128]{1,0:T(8,128)(2,1)}, bf16[2048,128]{1,0:T(8,128)(2,1)S(1)}, u32[]{:S(2)}, u32[]{:S(2)}) collective-permute-start(bf16[2048,128]{1,0:T(8,128)(2,1)} %bitcast.15), channel_id=1, source_target_pairs={{0,4},{4,0},{8,12},{12,8},{1,5},{5,1},{9,13},{13,9},{2,6},{6,2},{1... | collective-permute-start | bytes 1572872 | tf_op jit(solution)/shard_map/ppermute | solution.py:453
  1.6 15.5 %collective-permute-start = (bf16[2048,128]{1,0:T(8,128)(2,1)}, bf16[2048,128]{1,0:T(8,128)(2,1)S(1)}, u32[]{:S(2)}, u32[]{:S(2)}) collective-permute-start(bf16[2048,128]{1,0:T(8,128)(2,1)} %bitcast.16), channel_id=1, source_target_pairs={{4,8},{8,4},{5,9},{9,5},{6,10},{10,6},{7,11},{11,7},{20,24},{24,20... | collective-permute-start | bytes 1572872 | tf_op jit(solution)/shard_map/ppermute | solution.py:453
  17.1 40.0 %collective-permute-start.2 = (bf16[2048,128]{1,0:T(8,128)(2,1)S(1)}, bf16[2048,128]{1,0:T(8,128)(2,1)S(1)}, u32[]{:S(2)}, u32[]{:S(2)}) collective-permute-start(bf16[2048,128]{1,0:T(8,128)(2,1)S(1)} %collective-permute-done.refs_1_), channel_id=1, source_target_pairs={{4,0},{8,12},{5,1},{9,13},{6,2},{10,14},{7,3},{11,15},{20,16},{24,... | collective-permute-start | bytes 1572872 | tf_op jit(solution)/shard_map/ppermute | solution.py:453
  18.4 38.7 %collective-permute-start.3 = (bf16[2048,128]{1,0:T(8,128)(2,1)S(1)}, bf16[2048,128]{1,0:T(8,128)(2,1)S(1)}, u32[]{:S(2)}, u32[]{:S(2)}) collective-permute-start(bf16[2048,128]{1,0:T(8,128)(2,1)S(1)} %collective-permute-done.1.refs_1_), channel_id=1, source_target_pairs={{4,8},{8,4},{5,9},{9,5},{6,10},{10,6},{7,11},{11,7},{20,24},{24,20... | collective-permute-start | bytes 1572872 | tf_op jit(solution)/shard_map/ppermute | solution.py:453
  57.1 33.5 %collective-permute-start.4 = (bf16[2048,128]{1,0:T(8,128)(2,1)S(1)}, bf16[2048,128]{1,0:T(8,128)(2,1)S(1)}, u32[]{:S(2)}, u32[]{:S(2)}) collective-permute-start(bf16[2048,128]{1,0:T(8,128)(2,1)S(1)} %collective-permute-done.3.refs_1_), channel_id=1, source_target_pairs={{4,0},{8,12},{5,1},{9,13},{6,2},{10,14},{7,3},{11,15},{20,16},{24,... | collective-permute-start | bytes 1572872 | tf_op jit(solution)/shard_map/ppermute | solution.py:453

commit v7 on v6

--- a/solution.py
+++ b/solution.py
@@ -378,7 +378,8 @@
     place = lax.axis_index("req").reshape(1)
     row_pos = row_index[0]
     row_cos, row_sin = tables(row_pos.astype(jnp.float32), dim)
-    cos, sin = tables(block_len * jnp.arange(blocks, dtype=jnp.float32), dim)
+    starts = block_len * jnp.arange(blocks, dtype=jnp.float32)
+    cos, sin = tables(starts, dim)
     row_lanes = jnp.broadcast_to(row_pos[:, None], (rows, block_len))
     wide = heads * 2 * dim + dim
     turned, placed, close, table, peak = pl.pallas_call(
@@ -454,9 +455,11 @@
 
     beside = send(store, outer)
     across = send(store, inner)
-    beside, close, turned = lax.optimization_barrier((beside, close, turned))
-    third_in = send(beside, inner)
-    across, close, turned = lax.optimization_barrier((across, close, turned))
+    store, close, turned = lax.optimization_barrier((store, close, turned))
+    third_in = send(store, [(0, 2), (3, 1)])
+    beside, starts = lax.optimization_barrier((beside, starts))
+    cos, sin = tables(starts, dim)
+    across, close, turned, cos, sin = lax.optimization_barrier((across, close, turned, cos, sin))
     second = send(across, outward)
     state = attention(0, False, [close, beside], [lambda at: at, lambda at: at ^ 1], 1, 2, (peak,))
     second, third_in, state = lax.optimization_barrier((second, third_in, state))

time: 118 us -> 124 us (1.051)
  the two profiles are of different devices: /device:TPU:22 before, /device:TPU:20 now
where the time goes in v7:
time: 124 us; the launch traced here: 122 us
  Pallas kernels  96.9 us (78%)
  waiting for transfers between devices  15.5 us (12%)
  starting transfers between devices  7.59 us (6%)
  other arithmetic  1.62 us (1%)
    pallas_call x3, Pallas kernels, attention(): pl.pallas_call(functools.partial(attend, shards, pick, units, first, last...  90.6 us
    ppermute x5, waiting for transfers between devices, send(): return lax.ppermute(array, 'req', pairs)  15.5 us
    ppermute x5, starting transfers between devices, send(): return lax.ppermute(array, 'req', pairs)  7.59 us
    pallas_call x1, Pallas kernels, on_device(): pl.pallas_call(prepare, out_shape=(pltpu.VMEM((heads, tiles, lanes_rows,...  6.38 us
  transfers between devices with their start and end apart: 5, of which 2 were waited for; matrix products, arithmetic and copies ran while one was open for 1% of the time, Pallas kernels for 54%

profile of v7, /device:TPU:20, one launch (start us, length us, event | category | flops | bytes accessed | tf_op | source)
XLA Modules:
  0.0 121.9 jit_solution(16088228792162474751)
XLA Ops:
  0.0 0.0 copy-start
  0.0 1.6 %collective-permute-start.1 = (bf16[2048,128]{1,0:T(8,128)(2,1)}, bf16[2048,128]{1,0:T(8,128)(2,1)S(1)}, u32[]{:S(2)}, u32[]{:S(2)}) collective-permute-start(bf16[2048,128]{1,0:T(8,128)(2,1)} %bitcast.15), channel_id=1, source_target_pairs={{0,4},{4,0},{8,12},{12,8},{1,5},{5,1},{9,13},{13,9},{2,6},{6,2},{1... | collective-permute-start | bytes 1572872 | tf_op jit(solution)/shard_map/ppermute | solution.py:454
  1.6 1.9 %collective-permute-start = (bf16[2048,128]{1,0:T(8,128)(2,1)}, bf16[2048,128]{1,0:T(8,128)(2,1)S(1)}, u32[]{:S(2)}, u32[]{:S(2)}) collective-permute-start(bf16[2048,128]{1,0:T(8,128)(2,1)} %bitcast.16), channel_id=1, source_target_pairs={{4,8},{8,4},{5,9},{9,5},{6,10},{10,6},{7,11},{11,7},{20,24},{24,20... | collective-permute-start | bytes 1572872 | tf_op jit(solution)/shard_map/ppermute | solution.py:454
  3.5 0.7 reduce
  4.2 0.8 negate_select_fusion
  5.0 6.4 %prepare.1 = (bf16[2,6,512,128]{3,2,1,0:T(8,128)(2,1)S(1)}, bf16[3072,640]{1,0:T(8,128)(2,1)S(1)}, bf16[2048,128]{1,0:T(8,128)(2,1)S(1)}, s32[79]{0:T(128)S(4)}, f32[1]{0:T(128)S(4)}) custom-call(bf16[384,2048]{1,0:T(8,128)(2,1)} %bitcast.14, bf16[1536,128]{1,0:T(8,128)(2,1)} %bitcast.19, bf16[2048,128]{1,0:T(8,128)(2,1)} %bitcast.17, s32[1,24]{1,0:T(1,128)} %bitcast.20, ...), custom_call_target="tpu_custom_call" | custom-call | tf_op jit(solution)/shard_map/prepare/pallas_call | solution.py:385
  11.4 0.0 copy-done
  11.4 1.3 %collective-permute-start.3 = (bf16[2048,128]{1,0:T(8,128)(2,1)S(1)}, bf16[2048,128]{1,0:T(8,128)(2,1)S(1)}, u32[]{:S(2)}, u32[]{:S(2)}) collective-permute-start(bf16[2048,128]{1,0:T(8,128)(2,1)S(1)} %bitcast.18), channel_id=1, source_target_pairs={{0,8},{12,4},{1,9},{13,5},{2,10},{14,6},{3,11},{15,7},{16,24},{28,... | collective-permute-start | bytes 1572872 | tf_op jit(solution)/shard_map/ppermute | solution.py:454
  12.7 1.2 collective-permute-done.1.refs_1_
  13.9 0.1 negate_select_fusion.1
  14.0 14.3 %collective-permute-done.refs_1_ = bf16[2048,128]{1,0:T(8,128)(2,1)S(1)} collective-permute-done((bf16[2048,128]{1,0:T(8,128)(2,1)}, bf16[2048,128]{1,0:T(8,128)(2,1)S(1)}, u32[]{:S(2)}, u32[]{:S(2)}) %collective-permute-start) | collective-permute-done | bytes 524320 | tf_op jit(solution)/shard_map/ppermute | solution.py:454
  28.3 1.3 %collective-permute-start.2 = (bf16[2048,128]{1,0:T(8,128)(2,1)S(1)}, bf16[2048,128]{1,0:T(8,128)(2,1)S(1)}, u32[]{:S(2)}, u32[]{:S(2)}) collective-permute-start(bf16[2048,128]{1,0:T(8,128)(2,1)S(1)} %collective-permute-done.refs_1_), channel_id=1, source_target_pairs={{4,0},{8,12},{5,1},{9,13},{6,2},{10,14},{7,3},{11,15},{20,16},{24,... | collective-permute-start | bytes 1572872 | tf_op jit(solution)/shard_map/ppermute | solution.py:454
  29.6 0.1 broadcast_in_dim.4.refs_8_
  29.7 39.6 %attend_0.1 = (f32[2,6,512,128]{3,2,1,0:T(8,128)S(1)}, f32[2,6,512,128]{3,2,1,0:T(8,128)S(1)}, f32[2,6,512,128]{3,2,1,0:T(8,128)S(1)}, f32[1]{0:T(128)S(4)}) custom-call(bf16[2048,128]{1,0:T(8,128)(2,1)S(1)} %get-tuple-element.47.refs_0_, bf16[2048,128]{1,0:T(8,128)(2,1)S(1)} %collective-permute-done.1.refs_1_, s32[79]{0:T(128)S(4)} %get-tuple-element.49.refs_2_, ...), custom_call_target="tpu_custom_call" | custom-call | tf_op jit(solution)/shard_map/attend_0/pallas_call | solution.py:424
  69.4 0.0 collective-permute-done.3.refs_1_
  69.4 0.0 collective-permute-done.2.refs_0_
  69.4 1.5 %collective-permute-start.4 = (bf16[2048,128]{1,0:T(8,128)(2,1)S(1)}, bf16[2048,128]{1,0:T(8,128)(2,1)S(1)}, u32[]{:S(2)}, u32[]{:S(2)}) collective-permute-start(bf16[2048,128]{1,0:T(8,128)(2,1)S(1)} %collective-permute-done.3.refs_1_), channel_id=1, source_target_pairs={{4,0},{8,12},{5,1},{9,13},{6,2},{10,14},{7,3},{11,15},{20,16},{24,... | collective-permute-start | bytes 1572872 | tf_op jit(solution)/shard_map/ppermute | solution.py:454
  70.9 20.0 %attend_1.1 = (f32[2,6,512,128]{3,2,1,0:T(8,128)S(1)}, f32[2,6,512,128]{3,2,1,0:T(8,128)S(1)}, f32[2,6,512,128]{3,2,1,0:T(8,128)S(1)}, f32[1]{0:T(128)S(4)}) custom-call(bf16[2048,128]{1,0:T(8,128)(2,1)S(1)} %collective-permute-done.2.refs_0_, ...), custom_call_target="tpu_custom_call", output_to_operand_aliasing={{0}: (9, {}), {1}: (10, {}), {2}: (11, {})} | custom-call | tf_op jit(solution)/shard_map/attend_1/pallas_call | solution.py:424
  90.9 0.0 collective-permute-done.4.refs_0_
  90.9 31.0 %attend_2.1 = (f32[2,6,512,128]{3,2,1,0:T(8,128)S(1)}, f32[2,6,512,128]{3,2,1,0:T(8,128)S(1)}, f32[2,6,512,128]{3,2,1,0:T(8,128)S(1)}, f32[1]{0:T(128)S(4)}, bf16[384,2048]{1,0:T(8,128)(2,1)}) custom-call(bf16[2048,128]{1,0:T(8,128)(2,1)S(1)} %collective-permute-done.4.refs_0_, ...), custom_call_target="tpu_custom_call", output_to_operand_aliasing={{0}: (9, {}), {1}: (10, {}), {2}: (11, {})} | custom-call | tf_op jit(solution)/shard_map/attend_2/pallas_call | solution.py:424
  (4 shorter events, 0.0 us)
Async XLA Ops:
  0.0 11.4 %copy-start = (bf16[4,128,2,256]{3,2,1,0:T(2,128)(2,1)S(1)}, bf16[4,128,2,256]{3,2,1,0:T(2,128)(2,1)}, u32[]{:S(2)}) copy-start(bf16[4,128,2,256]{3,2,1,0:T(2,128)(2,1)} %param.7) | copy-start | bytes 1572868
  0.0 13.9 %collective-permute-start.1 = (bf16[2048,128]{1,0:T(8,128)(2,1)}, bf16[2048,128]{1,0:T(8,128)(2,1)S(1)}, u32[]{:S(2)}, u32[]{:S(2)}) collective-permute-start(bf16[2048,128]{1,0:T(8,128)(2,1)} %bitcast.15), channel_id=1, source_target_pairs={{0,4},{4,0},{8,12},{12,8},{1,5},{5,1},{9,13},{13,9},{2,6},{6,2},{1... | collective-permute-start | bytes 1572872 | tf_op jit(solution)/shard_map/ppermute | solution.py:454
  1.6 26.7 %collective-permute-start = (bf16[2048,128]{1,0:T(8,128)(2,1)}, bf16[2048,128]{1,0:T(8,128)(2,1)S(1)}, u32[]{:S(2)}, u32[]{:S(2)}) collective-permute-start(bf16[2048,128]{1,0:T(8,128)(2,1)} %bitcast.16), channel_id=1, source_target_pairs={{4,8},{8,4},{5,9},{9,5},{6,10},{10,6},{7,11},{11,7},{20,24},{24,20... | collective-permute-start | bytes 1572872 | tf_op jit(solution)/shard_map/ppermute | solution.py:454
  11.4 58.0 %collective-permute-start.3 = (bf16[2048,128]{1,0:T(8,128)(2,1)S(1)}, bf16[2048,128]{1,0:T(8,128)(2,1)S(1)}, u32[]{:S(2)}, u32[]{:S(2)}) collective-permute-start(bf16[2048,128]{1,0:T(8,128)(2,1)S(1)} %bitcast.18), channel_id=1, source_target_pairs={{0,8},{12,4},{1,9},{13,5},{2,10},{14,6},{3,11},{15,7},{16,24},{28,... | collective-permute-start | bytes 1572872 | tf_op jit(solution)/shard_map/ppermute | solution.py:454
  28.3 41.1 %collective-permute-start.2 = (bf16[2048,128]{1,0:T(8,128)(2,1)S(1)}, bf16[2048,128]{1,0:T(8,128)(2,1)S(1)}, u32[]{:S(2)}, u32[]{:S(2)}) collective-permute-start(bf16[2048,128]{1,0:T(8,128)(2,1)S(1)} %collective-permute-done.refs_1_), channel_id=1, source_target_pairs={{4,0},{8,12},{5,1},{9,13},{6,2},{10,14},{7,3},{11,15},{20,16},{24,... | collective-permute-start | bytes 1572872 | tf_op jit(solution)/shard_map/ppermute | solution.py:454
  69.4 21.5 %collective-permute-start.4 = (bf16[2048,128]{1,0:T(8,128)(2,1)S(1)}, bf16[2048,128]{1,0:T(8,128)(2,1)S(1)}, u32[]{:S(2)}, u32[]{:S(2)}) collective-permute-start(bf16[2048,128]{1,0:T(8,128)(2,1)S(1)} %collective-permute-done.3.refs_1_), channel_id=1, source_target_pairs={{4,0},{8,12},{5,1},{9,13},{6,2},{10,14},{7,3},{11,15},{20,16},{24,... | collective-permute-start | bytes 1572872 | tf_op jit(solution)/shard_map/ppermute | solution.py:454

commit v8 on v6

--- a/solution.py
+++ b/solution.py
@@ -454,8 +454,8 @@
 
     beside = send(store, outer)
     across = send(store, inner)
-    beside, close, turned = lax.optimization_barrier((beside, close, turned))
-    third_in = send(beside, inner)
+    store, close, turned = lax.optimization_barrier((store, close, turned))
+    third_in = send(store, [(0, 2), (3, 1)])
     across, close, turned = lax.optimization_barrier((across, close, turned))
     second = send(across, outward)
     state = attention(0, False, [close, beside], [lambda at: at, lambda at: at ^ 1], 1, 2, (peak,))

time: 118 us -> 120 us (1.017)
  the two profiles are of different devices: /device:TPU:22 before, /device:TPU:8 now
where the time goes in v8:
time: 120 us; the launch traced here: 119 us
  Pallas kernels  96.1 us (80%)
  starting transfers between devices  16.8 us (14%)
  waiting for transfers between devices  4.19 us (3%)
  other arithmetic  1.62 us (1%)
    pallas_call x3, Pallas kernels, attention(): pl.pallas_call(functools.partial(attend, shards, pick, units, first, last...  89.7 us
    ppermute x5, starting transfers between devices, send(): return lax.ppermute(array, 'req', pairs)  16.8 us
    pallas_call x1, Pallas kernels, on_device(): pl.pallas_call(prepare, out_shape=(pltpu.VMEM((heads, tiles, lanes_rows,...  6.37 us
    ppermute x5, waiting for transfers between devices, send(): return lax.ppermute(array, 'req', pairs)  4.19 us
  transfers between devices with their start and end apart: 5, of which 2 were waited for; matrix products, arithmetic and copies ran while one was open for 1% of the time, Pallas kernels for 58%

profile of v8, /device:TPU:8, one launch (start us, length us, event | category | flops | bytes accessed | tf_op | source)
XLA Modules:
  0.0 119.0 jit_solution(10519961400130775736)
XLA Ops:
  0.0 0.0 copy-start
  0.0 3.6 %collective-permute-start = (bf16[2048,128]{1,0:T(8,128)(2,1)}, bf16[2048,128]{1,0:T(8,128)(2,1)S(1)}, u32[]{:S(2)}, u32[]{:S(2)}) collective-permute-start(bf16[2048,128]{1,0:T(8,128)(2,1)} %bitcast.15), channel_id=1, source_target_pairs={{4,8},{8,4},{5,9},{9,5},{6,10},{10,6},{7,11},{11,7},{20,24},{24,20... | collective-permute-start | bytes 1572872 | tf_op jit(solution)/shard_map/ppermute | solution.py:453
  3.6 0.1 collective-permute-start.3
  3.7 0.7 reduce
  4.4 0.8 negate_select_fusion
  5.2 6.4 %prepare.1 = (bf16[2,6,512,128]{3,2,1,0:T(8,128)(2,1)S(1)}, bf16[3072,640]{1,0:T(8,128)(2,1)S(1)}, bf16[2048,128]{1,0:T(8,128)(2,1)S(1)}, s32[79]{0:T(128)S(4)}, f32[1]{0:T(128)S(4)}) custom-call(bf16[384,2048]{1,0:T(8,128)(2,1)} %bitcast.14, bf16[1536,128]{1,0:T(8,128)(2,1)} %bitcast.19, bf16[2048,128]{1,0:T(8,128)(2,1)} %bitcast.17, s32[1,24]{1,0:T(1,128)} %bitcast.20, ...), custom_call_target="tpu_custom_call" | custom-call | tf_op jit(solution)/shard_map/prepare/pallas_call | solution.py:384
  11.6 0.0 copy-done
  11.6 1.3 %collective-permute-start.2 = (bf16[2048,128]{1,0:T(8,128)(2,1)S(1)}, bf16[2048,128]{1,0:T(8,128)(2,1)S(1)}, u32[]{:S(2)}, u32[]{:S(2)}) collective-permute-start(bf16[2048,128]{1,0:T(8,128)(2,1)S(1)} %bitcast.18), channel_id=1, source_target_pairs={{0,8},{12,4},{1,9},{13,5},{2,10},{14,6},{3,11},{15,7},{16,24},{28,... | collective-permute-start | bytes 1572872 | tf_op jit(solution)/shard_map/ppermute | solution.py:453
  12.9 3.0 %collective-permute-done.refs_1_ = bf16[2048,128]{1,0:T(8,128)(2,1)S(1)} collective-permute-done((bf16[2048,128]{1,0:T(8,128)(2,1)}, bf16[2048,128]{1,0:T(8,128)(2,1)S(1)}, u32[]{:S(2)}, u32[]{:S(2)}) %collective-permute-start) | collective-permute-done | bytes 524320 | tf_op jit(solution)/shard_map/ppermute | solution.py:453
  15.9 1.5 %collective-permute-start.1 = (bf16[2048,128]{1,0:T(8,128)(2,1)S(1)}, bf16[2048,128]{1,0:T(8,128)(2,1)S(1)}, u32[]{:S(2)}, u32[]{:S(2)}) collective-permute-start(bf16[2048,128]{1,0:T(8,128)(2,1)S(1)} %collective-permute-done.refs_1_), channel_id=1, source_target_pairs={{4,0},{8,12},{5,1},{9,13},{6,2},{10,14},{7,3},{11,15},{20,16},{24,... | collective-permute-start | bytes 1572872 | tf_op jit(solution)/shard_map/ppermute | solution.py:453
  17.4 0.1 negate_select_fusion.1
  17.6 1.2 collective-permute-done.3.refs_1_
  18.7 0.1 broadcast_in_dim.4.refs_8_
  18.9 40.5 %attend_0.1 = (f32[2,6,512,128]{3,2,1,0:T(8,128)S(1)}, f32[2,6,512,128]{3,2,1,0:T(8,128)S(1)}, f32[2,6,512,128]{3,2,1,0:T(8,128)S(1)}, f32[1]{0:T(128)S(4)}) custom-call(bf16[2048,128]{1,0:T(8,128)(2,1)S(1)} %get-tuple-element.42.refs_0_, bf16[2048,128]{1,0:T(8,128)(2,1)S(1)} %collective-permute-done.3.refs_1_, s32[79]{0:T(128)S(4)} %get-tuple-element.43.refs_2_, ...), custom_call_target="tpu_custom_call" | custom-call | tf_op jit(solution)/shard_map/attend_0/pallas_call | solution.py:423
  59.4 0.0 collective-permute-done.2.refs_1_
  59.4 0.0 collective-permute-done.1.refs_0_
  59.4 10.3 %collective-permute-start.4 = (bf16[2048,128]{1,0:T(8,128)(2,1)S(1)}, bf16[2048,128]{1,0:T(8,128)(2,1)S(1)}, u32[]{:S(2)}, u32[]{:S(2)}) collective-permute-start(bf16[2048,128]{1,0:T(8,128)(2,1)S(1)} %collective-permute-done.2.refs_1_), channel_id=1, source_target_pairs={{4,0},{8,12},{5,1},{9,13},{6,2},{10,14},{7,3},{11,15},{20,16},{24,... | collective-permute-start | bytes 1572872 | tf_op jit(solution)/shard_map/ppermute | solution.py:453
  69.7 22.5 %attend_1.1 = (f32[2,6,512,128]{3,2,1,0:T(8,128)S(1)}, f32[2,6,512,128]{3,2,1,0:T(8,128)S(1)}, f32[2,6,512,128]{3,2,1,0:T(8,128)S(1)}, f32[1]{0:T(128)S(4)}) custom-call(bf16[2048,128]{1,0:T(8,128)(2,1)S(1)} %collective-permute-done.1.refs_0_, ...), custom_call_target="tpu_custom_call", output_to_operand_aliasing={{0}: (9, {}), {1}: (10, {}), {2}: (11, {})} | custom-call | tf_op jit(solution)/shard_map/attend_1/pallas_call | solution.py:423
  92.3 0.0 collective-permute-done.4.refs_0_
  92.3 26.7 %attend_2.1 = (f32[2,6,512,128]{3,2,1,0:T(8,128)S(1)}, f32[2,6,512,128]{3,2,1,0:T(8,128)S(1)}, f32[2,6,512,128]{3,2,1,0:T(8,128)S(1)}, f32[1]{0:T(128)S(4)}, bf16[384,2048]{1,0:T(8,128)(2,1)}) custom-call(bf16[2048,128]{1,0:T(8,128)(2,1)S(1)} %collective-permute-done.4.refs_0_, ...), custom_call_target="tpu_custom_call", output_to_operand_aliasing={{0}: (9, {}), {1}: (10, {}), {2}: (11, {})} | custom-call | tf_op jit(solution)/shard_map/attend_2/pallas_call | solution.py:423
  (4 shorter events, 0.0 us)
Async XLA Ops:
  0.0 11.6 %copy-start = (bf16[4,128,2,256]{3,2,1,0:T(2,128)(2,1)S(1)}, bf16[4,128,2,256]{3,2,1,0:T(2,128)(2,1)}, u32[]{:S(2)}) copy-start(bf16[4,128,2,256]{3,2,1,0:T(2,128)(2,1)} %param.7) | copy-start | bytes 1572868
  0.0 15.9 %collective-permute-start = (bf16[2048,128]{1,0:T(8,128)(2,1)}, bf16[2048,128]{1,0:T(8,128)(2,1)S(1)}, u32[]{:S(2)}, u32[]{:S(2)}) collective-permute-start(bf16[2048,128]{1,0:T(8,128)(2,1)} %bitcast.15), channel_id=1, source_target_pairs={{4,8},{8,4},{5,9},{9,5},{6,10},{10,6},{7,11},{11,7},{20,24},{24,20... | collective-permute-start | bytes 1572872 | tf_op jit(solution)/shard_map/ppermute | solution.py:453
  3.6 15.1 %collective-permute-start.3 = (bf16[2048,128]{1,0:T(8,128)(2,1)}, bf16[2048,128]{1,0:T(8,128)(2,1)S(1)}, u32[]{:S(2)}, u32[]{:S(2)}) collective-permute-start(bf16[2048,128]{1,0:T(8,128)(2,1)} %bitcast.16), channel_id=1, source_target_pairs={{0,4},{4,0},{8,12},{12,8},{1,5},{5,1},{9,13},{13,9},{2,6},{6,2},{1... | collective-permute-start | bytes 1572872 | tf_op jit(solution)/shard_map/ppermute | solution.py:453
  11.6 47.8 %collective-permute-start.2 = (bf16[2048,128]{1,0:T(8,128)(2,1)S(1)}, bf16[2048,128]{1,0:T(8,128)(2,1)S(1)}, u32[]{:S(2)}, u32[]{:S(2)}) collective-permute-start(bf16[2048,128]{1,0:T(8,128)(2,1)S(1)} %bitcast.18), channel_id=1, source_target_pairs={{0,8},{12,4},{1,9},{13,5},{2,10},{14,6},{3,11},{15,7},{16,24},{28,... | collective-permute-start | bytes 1572872 | tf_op jit(solution)/shard_map/ppermute | solution.py:453
  15.9 43.5 %collective-permute-start.1 = (bf16[2048,128]{1,0:T(8,128)(2,1)S(1)}, bf16[2048,128]{1,0:T(8,128)(2,1)S(1)}, u32[]{:S(2)}, u32[]{:S(2)}) collective-permute-start(bf16[2048,128]{1,0:T(8,128)(2,1)S(1)} %collective-permute-done.refs_1_), channel_id=1, source_target_pairs={{4,0},{8,12},{5,1},{9,13},{6,2},{10,14},{7,3},{11,15},{20,16},{24,... | collective-permute-start | bytes 1572872 | tf_op jit(solution)/shard_map/ppermute | solution.py:453
  59.4 32.9 %collective-permute-start.4 = (bf16[2048,128]{1,0:T(8,128)(2,1)S(1)}, bf16[2048,128]{1,0:T(8,128)(2,1)S(1)}, u32[]{:S(2)}, u32[]{:S(2)}) collective-permute-start(bf16[2048,128]{1,0:T(8,128)(2,1)S(1)} %collective-permute-done.2.refs_1_), channel_id=1, source_target_pairs={{4,0},{8,12},{5,1},{9,13},{6,2},{10,14},{7,3},{11,15},{20,16},{24,... | collective-permute-start | bytes 1572872 | tf_op jit(solution)/shard_map/ppermute | solution.py:453

commit v9 on v8

--- a/solution.py
+++ b/solution.py
@@ -158,8 +158,9 @@
     most_out, sum_out, acc_out, calm_out = refs[:4]
     refs = refs[4:]
     if last:
-        out_ref = refs[0]
-        refs = refs[1:]
+        whole_ref = refs[0]
+        out_ref, out_sems = refs[-2:]
+        refs = refs[1:-2]
     wide_ref, key_ref, value_ref, list_ref = refs
     heads, tiles, lanes_rows, dim = turned_ref.shape
     group = lanes_rows // tile_rows
@@ -269,6 +270,12 @@
                 member * tile_rows : (member + 1) * tile_rows
             ]
 
+    def leave(tile):
+        row_at = pl.ds(pl.multiple_of(tile * tile_rows, tile_rows), tile_rows)
+        return pltpu.make_async_copy(
+            out_ref.at[row_at, :], whole_ref.at[row_at, :], out_sems.at[tile]
+        )
+
     def quick(tile, carry):
         furthest = table_ref[3 * blocks + tile]
         visible = query_mask(tile)
@@ -300,6 +307,8 @@
                             acc = before[1][head, tile] + acc
                         after(head, tile, total, acc)
 
+        if last:
+            leave(tile).start()
         return carry
 
     def careful(tile, carry):
@@ -348,6 +357,7 @@
         if last:
             for head in range(heads):
                 finish(head, tile, sum_out[head, tile], acc_out[head, tile])
+            leave(tile).start()
         return carry
 
     @pl.when(calm > 0.5)
@@ -357,6 +367,10 @@
     @pl.when(calm < 0.5)
     def _():
         lax.fori_loop(0, tiles, careful, 0)
+
+    if last:
+        for tile in range(tiles):
+            leave(tile).wait()
 
 
 def on_device(count, store_kv, block_owner, block_slot, span_len, row_index, fresh_q, fresh_kv):
@@ -424,7 +438,7 @@
             functools.partial(attend, shards, pick, units, first, last),
             out_shape=[state_shape] * 3 + [pltpu.SMEM((1,), jnp.float32)] + result,
             in_specs=specs + [vmem] * (len(state) - 1),
-            out_specs=[vmem] * 3 + [smem] + [vmem] * len(result),
+            out_specs=[vmem] * 3 + [smem] + [anywhere] * len(result),
             input_output_aliases={}
             if first
             else {len(specs) + entry: entry for entry in range(3)},
@@ -433,7 +447,15 @@
                 pltpu.VMEM((heads, spots * block_len, dim), jnp.bfloat16),
                 pltpu.VMEM((heads, spots * block_len, dim), jnp.bfloat16),
                 pltpu.SMEM((blocks + 1,), jnp.int32),
-            ],
+            ]
+            + (
+                [
+                    pltpu.VMEM((rows, heads * group * dim), jnp.bfloat16),
+                    pltpu.SemaphoreType.DMA((tiles,)),
+                ]
+                if last
+                else []
+            ),
             compiler_params=params,
             name=f"attend_{number}",
         )(*inputs, *[near(entry) for entry in state[:-1]])
@@ -456,10 +478,11 @@
     across = send(store, inner)
     store, close, turned = lax.optimization_barrier((store, close, turned))
     third_in = send(store, [(0, 2), (3, 1)])
-    across, close, turned = lax.optimization_barrier((across, close, turned))
+    across, turned = lax.optimization_barrier((across, turned))
     second = send(across, outward)
+    beside, close, placed = lax.optimization_barrier((beside, close, placed))
     state = attention(0, False, [close, beside], [lambda at: at, lambda at: at ^ 1], 1, 2, (peak,))
-    second, third_in, state = lax.optimization_barrier((second, third_in, state))
+    third_in, table, state = lax.optimization_barrier((third_in, table, state))
     third = send(third_in, outward)
     state = attention(
         1,

time: 120 us -> 118 us (0.983); the launches traced: 119 us -> 120 us
  starting transfers between devices: 16.8 us -> 14 us
  Pallas kernels: 96.1 us -> 98.3 us
  waiting for transfers between devices: 4.19 us -> 5.72 us
    ppermute x5, starting transfers between devices: 16.8 us -> 14 us  [send(): return lax.ppermute(array, 'req', pairs)]
    pallas_call x3, Pallas kernels: 89.7 us -> 91.9 us  [attention(): pl.pallas_call(functools.partial(attend, shards, pick, units, first, last...]
    ppermute x5, waiting for transfers between devices: 4.19 us -> 5.72 us  [send(): return lax.ppermute(array, 'req', pairs)]
  transfers between devices with their start and end apart: 5 -> 5, of which waited for: 2 -> 1; matrix products, arithmetic and copies ran while one was open for 1% -> 1% of each run, Pallas kernels for 58% -> 56%
where the time goes in v9:
time: 118 us; the launch traced here: 120 us
  Pallas kernels  98.3 us (83%)
  starting transfers between devices  14 us (12%)
  waiting for transfers between devices  5.72 us (5%)
  other arithmetic  1.62 us (1%)
    pallas_call x3, Pallas kernels, attention(): pl.pallas_call(functools.partial(attend, shards, pick, units, first, last...  91.9 us
    ppermute x5, starting transfers between devices, send(): return lax.ppermute(array, 'req', pairs)  14 us
    pallas_call x1, Pallas kernels, on_device(): pl.pallas_call(prepare, out_shape=(pltpu.VMEM((heads, tiles, lanes_rows,...  6.36 us
    ppermute x5, waiting for transfers between devices, send(): return lax.ppermute(array, 'req', pairs)  5.72 us
  transfers between devices with their start and end apart: 5, of which 1 were waited for; matrix products, arithmetic and copies ran while one was open for 1% of the time, Pallas kernels for 56%

profile of v9, /device:TPU:8, one launch (start us, length us, event | category | flops | bytes accessed | tf_op | source)
XLA Modules:
  0.0 120.0 jit_solution(1844202425421264943)
XLA Ops:
  0.0 0.0 copy-start
  0.0 3.6 %collective-permute-start.2 = (bf16[2048,128]{1,0:T(8,128)(2,1)}, bf16[2048,128]{1,0:T(8,128)(2,1)S(1)}, u32[]{:S(2)}, u32[]{:S(2)}) collective-permute-start(bf16[2048,128]{1,0:T(8,128)(2,1)} %bitcast.15), channel_id=1, source_target_pairs={{4,8},{8,4},{5,9},{9,5},{6,10},{10,6},{7,11},{11,7},{20,24},{24,20... | collective-permute-start | bytes 1572872 | tf_op jit(solution)/shard_map/ppermute | solution.py:475
  3.6 0.1 collective-permute-start.1
  3.7 0.7 reduce
  4.4 0.8 negate_select_fusion
  5.2 6.4 %prepare.1 = (bf16[2,6,512,128]{3,2,1,0:T(8,128)(2,1)S(1)}, bf16[3072,640]{1,0:T(8,128)(2,1)S(1)}, bf16[2048,128]{1,0:T(8,128)(2,1)S(1)}, s32[79]{0:T(128)S(4)}, f32[1]{0:T(128)S(4)}) custom-call(bf16[384,2048]{1,0:T(8,128)(2,1)} %bitcast.14, bf16[1536,128]{1,0:T(8,128)(2,1)} %bitcast.19, bf16[2048,128]{1,0:T(8,128)(2,1)} %bitcast.17, s32[1,24]{1,0:T(1,128)} %bitcast.20, ...), custom_call_target="tpu_custom_call" | custom-call | tf_op jit(solution)/shard_map/prepare/pallas_call | solution.py:398
  11.6 0.0 copy-done
  11.6 1.3 %collective-permute-start = (bf16[2048,128]{1,0:T(8,128)(2,1)S(1)}, bf16[2048,128]{1,0:T(8,128)(2,1)S(1)}, u32[]{:S(2)}, u32[]{:S(2)}) collective-permute-start(bf16[2048,128]{1,0:T(8,128)(2,1)S(1)} %bitcast.18), channel_id=1, source_target_pairs={{0,8},{12,4},{1,9},{13,5},{2,10},{14,6},{3,11},{15,7},{16,24},{28,... | collective-permute-start | bytes 1572872 | tf_op jit(solution)/shard_map/ppermute | solution.py:475
  12.9 0.1 negate_select_fusion.1
  13.0 5.7 %collective-permute-done.1.refs_1_ = bf16[2048,128]{1,0:T(8,128)(2,1)S(1)} collective-permute-done((bf16[2048,128]{1,0:T(8,128)(2,1)}, bf16[2048,128]{1,0:T(8,128)(2,1)S(1)}, u32[]{:S(2)}, u32[]{:S(2)}) %collective-permute-start.1) | collective-permute-done | bytes 524320 | tf_op jit(solution)/shard_map/ppermute | solution.py:475
  18.7 0.0 collective-permute-done.2.refs_1_
  18.7 1.6 %collective-permute-start.4 = (bf16[2048,128]{1,0:T(8,128)(2,1)S(1)}, bf16[2048,128]{1,0:T(8,128)(2,1)S(1)}, u32[]{:S(2)}, u32[]{:S(2)}) collective-permute-start(bf16[2048,128]{1,0:T(8,128)(2,1)S(1)} %collective-permute-done.2.refs_1_), channel_id=1, source_target_pairs={{4,0},{8,12},{5,1},{9,13},{6,2},{10,14},{7,3},{11,15},{20,16},{24,... | collective-permute-start | bytes 1572872 | tf_op jit(solution)/shard_map/ppermute | solution.py:475
  20.3 0.1 broadcast_in_dim.4.refs_8_
  20.4 35.4 %attend_0.1 = (f32[2,6,512,128]{3,2,1,0:T(8,128)S(1)}, f32[2,6,512,128]{3,2,1,0:T(8,128)S(1)}, f32[2,6,512,128]{3,2,1,0:T(8,128)S(1)}, f32[1]{0:T(128)S(4)}) custom-call(bf16[2048,128]{1,0:T(8,128)(2,1)S(1)} %get-tuple-element.44.refs_0_, bf16[2048,128]{1,0:T(8,128)(2,1)S(1)} %collective-permute-done.1.refs_1_, s32[79]{0:T(128)S(4)} %get-tuple-element.56.refs_2_, ...), custom_call_target="tpu_custom_call" | custom-call | tf_op jit(solution)/shard_map/attend_0/pallas_call | solution.py:437
  55.8 0.0 collective-permute-done.refs_1_
  55.8 7.5 %collective-permute-start.3 = (bf16[2048,128]{1,0:T(8,128)(2,1)S(1)}, bf16[2048,128]{1,0:T(8,128)(2,1)S(1)}, u32[]{:S(2)}, u32[]{:S(2)}) collective-permute-start(bf16[2048,128]{1,0:T(8,128)(2,1)S(1)} %collective-permute-done.refs_1_), channel_id=1, source_target_pairs={{4,0},{8,12},{5,1},{9,13},{6,2},{10,14},{7,3},{11,15},{20,16},{24,... | collective-permute-start | bytes 1572872 | tf_op jit(solution)/shard_map/ppermute | solution.py:475
  63.3 0.0 collective-permute-done.4.refs_0_
  63.3 26.0 %attend_1.1 = (f32[2,6,512,128]{3,2,1,0:T(8,128)S(1)}, f32[2,6,512,128]{3,2,1,0:T(8,128)S(1)}, f32[2,6,512,128]{3,2,1,0:T(8,128)S(1)}, f32[1]{0:T(128)S(4)}) custom-call(bf16[2048,128]{1,0:T(8,128)(2,1)S(1)} %collective-permute-done.4.refs_0_, ...), custom_call_target="tpu_custom_call", output_to_operand_aliasing={{0}: (9, {}), {1}: (10, {}), {2}: (11, {})} | custom-call | tf_op jit(solution)/shard_map/attend_1/pallas_call | solution.py:437
  89.3 0.0 collective-permute-done.3.refs_0_
  89.3 30.6 %attend_2.1 = (f32[2,6,512,128]{3,2,1,0:T(8,128)S(1)}, f32[2,6,512,128]{3,2,1,0:T(8,128)S(1)}, f32[2,6,512,128]{3,2,1,0:T(8,128)S(1)}, f32[1]{0:T(128)S(4)}, bf16[384,2048]{1,0:T(8,128)(2,1)}) custom-call(bf16[2048,128]{1,0:T(8,128)(2,1)S(1)} %collective-permute-done.3.refs_0_, ...), custom_call_target="tpu_custom_call", output_to_operand_aliasing={{0}: (9, {}), {1}: (10, {}), {2}: (11, {})} | custom-call | tf_op jit(solution)/shard_map/attend_2/pallas_call | solution.py:437
  (4 shorter events, 0.0 us)
Async XLA Ops:
  0.0 11.6 %copy-start = (bf16[4,128,2,256]{3,2,1,0:T(2,128)(2,1)S(1)}, bf16[4,128,2,256]{3,2,1,0:T(2,128)(2,1)}, u32[]{:S(2)}) copy-start(bf16[4,128,2,256]{3,2,1,0:T(2,128)(2,1)} %param.7) | copy-start | bytes 1572868
  0.0 18.7 %collective-permute-start.2 = (bf16[2048,128]{1,0:T(8,128)(2,1)}, bf16[2048,128]{1,0:T(8,128)(2,1)S(1)}, u32[]{:S(2)}, u32[]{:S(2)}) collective-permute-start(bf16[2048,128]{1,0:T(8,128)(2,1)} %bitcast.15), channel_id=1, source_target_pairs={{4,8},{8,4},{5,9},{9,5},{6,10},{10,6},{7,11},{11,7},{20,24},{24,20... | collective-permute-start | bytes 1572872 | tf_op jit(solution)/shard_map/ppermute | solution.py:475
  3.6 15.1 %collective-permute-start.1 = (bf16[2048,128]{1,0:T(8,128)(2,1)}, bf16[2048,128]{1,0:T(8,128)(2,1)S(1)}, u32[]{:S(2)}, u32[]{:S(2)}) collective-permute-start(bf16[2048,128]{1,0:T(8,128)(2,1)} %bitcast.16), channel_id=1, source_target_pairs={{0,4},{4,0},{8,12},{12,8},{1,5},{5,1},{9,13},{13,9},{2,6},{6,2},{1... | collective-permute-start | bytes 1572872 | tf_op jit(solution)/shard_map/ppermute | solution.py:475
  11.6 44.2 %collective-permute-start = (bf16[2048,128]{1,0:T(8,128)(2,1)S(1)}, bf16[2048,128]{1,0:T(8,128)(2,1)S(1)}, u32[]{:S(2)}, u32[]{:S(2)}) collective-permute-start(bf16[2048,128]{1,0:T(8,128)(2,1)S(1)} %bitcast.18), channel_id=1, source_target_pairs={{0,8},{12,4},{1,9},{13,5},{2,10},{14,6},{3,11},{15,7},{16,24},{28,... | collective-permute-start | bytes 1572872 | tf_op jit(solution)/shard_map/ppermute | solution.py:475
  18.7 44.6 %collective-permute-start.4 = (bf16[2048,128]{1,0:T(8,128)(2,1)S(1)}, bf16[2048,128]{1,0:T(8,128)(2,1)S(1)}, u32[]{:S(2)}, u32[]{:S(2)}) collective-permute-start(bf16[2048,128]{1,0:T(8,128)(2,1)S(1)} %collective-permute-done.2.refs_1_), channel_id=1, source_target_pairs={{4,0},{8,12},{5,1},{9,13},{6,2},{10,14},{7,3},{11,15},{20,16},{24,... | collective-permute-start | bytes 1572872 | tf_op jit(solution)/shard_map/ppermute | solution.py:475
  55.8 33.5 %collective-permute-start.3 = (bf16[2048,128]{1,0:T(8,128)(2,1)S(1)}, bf16[2048,128]{1,0:T(8,128)(2,1)S(1)}, u32[]{:S(2)}, u32[]{:S(2)}) collective-permute-start(bf16[2048,128]{1,0:T(8,128)(2,1)S(1)} %collective-permute-done.refs_1_), channel_id=1, source_target_pairs={{4,0},{8,12},{5,1},{9,13},{6,2},{10,14},{7,3},{11,15},{20,16},{24,... | collective-permute-start | bytes 1572872 | tf_op jit(solution)/shard_map/ppermute | solution.py:475
